TPU v7x, 512 devices: a whole 4x8x8 slice. The times are simulated.
512 devices in a mesh: emit: 32 (over x, z), vx: 8 (over y), vy: 2 (over core).
Axes of the slice: x: 4, y: 8, z: 8, core: 2. Of those that a mesh axis runs over, the one named last changes fastest.
Arguments:
- fwd_state: float32 [3, 32, 2048, 512], P(None, 'emit', 'vx', 'vy'), may hold values from -6 to 6
- adj_state: float32 [3, 32, 2048, 512], P(None, 'emit', 'vx', 'vy'), may hold values from -6 to 6
- courant: float32 [2048, 512], P('vx', 'vy'), may hold values from 0.2 to 0.45
- decay_rate: float32 [2048, 512], P('vx', 'vy'), may hold values from 0.2 to 0.9
- strength: float32 [2048, 512], P('vx', 'vy'), may hold values from 0.05 to 0.4
- footprint: int32 [32, 8, 2, 16], P('emit', 'vx', 'vy'), may hold values from 0 to 31, all different within a row
- owner_map: int32 [8, 2, 32], P('vx', 'vy'), may hold values from 0 to 31, each once within a row
Outputs:
- gradient: float32 [32, 128, 256], P('emit', 'vx', 'vy')
- pressure: float32 [32, 2048, 512], P('emit', 'vx', 'vy')
Inputs may be any that keep to these rules, and one draw needn't show every extreme that they name: `footprint`: in each row the 16 ids are distinct block ids of one tile. `owner_map`: for each tile a permutation of its 32 block ids.
All inputs are finite; a program needn't handle non-finite values.
Results may differ from a plain program's by a relative error of at most 0.0003.
Values sent between devices are 32-bit elements; how exact they have to be, the bound alone decides.
No kernel may reach another device: no remote copies, remote signals or barrier semaphores. Data moves between devices by JAX's collectives and lax.ppermute only.
A program may use at most 64 MiB of HBM per device.

v0:
```python
import jax
import jax.numpy as jnp
from jax import lax
from jax.sharding import PartitionSpec as P

BR = 16
BC = 128
BX = 16
BY = 2
STEPS = 4


def with_halo(block, sides, width):
    for axis, dim in sides:
        count = lax.axis_size(axis)
        forward = [(i, i + 1) for i in range(count - 1)]
        backward = [(target, source) for source, target in forward]
        low = lax.ppermute(
            lax.slice_in_dim(block, block.shape[dim] - width, None, axis=dim), axis, forward
        )
        high = lax.ppermute(lax.slice_in_dim(block, 0, width, axis=dim), axis, backward)
        block = jnp.concatenate([low, block, high], axis=dim)
    return block


def halo_laplace(field):
    padded = with_halo(field, (("vx", 0), ("vy", 1)), 1)
    return padded[2:, 1:-1] + padded[:-2, 1:-1] + padded[1:-1, 2:] + padded[1:-1, :-2] - 4.0 * field


def keep_all(field):
    return field


def advance(state, courant, decay_rate, strength, laplace_fn):
    former, current, memory = state
    curve = laplace_fn(current)
    memory = decay_rate * memory + strength * curve
    following = 2.0 * current - former + courant * (curve - memory)
    return (current, following, memory)


def propagate(state, courant, decay_rate, strength, laplace_fn, crop):
    levels = [crop(state[0]), crop(state[1])]
    for number in range(STEPS):
        state = advance(state, courant, decay_rate, strength, laplace_fn)
        levels.append(crop(state[1]))
    return levels


def imaging(forward, adjoint, scale):
    result = None
    for level in range(1, STEPS + 1):
        second = forward[level + 1] - 2.0 * forward[level] + forward[level - 1]
        term = adjoint[STEPS + 2 - level] * second
        result = term if result is None else result + term
    return result * scale


def shards(fwd_state, adj_state, courant, decay_rate, strength, footprint, owner_map):
    groups = lax.axis_size("emit")
    blocks_count = owner_map.shape[-1]
    forward_in = (fwd_state[0, 0], fwd_state[1, 0], fwd_state[2, 0])
    adjoint_in = (adj_state[0, 0], adj_state[1, 0], adj_state[2, 0])
    forward = propagate(forward_in, courant, decay_rate, strength, halo_laplace, keep_all)
    adjoint = propagate(adjoint_in, courant, decay_rate, strength, halo_laplace, keep_all)
    gradient = imaging(forward, adjoint, 1.0 / groups)
    tiled = gradient.reshape(BX, BR, BY, BC).transpose(0, 2, 1, 3).reshape(blocks_count, BR, BC)
    listed = footprint.reshape(-1)
    block_ids = jnp.arange(blocks_count, dtype=jnp.int32)
    hits = jnp.any(listed[:, None] == block_ids[None, :], axis=0).astype(jnp.float32)
    masked = tiled * hits[:, None, None]
    ordered = jnp.take(masked, owner_map.reshape(-1), axis=0)
    gradient_out = lax.psum_scatter(ordered, "emit", scatter_dimension=0, tiled=True)
    return (gradient_out, forward[STEPS + 1][None])


def solution(mesh):
    in_specs = (
        P(None, "emit", "vx", "vy"),
        P(None, "emit", "vx", "vy"),
        P("vx", "vy"),
        P("vx", "vy"),
        P("vx", "vy"),
        P("emit", "vx", "vy", None),
        P("vx", "vy", None),
    )
    out_specs = (P("emit", "vx", "vy"), P("emit", "vx", "vy"))
    return jax.shard_map(shards, mesh=mesh, in_specs=in_specs, out_specs=out_specs, check_vma=False)
```

profile of v0, /device:TPU:40, one launch (start us, length us, event | category | flops | bytes accessed | tf_op | source)
XLA Modules:
  0.0 339.7 jit_solution(8120311697876734829)
XLA Ops:
  7.9 3.2 collective-permute-start
  11.2 2.6 collective-permute-start.1
  14.5 3.2 collective-permute-start.16
  17.8 2.6 collective-permute-start.17
  23.8 1.4 collective-permute-start.3
  25.2 1.3 collective-permute-start.2
  26.7 3.2 collective-permute-start.19
  29.9 1.4 collective-permute-start.18
  31.7 3.3 collective-permute-start.4
  35.0 2.6 collective-permute-start.5
  37.9 4.1 %collective-permute-start.20 = (f32[1,256]{1,0:T(1,128)S(1)}, f32[1,256]{1,0:T(1,128)S(1)}, u32[]{:S(2)}, u32[]{:S(2)}) collective-permute-start(f32[1,256]{1,0:T(1,128)S(1)} %get-tuple-element.33), channel_id=1, source_target_pairs={{2,0},{4,2},{6,4},{8,6},{10,8},{12,10},{14,12},{3,1},{5,3},{7,5},{... | collective-permute-start | bytes 3080 | tf_op jit(solution)/shard_map/ppermute | solution.py:21
  42.1 1.9 collective-permute-start.21
  44.1 2.5 collective-permute-start.7
  46.6 1.3 collective-permute-start.6
  48.9 2.3 collective-permute-start.23
  51.1 1.3 collective-permute-start.22
  52.8 4.9 %collective-permute-start.8 = (f32[1,256]{1,0:T(1,128)S(1)}, f32[1,256]{1,0:T(1,128)S(1)}, u32[]{:S(2)}, u32[]{:S(2)}) collective-permute-start(f32[1,256]{1,0:T(1,128)S(1)} %get-tuple-element.37), channel_id=1, source_target_pairs={{2,0},{4,2},{6,4},{8,6},{10,8},{12,10},{14,12},{3,1},{5,3},{7,5},{... | collective-permute-start | bytes 3080 | tf_op jit(solution)/shard_map/ppermute | solution.py:21
  57.7 1.9 collective-permute-start.9
  59.9 4.9 %collective-permute-start.24 = (f32[1,256]{1,0:T(1,128)S(1)}, f32[1,256]{1,0:T(1,128)S(1)}, u32[]{:S(2)}, u32[]{:S(2)}) collective-permute-start(f32[1,256]{1,0:T(1,128)S(1)} %get-tuple-element.31), channel_id=1, source_target_pairs={{2,0},{4,2},{6,4},{8,6},{10,8},{12,10},{14,12},{3,1},{5,3},{7,5},{... | collective-permute-start | bytes 3080 | tf_op jit(solution)/shard_map/ppermute | solution.py:21
  64.8 1.9 collective-permute-start.25
  66.9 2.5 collective-permute-start.11
  71.6 2.3 collective-permute-start.27
  75.7 4.9 %collective-permute-start.12 = (f32[1,256]{1,0:T(1,128)S(1)}, f32[1,256]{1,0:T(1,128)S(1)}, u32[]{:S(2)}, u32[]{:S(2)}) collective-permute-start(f32[1,256]{1,0:T(1,128)S(1)} %get-tuple-element.35), channel_id=1, source_target_pairs={{2,0},{4,2},{6,4},{8,6},{10,8},{12,10},{14,12},{3,1},{5,3},{7,5},{... | collective-permute-start | bytes 3080 | tf_op jit(solution)/shard_map/ppermute | solution.py:21
  80.6 1.9 collective-permute-start.13
  83.1 4.9 %collective-permute-start.28 = (f32[1,256]{1,0:T(1,128)S(1)}, f32[1,256]{1,0:T(1,128)S(1)}, u32[]{:S(2)}, u32[]{:S(2)}) collective-permute-start(f32[1,256]{1,0:T(1,128)S(1)} %get-tuple-element.29), channel_id=1, source_target_pairs={{2,0},{4,2},{6,4},{8,6},{10,8},{12,10},{14,12},{3,1},{5,3},{7,5},{... | collective-permute-start | bytes 3080 | tf_op jit(solution)/shard_map/ppermute | solution.py:21
  88.0 1.9 collective-permute-start.29
  90.0 2.5 collective-permute-start.15
  92.5 1.3 collective-permute-start.14
  94.8 2.3 collective-permute-start.31
  101.0 2.4 fusion.38
  104.9 1.4 broadcast_select_fusion
  108.5 224.3 %reduce-scatter.2.cloned.1.call-done = f32[1,16,128]{2,1,0:T(8,128)} async-done(((f32[32,16,128]{2,1,0:T(8,128)}), f32[1,16,128]{2,1,0:T(8,128)}) %reduce-scatter.2.cloned.1.call-update) | async-done | bytes 8208 | tf_op jit(solution)/shard_map/reduce_scatter | solution.py:74
  (111 shorter events, 20.6 us)
Async XLA Ops:
  7.2 325.6 %reduce-scatter.2.cloned.1.call-start = ((), (), s32[]{:S(2)}) async-start(), calls=%async_computation.1 | async-start | bytes 270336 | tf_op jit(solution)/shard_map/reduce_scatter | solution.py:74
  7.9 15.7 %collective-permute-start = (f32[1,256]{1,0:T(1,128)S(1)}, f32[1,256]{1,0:T(1,128)S(1)}, u32[]{:S(2)}, u32[]{:S(2)}) collective-permute-start(f32[1,256]{1,0:T(1,128)S(1)} %get-tuple-element.11), channel_id=1, source_target_pairs={{2,0},{4,2},{6,4},{8,6},{10,8},{12,10},{14,12},{3,1},{5,3},{7,5},{... | collective-permute-start | bytes 3080 | tf_op jit(solution)/shard_map/ppermute | solution.py:21
  11.2 12.4 %collective-permute-start.1 = (f32[1,256]{1,0:T(1,128)S(1)}, f32[1,256]{1,0:T(1,128)S(1)}, u32[]{:S(2)}, u32[]{:S(2)}) collective-permute-start(f32[1,256]{1,0:T(1,128)S(1)} %get-tuple-element.10), channel_id=1, source_target_pairs={{0,2},{2,4},{4,6},{6,8},{8,10},{10,12},{12,14},{1,3},{3,5},{5,7},{... | collective-permute-start | bytes 3080 | tf_op jit(solution)/shard_map/ppermute | solution.py:18
  14.5 12.0 %collective-permute-start.16 = (f32[1,256]{1,0:T(1,128)S(1)}, f32[1,256]{1,0:T(1,128)S(1)}, u32[]{:S(2)}, u32[]{:S(2)}) collective-permute-start(f32[1,256]{1,0:T(1,128)S(1)} %get-tuple-element.9), channel_id=1, source_target_pairs={{2,0},{4,2},{6,4},{8,6},{10,8},{12,10},{14,12},{3,1},{5,3},{7,5},{... | collective-permute-start | bytes 3080 | tf_op jit(solution)/shard_map/ppermute | solution.py:21
  17.8 8.8 %collective-permute-start.17 = (f32[1,256]{1,0:T(1,128)S(1)}, f32[1,256]{1,0:T(1,128)S(1)}, u32[]{:S(2)}, u32[]{:S(2)}) collective-permute-start(f32[1,256]{1,0:T(1,128)S(1)} %get-tuple-element.8), channel_id=1, source_target_pairs={{0,2},{2,4},{4,6},{6,8},{8,10},{10,12},{12,14},{1,3},{3,5},{5,7},{... | collective-permute-start | bytes 3080 | tf_op jit(solution)/shard_map/ppermute | solution.py:18
  23.8 7.6 %collective-permute-start.3 = (f32[258,1]{1,0:T(8,128)S(1)}, f32[258,1]{1,0:T(8,128)S(1)}, u32[]{:S(2)}, u32[]{:S(2)}) collective-permute-start(f32[258,1]{1,0:T(8,128)S(1)} %get-tuple-element.27), channel_id=1, source_target_pairs={{0,1},{2,3},{4,5},{6,7},{8,9},{10,11},{12,13},{14,15},{16,17},{18,... | collective-permute-start | bytes 3104 | tf_op jit(solution)/shard_map/ppermute | solution.py:18
  25.2 6.1 %collective-permute-start.2 = (f32[258,1]{1,0:T(8,128)S(1)}, f32[258,1]{1,0:T(8,128)S(1)}, u32[]{:S(2)}, u32[]{:S(2)}) collective-permute-start(f32[258,1]{1,0:T(8,128)S(1)} %get-tuple-element.26), channel_id=1, source_target_pairs={{1,0},{3,2},{5,4},{7,6},{9,8},{11,10},{13,12},{15,14},{17,16},{19,... | collective-permute-start | bytes 3104 | tf_op jit(solution)/shard_map/ppermute | solution.py:21
  26.7 10.9 %collective-permute-start.19 = (f32[258,1]{1,0:T(8,128)S(1)}, f32[258,1]{1,0:T(8,128)S(1)}, u32[]{:S(2)}, u32[]{:S(2)}) collective-permute-start(f32[258,1]{1,0:T(8,128)S(1)} %get-tuple-element.23), channel_id=1, source_target_pairs={{0,1},{2,3},{4,5},{6,7},{8,9},{10,11},{12,13},{14,15},{16,17},{18,... | collective-permute-start | bytes 3104 | tf_op jit(solution)/shard_map/ppermute | solution.py:18
  29.9 7.7 %collective-permute-start.18 = (f32[258,1]{1,0:T(8,128)S(1)}, f32[258,1]{1,0:T(8,128)S(1)}, u32[]{:S(2)}, u32[]{:S(2)}) collective-permute-start(f32[258,1]{1,0:T(8,128)S(1)} %get-tuple-element.22), channel_id=1, source_target_pairs={{1,0},{3,2},{5,4},{7,6},{9,8},{11,10},{13,12},{15,14},{17,16},{19,... | collective-permute-start | bytes 3104 | tf_op jit(solution)/shard_map/ppermute | solution.py:21
  31.7 12.3 %collective-permute-start.4 = (f32[1,256]{1,0:T(1,128)S(1)}, f32[1,256]{1,0:T(1,128)S(1)}, u32[]{:S(2)}, u32[]{:S(2)}) collective-permute-start(f32[1,256]{1,0:T(1,128)S(1)} %get-tuple-element.39), channel_id=1, source_target_pairs={{2,0},{4,2},{6,4},{8,6},{10,8},{12,10},{14,12},{3,1},{5,3},{7,5},{... | collective-permute-start | bytes 3080 | tf_op jit(solution)/shard_map/ppermute | solution.py:21
  35.0 9.0 %collective-permute-start.5 = (f32[1,256]{1,0:T(1,128)S(1)}, f32[1,256]{1,0:T(1,128)S(1)}, u32[]{:S(2)}, u32[]{:S(2)}) collective-permute-start(f32[1,256]{1,0:T(1,128)S(1)} %get-tuple-element.38), channel_id=1, source_target_pairs={{0,2},{2,4},{4,6},{6,8},{8,10},{10,12},{12,14},{1,3},{3,5},{5,7},{... | collective-permute-start | bytes 3080 | tf_op jit(solution)/shard_map/ppermute | solution.py:18
  37.9 10.0 %collective-permute-start.20 = (f32[1,256]{1,0:T(1,128)S(1)}, f32[1,256]{1,0:T(1,128)S(1)}, u32[]{:S(2)}, u32[]{:S(2)}) collective-permute-start(f32[1,256]{1,0:T(1,128)S(1)} %get-tuple-element.33), channel_id=1, source_target_pairs={{2,0},{4,2},{6,4},{8,6},{10,8},{12,10},{14,12},{3,1},{5,3},{7,5},{... | collective-permute-start | bytes 3080 | tf_op jit(solution)/shard_map/ppermute | solution.py:21
  42.1 6.7 %collective-permute-start.21 = (f32[1,256]{1,0:T(1,128)S(1)}, f32[1,256]{1,0:T(1,128)S(1)}, u32[]{:S(2)}, u32[]{:S(2)}) collective-permute-start(f32[1,256]{1,0:T(1,128)S(1)} %get-tuple-element.32), channel_id=1, source_target_pairs={{0,2},{2,4},{4,6},{6,8},{8,10},{10,12},{12,14},{1,3},{3,5},{5,7},{... | collective-permute-start | bytes 3080 | tf_op jit(solution)/shard_map/ppermute | solution.py:18
  44.1 8.3 %collective-permute-start.7 = (f32[258,1]{1,0:T(8,128)S(1)}, f32[258,1]{1,0:T(8,128)S(1)}, u32[]{:S(2)}, u32[]{:S(2)}) collective-permute-start(f32[258,1]{1,0:T(8,128)S(1)} %get-tuple-element.25), channel_id=1, source_target_pairs={{0,1},{2,3},{4,5},{6,7},{8,9},{10,11},{12,13},{14,15},{16,17},{18,... | collective-permute-start | bytes 3104 | tf_op jit(solution)/shard_map/ppermute | solution.py:18
  46.6 5.8 %collective-permute-start.6 = (f32[258,1]{1,0:T(8,128)S(1)}, f32[258,1]{1,0:T(8,128)S(1)}, u32[]{:S(2)}, u32[]{:S(2)}) collective-permute-start(f32[258,1]{1,0:T(8,128)S(1)} %get-tuple-element.24), channel_id=1, source_target_pairs={{1,0},{3,2},{5,4},{7,6},{9,8},{11,10},{13,12},{15,14},{17,16},{19,... | collective-permute-start | bytes 3104 | tf_op jit(solution)/shard_map/ppermute | solution.py:21
  48.9 10.7 %collective-permute-start.23 = (f32[258,1]{1,0:T(8,128)S(1)}, f32[258,1]{1,0:T(8,128)S(1)}, u32[]{:S(2)}, u32[]{:S(2)}) collective-permute-start(f32[258,1]{1,0:T(8,128)S(1)} %get-tuple-element.17), channel_id=1, source_target_pairs={{0,1},{2,3},{4,5},{6,7},{8,9},{10,11},{12,13},{14,15},{16,17},{18,... | collective-permute-start | bytes 3104 | tf_op jit(solution)/shard_map/ppermute | solution.py:18
  51.1 8.5 %collective-permute-start.22 = (f32[258,1]{1,0:T(8,128)S(1)}, f32[258,1]{1,0:T(8,128)S(1)}, u32[]{:S(2)}, u32[]{:S(2)}) collective-permute-start(f32[258,1]{1,0:T(8,128)S(1)} %get-tuple-element.16), channel_id=1, source_target_pairs={{1,0},{3,2},{5,4},{7,6},{9,8},{11,10},{13,12},{15,14},{17,16},{19,... | collective-permute-start | bytes 3104 | tf_op jit(solution)/shard_map/ppermute | solution.py:21
  52.8 13.9 %collective-permute-start.8 = (f32[1,256]{1,0:T(1,128)S(1)}, f32[1,256]{1,0:T(1,128)S(1)}, u32[]{:S(2)}, u32[]{:S(2)}) collective-permute-start(f32[1,256]{1,0:T(1,128)S(1)} %get-tuple-element.37), channel_id=1, source_target_pairs={{2,0},{4,2},{6,4},{8,6},{10,8},{12,10},{14,12},{3,1},{5,3},{7,5},{... | collective-permute-start | bytes 3080 | tf_op jit(solution)/shard_map/ppermute | solution.py:21
  57.7 9.1 %collective-permute-start.9 = (f32[1,256]{1,0:T(1,128)S(1)}, f32[1,256]{1,0:T(1,128)S(1)}, u32[]{:S(2)}, u32[]{:S(2)}) collective-permute-start(f32[1,256]{1,0:T(1,128)S(1)} %get-tuple-element.36), channel_id=1, source_target_pairs={{0,2},{2,4},{4,6},{6,8},{8,10},{10,12},{12,14},{1,3},{3,5},{5,7},{... | collective-permute-start | bytes 3080 | tf_op jit(solution)/shard_map/ppermute | solution.py:18
  59.9 10.7 %collective-permute-start.24 = (f32[1,256]{1,0:T(1,128)S(1)}, f32[1,256]{1,0:T(1,128)S(1)}, u32[]{:S(2)}, u32[]{:S(2)}) collective-permute-start(f32[1,256]{1,0:T(1,128)S(1)} %get-tuple-element.31), channel_id=1, source_target_pairs={{2,0},{4,2},{6,4},{8,6},{10,8},{12,10},{14,12},{3,1},{5,3},{7,5},{... | collective-permute-start | bytes 3080 | tf_op jit(solution)/shard_map/ppermute | solution.py:21
  64.8 6.7 %collective-permute-start.25 = (f32[1,256]{1,0:T(1,128)S(1)}, f32[1,256]{1,0:T(1,128)S(1)}, u32[]{:S(2)}, u32[]{:S(2)}) collective-permute-start(f32[1,256]{1,0:T(1,128)S(1)} %get-tuple-element.30), channel_id=1, source_target_pairs={{0,2},{2,4},{4,6},{6,8},{8,10},{10,12},{12,14},{1,3},{3,5},{5,7},{... | collective-permute-start | bytes 3080 | tf_op jit(solution)/shard_map/ppermute | solution.py:18
  66.9 8.3 %collective-permute-start.11 = (f32[258,1]{1,0:T(8,128)S(1)}, f32[258,1]{1,0:T(8,128)S(1)}, u32[]{:S(2)}, u32[]{:S(2)}) collective-permute-start(f32[258,1]{1,0:T(8,128)S(1)} %get-tuple-element.21), channel_id=1, source_target_pairs={{0,1},{2,3},{4,5},{6,7},{8,9},{10,11},{12,13},{14,15},{16,17},{18,... | collective-permute-start | bytes 3104 | tf_op jit(solution)/shard_map/ppermute | solution.py:18
  69.4 5.8 %collective-permute-start.10 = (f32[258,1]{1,0:T(8,128)S(1)}, f32[258,1]{1,0:T(8,128)S(1)}, u32[]{:S(2)}, u32[]{:S(2)}) collective-permute-start(f32[258,1]{1,0:T(8,128)S(1)} %get-tuple-element.20), channel_id=1, source_target_pairs={{1,0},{3,2},{5,4},{7,6},{9,8},{11,10},{13,12},{15,14},{17,16},{19,... | collective-permute-start | bytes 3104 | tf_op jit(solution)/shard_map/ppermute | solution.py:21
  71.6 10.9 %collective-permute-start.27 = (f32[258,1]{1,0:T(8,128)S(1)}, f32[258,1]{1,0:T(8,128)S(1)}, u32[]{:S(2)}, u32[]{:S(2)}) collective-permute-start(f32[258,1]{1,0:T(8,128)S(1)} %get-tuple-element.15), channel_id=1, source_target_pairs={{0,1},{2,3},{4,5},{6,7},{8,9},{10,11},{12,13},{14,15},{16,17},{18,... | collective-permute-start | bytes 3104 | tf_op jit(solution)/shard_map/ppermute | solution.py:18
  73.9 8.7 %collective-permute-start.26 = (f32[258,1]{1,0:T(8,128)S(1)}, f32[258,1]{1,0:T(8,128)S(1)}, u32[]{:S(2)}, u32[]{:S(2)}) collective-permute-start(f32[258,1]{1,0:T(8,128)S(1)} %get-tuple-element.14), channel_id=1, source_target_pairs={{1,0},{3,2},{5,4},{7,6},{9,8},{11,10},{13,12},{15,14},{17,16},{19,... | collective-permute-start | bytes 3104 | tf_op jit(solution)/shard_map/ppermute | solution.py:21
  75.7 14.2 %collective-permute-start.12 = (f32[1,256]{1,0:T(1,128)S(1)}, f32[1,256]{1,0:T(1,128)S(1)}, u32[]{:S(2)}, u32[]{:S(2)}) collective-permute-start(f32[1,256]{1,0:T(1,128)S(1)} %get-tuple-element.35), channel_id=1, source_target_pairs={{2,0},{4,2},{6,4},{8,6},{10,8},{12,10},{14,12},{3,1},{5,3},{7,5},{... | collective-permute-start | bytes 3080 | tf_op jit(solution)/shard_map/ppermute | solution.py:21
  80.6 9.3 %collective-permute-start.13 = (f32[1,256]{1,0:T(1,128)S(1)}, f32[1,256]{1,0:T(1,128)S(1)}, u32[]{:S(2)}, u32[]{:S(2)}) collective-permute-start(f32[1,256]{1,0:T(1,128)S(1)} %get-tuple-element.34), channel_id=1, source_target_pairs={{0,2},{2,4},{4,6},{6,8},{8,10},{10,12},{12,14},{1,3},{3,5},{5,7},{... | collective-permute-start | bytes 3080 | tf_op jit(solution)/shard_map/ppermute | solution.py:18
  83.1 10.7 %collective-permute-start.28 = (f32[1,256]{1,0:T(1,128)S(1)}, f32[1,256]{1,0:T(1,128)S(1)}, u32[]{:S(2)}, u32[]{:S(2)}) collective-permute-start(f32[1,256]{1,0:T(1,128)S(1)} %get-tuple-element.29), channel_id=1, source_target_pairs={{2,0},{4,2},{6,4},{8,6},{10,8},{12,10},{14,12},{3,1},{5,3},{7,5},{... | collective-permute-start | bytes 3080 | tf_op jit(solution)/shard_map/ppermute | solution.py:21
  88.0 6.7 %collective-permute-start.29 = (f32[1,256]{1,0:T(1,128)S(1)}, f32[1,256]{1,0:T(1,128)S(1)}, u32[]{:S(2)}, u32[]{:S(2)}) collective-permute-start(f32[1,256]{1,0:T(1,128)S(1)} %get-tuple-element.28), channel_id=1, source_target_pairs={{0,2},{2,4},{4,6},{6,8},{8,10},{10,12},{12,14},{1,3},{3,5},{5,7},{... | collective-permute-start | bytes 3080 | tf_op jit(solution)/shard_map/ppermute | solution.py:18
  90.0 9.4 %collective-permute-start.15 = (f32[258,1]{1,0:T(8,128)S(1)}, f32[258,1]{1,0:T(8,128)S(1)}, u32[]{:S(2)}, u32[]{:S(2)}) collective-permute-start(f32[258,1]{1,0:T(8,128)S(1)} %get-tuple-element.19), channel_id=1, source_target_pairs={{0,1},{2,3},{4,5},{6,7},{8,9},{10,11},{12,13},{14,15},{16,17},{18,... | collective-permute-start | bytes 3104 | tf_op jit(solution)/shard_map/ppermute | solution.py:18
  92.5 6.9 %collective-permute-start.14 = (f32[258,1]{1,0:T(8,128)S(1)}, f32[258,1]{1,0:T(8,128)S(1)}, u32[]{:S(2)}, u32[]{:S(2)}) collective-permute-start(f32[258,1]{1,0:T(8,128)S(1)} %get-tuple-element.18), channel_id=1, source_target_pairs={{1,0},{3,2},{5,4},{7,6},{9,8},{11,10},{13,12},{15,14},{17,16},{19,... | collective-permute-start | bytes 3104 | tf_op jit(solution)/shard_map/ppermute | solution.py:21
  94.8 4.7 %collective-permute-start.31 = (f32[258,1]{1,0:T(8,128)S(1)}, f32[258,1]{1,0:T(8,128)S(1)}, u32[]{:S(2)}, u32[]{:S(2)}) collective-permute-start(f32[258,1]{1,0:T(8,128)S(1)} %get-tuple-element.13), channel_id=1, source_target_pairs={{0,1},{2,3},{4,5},{6,7},{8,9},{10,11},{12,13},{14,15},{16,17},{18,... | collective-permute-start | bytes 3104 | tf_op jit(solution)/shard_map/ppermute | solution.py:18
  (17 other events, 103.3 us)
Sparse Core Ops, SparseCore 0:
  106.5 226.2 reduce-scatter.1
where the time goes:
time: 341 us; the launch traced here: 340 us
  waiting for transfers between devices  228 us (67%)
  starting transfers between devices  80 us (23%)
  between operations  14.8 us (4%)
  other arithmetic  9.41 us (3%)
  local copies, waits for them, and re-layouts  7.82 us (2%)
    reduce_scatter x1, waiting for transfers between devices, shards(): lax.psum_scatter(ordered, 'emit', scatter_dimension=0, tiled=True)  224 us
    ppermute x16, starting transfers between devices, with_halo(): lax.ppermute(lax.slice_in_dim(block, 0, width, axis=dim), axis, backward)  43.7 us
    ppermute x16, starting transfers between devices, with_halo(): lax.ppermute(lax.slice_in_dim(block, block.shape[dim] - width, None, axis...  36.2 us
  transfers between devices with their start and end apart: 33, of which 5 were waited for; matrix products, arithmetic and copies ran while one was open for 3% of the time, Pallas kernels for 0%

commit v1 on v0

v1 whole, which is shorter than its diff:
```python
import jax
import jax.numpy as jnp
from jax import lax
from jax.experimental import pallas as pl
from jax.experimental.pallas import tpu as pltpu
from jax.sharding import PartitionSpec as P

BR = 16
BC = 128
STEPS = 4
HALO = 4
SUB = 8
LANES = 128
FIELDS = 9
TILE_AT = 2 * SUB
VMEM_LIMIT = 48 * 1024 * 1024


def pack_kernel(fwd, adj, courant, decay, strength, side_out, top_out, low_out, cols, tops, lows, sem):
    rows = courant.shape[0]
    vy = lax.axis_index("vy")
    edge = pl.ds(pl.multiple_of((1 - vy) * LANES, LANES), LANES)
    copies = []
    for number, state in enumerate((fwd, adj)):
        at = pl.ds(3 * number, 3)
        copies.append((state.at[:, 0, :, edge], cols.at[at]))
        copies.append((state.at[:, 0, pl.ds(0, SUB), :], tops.at[at]))
        copies.append((state.at[:, 0, pl.ds(rows - SUB, SUB), :], lows.at[at]))
    for number, field in enumerate((courant, decay, strength)):
        copies.append((field.at[:, edge], cols.at[6 + number]))
        copies.append((field.at[pl.ds(0, SUB), :], tops.at[6 + number]))
        copies.append((field.at[pl.ds(rows - SUB, SUB), :], lows.at[6 + number]))
    started = [pltpu.make_async_copy(src, dst, sem.at[n]) for n, (src, dst) in enumerate(copies)]
    for copy in started:
        copy.start()
    for copy in started:
        copy.wait()
    lane = lax.broadcasted_iota(jnp.int32, (SUB, LANES), 1)

    def chunk(number, carry):
        at = pl.ds(pl.multiple_of(number * SUB, SUB), SUB)
        packed = jnp.zeros((SUB, LANES), jnp.float32)
        for field in range(FIELDS):
            moved = pltpu.roll(cols[field, at, :], HALO * field + HALO * (1 - vy), 1)
            here = (lane >= HALO * field) & (lane < HALO * (field + 1))
            packed = jnp.where(here, moved, packed)
        side_out[at, :] = packed
        return carry

    lax.fori_loop(0, rows // SUB, chunk, 0)
    for out, edges, first in ((top_out, tops, 0), (low_out, lows, SUB - HALO)):
        for field in range(FIELDS):
            out[HALO * field : HALO * (field + 1), :] = edges[field, first : first + HALO, :]
        out[HALO * FIELDS : HALO * (FIELDS + 1), :] = jnp.zeros((HALO, 2 * LANES), jnp.float32)


def pack(fwd_state, adj_state, courant, decay_rate, strength):
    rows, columns = courant.shape
    edge = jax.ShapeDtypeStruct((HALO * (FIELDS + 1), columns), jnp.float32)
    return pl.pallas_call(
        pack_kernel,
        out_shape=(jax.ShapeDtypeStruct((rows, LANES), jnp.float32), edge, edge),
        in_specs=[pl.BlockSpec(memory_space=pl.ANY)] * 5,
        out_specs=[pl.BlockSpec(memory_space=pltpu.VMEM)] * 3,
        scratch_shapes=[
            pltpu.VMEM((FIELDS, rows, LANES), jnp.float32),
            pltpu.VMEM((FIELDS, SUB, columns), jnp.float32),
            pltpu.VMEM((FIELDS, SUB, columns), jnp.float32),
            pltpu.SemaphoreType.DMA((15,)),
        ],
        compiler_params=pltpu.CompilerParams(vmem_limit_bytes=VMEM_LIMIT),
        cost_estimate=pl.CostEstimate(flops=600000, bytes_accessed=1500000, transcendentals=0),
        name="pack",
    )(fwd_state, adj_state, courant, decay_rate, strength)


def steps_kernel(
    scale, fwd, adj, courant, decay, strength, side, above, below, footprint, owner,
    ordered, pressure, held, fore, back, curves, partial, slot_of, gain_of, sem,
):
    rows = courant.shape[0]
    chunks = rows // SUB
    vy = lax.axis_index("vy")
    copies = []
    for half in range(2):
        columns = pl.ds(half * LANES, LANES)
        for number, state in enumerate((fwd, adj)):
            copies.append((state.at[:, 0, :, columns], held.at[pl.ds(3 * number, 3), half, pl.ds(TILE_AT, rows), :]))
        for number, field in enumerate((courant, decay, strength)):
            copies.append((field.at[:, columns], held.at[6 + number, half, pl.ds(TILE_AT, rows), :]))
    started = [pltpu.make_async_copy(src, dst, sem.at[n]) for n, (src, dst) in enumerate(copies)]
    for copy in started:
        copy.start()

    lane = lax.broadcasted_iota(jnp.int32, (SUB, LANES), 1)
    sub = lax.broadcasted_iota(jnp.int32, (SUB, LANES), 0)
    beside = (lane >= (LANES - HALO) * vy) & (lane < (LANES - HALO) * vy + HALO)
    zero = jnp.zeros((SUB, LANES), jnp.float32)
    first, last = sub == 0, sub == SUB - 1
    lane_first, lane_last = lane == 0, lane == LANES - 1

    def spread(strip, field):
        shift = lax.rem(LANES - HALO * field + (LANES - HALO) * vy, LANES)
        return jnp.where(beside, pltpu.roll(strip, shift, 1), zero)

    def clear(number, carry):
        gain_of[number] = jnp.float32(0.0)
        return carry

    lax.fori_loop(0, gain_of.shape[0], clear, 0)

    def list_block(number, carry):
        gain_of[footprint[number]] = jnp.float32(scale)
        return carry

    lax.fori_loop(0, footprint.shape[0], list_block, 0)

    def place(number, carry):
        slot_of[owner[number]] = number
        return carry

    lax.fori_loop(0, owner.shape[0], place, 0)

    for buffers in (held, fore, back):
        for field in range(buffers.shape[0]):
            for part in range(3):
                buffers[field, part, 0:SUB, :] = zero
                buffers[field, part, rows + 3 * SUB : rows + 4 * SUB, :] = zero
    corner_above = above[HALO * (FIELDS - 1) : HALO * (FIELDS + 1), 0:LANES]
    corner_below = pltpu.roll(below[HALO * (FIELDS - 1) : HALO * (FIELDS + 1), 0:LANES], HALO, 0)
    upper, lower = sub >= HALO, sub < HALO
    for field in range(FIELDS):
        at = (field // 2) * SUB
        for half in range(2):
            columns = slice(half * LANES, (half + 1) * LANES)
            value = above[at : at + SUB, columns]
            if field % 2 == 0:
                value = pltpu.roll(value, HALO, 0)
            held[field, half, SUB : 2 * SUB, :] = jnp.where(upper, value, zero)
            value = below[at : at + SUB, columns]
            if field % 2 == 1:
                value = pltpu.roll(value, HALO, 0)
            held[field, half, rows + 2 * SUB : rows + 3 * SUB, :] = jnp.where(lower, value, zero)
        held[field, 2, SUB : 2 * SUB, :] = jnp.where(upper, spread(corner_above, field), zero)
        held[field, 2, rows + 2 * SUB : rows + 3 * SUB, :] = jnp.where(lower, spread(corner_below, field), zero)

    def beside_tile(number, carry):
        strip = side[pl.ds(pl.multiple_of(number * SUB, SUB), SUB), :]
        at = pl.ds(pl.multiple_of(number * SUB + TILE_AT, SUB), SUB)
        for field in range(FIELDS):
            held[field, 2, at, :] = spread(strip, field)
        return carry

    lax.fori_loop(0, chunks, beside_tile, 0)
    for copy in started:
        copy.wait()

    def laplace(buffers, level, at):
        before = pl.ds(pl.multiple_of(at - SUB, SUB), SUB)
        now = pl.ds(pl.multiple_of(at, SUB), SUB)
        after = pl.ds(pl.multiple_of(at + SUB, SUB), SUB)
        centre = [buffers[level, part, now, :] for part in range(3)]
        right = [pltpu.roll(value, LANES - 1, 1) for value in centre]
        left = [pltpu.roll(value, 1, 1) for value in centre]
        result = []
        for part in range(3):
            up = jnp.where(first, pltpu.roll(buffers[level, part, before, :], 1, 0), pltpu.roll(centre[part], 1, 0))
            down = jnp.where(
                last, pltpu.roll(buffers[level, part, after, :], SUB - 1, 0), pltpu.roll(centre[part], SUB - 1, 0)
            )
            west = jnp.where(lane_first, left[(part + 2) % 3], left[part])
            east = jnp.where(lane_last, right[(part + 1) % 3], right[part])
            result.append((down + up) + (east + west) - 4.0 * centre[part])
        return centre, result

    def level_of(own, base, step):
        if step == 1:
            return held, base, held, base + 1
        if step == 2:
            return held, base + 1, own, 0
        return own, step - 3, own, step - 2

    for step in range(1, STEPS + 1):
        final = step == STEPS

        def advance(number, carry, step=step, final=final):
            at = number * SUB + (TILE_AT if final else SUB)
            now = pl.ds(pl.multiple_of(at, SUB), SUB)
            speed = [held[6, part, now, :] for part in range(3)]
            keep = [held[7, part, now, :] for part in range(3)]
            loss = [held[8, part, now, :] for part in range(3)]
            parts = range(2) if final else range(3)
            found = []
            for own, base in ((fore, 0), (back, 3)):
                old, old_at, new, new_at = level_of(own, base, step)
                centre, curve = laplace(new, new_at, at)
                seconds, nexts = [], []
                for part in parts:
                    memory = keep[part] * held[base + 2, part, now, :] + loss[part] * curve[part]
                    second = speed[part] * (curve[part] - memory)
                    following = 2.0 * centre[part] - old[old_at, part, now, :] + second
                    if not final:
                        held[base + 2, part, now, :] = memory
                        own[step - 1, part, now, :] = following
                    seconds.append(second)
                    nexts.append(following)
                found.append((seconds, nexts))
            seconds, nexts = found[0]
            adjoint = found[1][1]
            for part in range(2):
                if step <= 2:
                    curves[step - 1, part, now, :] = seconds[part]
                elif step == 3:
                    partial[part, now, :] = seconds[part] * back[1, part, now, :] + curves[1, part, now, :] * adjoint[part]
                else:
                    total = partial[part, now, :] + (
                        seconds[part] * back[0, part, now, :] + curves[0, part, now, :] * adjoint[part]
                    )
                    block = (number // 2) * 2 + part
                    inside = pl.ds(pl.multiple_of(lax.rem(number, 2) * SUB, SUB), SUB)
                    ordered[slot_of[block], inside, :] = total * gain_of[block]
                    tile = pl.ds(pl.multiple_of(number * SUB, SUB), SUB)
                    pressure[0, tile, part * LANES : (part + 1) * LANES] = nexts[part]
            return carry

        lax.fori_loop(0, chunks if final else chunks + 2, advance, 0)


def run_steps(scale, fwd_state, adj_state, courant, decay_rate, strength, side, above, below, footprint, owner_map):
    rows, columns = courant.shape
    blocks = owner_map.shape[0]
    extended = (3, rows + 4 * SUB, LANES)
    return pl.pallas_call(
        lambda *refs: steps_kernel(scale, *refs),
        out_shape=(
            jax.ShapeDtypeStruct((blocks, BR, BC), jnp.float32),
            jax.ShapeDtypeStruct((1, rows, columns), jnp.float32),
        ),
        in_specs=[pl.BlockSpec(memory_space=pl.ANY)] * 5
        + [pl.BlockSpec(memory_space=pltpu.VMEM)] * 3
        + [pl.BlockSpec(memory_space=pltpu.SMEM)] * 2,
        out_specs=[pl.BlockSpec(memory_space=pltpu.VMEM)] * 2,
        scratch_shapes=[
            pltpu.VMEM((FIELDS,) + extended, jnp.float32),
            pltpu.VMEM((STEPS - 1,) + extended, jnp.float32),
            pltpu.VMEM((STEPS - 1,) + extended, jnp.float32),
            pltpu.VMEM((2,) + extended, jnp.float32),
            pltpu.VMEM(extended, jnp.float32),
            pltpu.SMEM((blocks,), jnp.int32),
            pltpu.SMEM((blocks,), jnp.float32),
            pltpu.SemaphoreType.DMA((10,)),
        ],
        compiler_params=pltpu.CompilerParams(vmem_limit_bytes=VMEM_LIMIT),
        cost_estimate=pl.CostEstimate(flops=14000000, bytes_accessed=2900000, transcendentals=0),
        name="steps",
    )(fwd_state, adj_state, courant, decay_rate, strength, side, above, below, footprint, owner_map)


def shards(fwd_state, adj_state, courant, decay_rate, strength, footprint, owner_map):
    groups = lax.axis_size("emit")
    tiles = lax.axis_size("vx")
    rows = courant.shape[0]
    fields = (fwd_state, adj_state, courant, decay_rate, strength)
    side, top, low = pack(*fields)
    side = lax.ppermute(side, "vy", [(0, 1), (1, 0)])
    corners = (HALO * FIELDS, 0)
    top = lax.dynamic_update_slice(top, side[:HALO], corners)
    low = lax.dynamic_update_slice(low, side[rows - HALO :], corners)
    below = lax.ppermute(top, "vx", [(i + 1, i) for i in range(tiles - 1)])
    above = lax.ppermute(low, "vx", [(i, i + 1) for i in range(tiles - 1)])
    ordered, pressure = run_steps(
        1.0 / groups, *fields, side, above, below, footprint.reshape(-1), owner_map.reshape(-1)
    )
    sent = lax.all_to_all(ordered, "emit", 0, 0, tiled=True)
    gradient = jnp.sum(sent.reshape(groups, -1, BR, BC), axis=0)
    return gradient, pressure


def solution(mesh):
    in_specs = (
        P(None, "emit", "vx", "vy"),
        P(None, "emit", "vx", "vy"),
        P("vx", "vy"),
        P("vx", "vy"),
        P("vx", "vy"),
        P("emit", "vx", "vy", None),
        P("vx", "vy", None),
    )
    out_specs = (P("emit", "vx", "vy"), P("emit", "vx", "vy"))
    return jax.shard_map(shards, mesh=mesh, in_specs=in_specs, out_specs=out_specs, check_vma=False)
```

time: 341 us -> 64 us (0.19)
  the two profiles are of different devices: /device:TPU:40 before, /device:TPU:32 now
where the time goes in v1:
time: 64 us; the launch traced here: 63.6 us
  blocking collectives  24.2 us (38%)
  Pallas kernels  19.6 us (31%)
  starting transfers between devices  7.75 us (12%)
  local copies, waits for them, and re-layouts  5.79 us (9%)
  waiting for transfers between devices  4.93 us (8%)
  between operations  0.69 us (1%)
    all_to_all x1, blocking collectives, shards(): sent = lax.all_to_all(ordered, 'emit', 0, 0, tiled=True)  24.2 us
    pallas_call x1, Pallas kernels, run_steps(): pl.pallas_call(lambda *refs: steps_kernel(scale, *refs), out_shape=(jax.S...  16.7 us
    unnamed x14, local copies, waits for them, and re-layouts  5.78 us
    ppermute x1, waiting for transfers between devices, shards(): above = lax.ppermute(low, 'vx', [(i, i + 1) for i in range(tiles - 1)])  3.58 us
    ppermute x1, starting transfers between devices, shards(): above = lax.ppermute(low, 'vx', [(i, i + 1) for i in range(tiles - 1)])  3.48 us
    pallas_call x1, Pallas kernels, pack(): pl.pallas_call(pack_kernel, out_shape=(jax.ShapeDtypeStruct((rows, LANES)...  2.91 us
    ppermute x1, starting transfers between devices, shards(): below = lax.ppermute(top, 'vx', [(i + 1, i) for i in range(tiles - 1)])  2.35 us
    ppermute x1, starting transfers between devices, shards(): side = lax.ppermute(side, 'vy', [(0, 1), (1, 0)])  1.92 us
  transfers between devices with their start and end apart: 3, of which 2 were waited for; matrix products, arithmetic and copies ran while one was open for 0% of the time, Pallas kernels for 0%

profile of v1, /device:TPU:32, one launch (start us, length us, event | category | flops | bytes accessed | tf_op | source)
XLA Modules:
  0.0 63.6 jit_solution(11094255554191404673)
XLA Ops:
  0.6 0.0 copy-start
  0.6 1.1 %copy-done = f32[3,1,256,256]{3,2,1,0:T(8,128)S(1)} copy-done((f32[3,1,256,256]{3,2,1,0:T(8,128)S(1)}, f32[3,1,256,256]{3,2,1,0:T(8,128)}, u32[]{:S(2)}) %copy-start) | copy-done | bytes 786456
  1.8 0.0 copy-start.1
  1.8 1.1 %copy-done.1 = f32[3,1,256,256]{3,2,1,0:T(8,128)S(1)} copy-done((f32[3,1,256,256]{3,2,1,0:T(8,128)S(1)}, f32[3,1,256,256]{3,2,1,0:T(8,128)}, u32[]{:S(2)}) %copy-start.1) | copy-done | bytes 786456
  2.9 0.0 copy-start.2
  2.9 0.9 %copy-done.2 = f32[256,256]{1,0:T(8,128)S(1)} copy-done((f32[256,256]{1,0:T(8,128)S(1)}, f32[256,256]{1,0:T(8,128)}, u32[]{:S(2)}) %copy-start.2) | copy-done | bytes 262168
  3.8 0.0 copy-start.3
  3.9 0.9 %copy-done.3 = f32[256,256]{1,0:T(8,128)S(1)} copy-done((f32[256,256]{1,0:T(8,128)S(1)}, f32[256,256]{1,0:T(8,128)}, u32[]{:S(2)}) %copy-start.3) | copy-done | bytes 262168
  4.8 0.0 copy-start.4
  4.8 0.9 %copy-done.4 = f32[256,256]{1,0:T(8,128)S(1)} copy-done((f32[256,256]{1,0:T(8,128)S(1)}, f32[256,256]{1,0:T(8,128)}, u32[]{:S(2)}) %copy-start.4) | copy-done | bytes 262168
  5.8 2.9 %pack.1 = (f32[256,128]{1,0:T(8,128)S(1)}, f32[40,256]{1,0:T(8,128)S(1)}, f32[40,256]{1,0:T(8,128)S(1)}) custom-call(f32[3,1,256,256]{3,2,1,0:T(8,128)S(1)} %copy-done, f32[3,1,256,256]{3,2,1,0:T(8,128)S(1)} %copy-done.1, f32[256,256]{1,0:T(8,128)S(1)} %copy-done.2, f32[256,256]{1,0:T(8,128)S(1)} %copy-done.3, f32[256,256]{1,0:T(8,128)S(1)} %copy-done.4), custom_call_target="tpu_custom_call" | custom-call | flops 600000 | bytes 1500000 | tf_op jit(solution)/shard_map/pack/pallas_call | solution.py:60
  8.7 1.9 %collective-permute-start = (f32[256,128]{1,0:T(8,128)S(1)}, f32[256,128]{1,0:T(8,128)S(1)}, u32[]{:S(2)}, u32[]{:S(2)}) collective-permute-start(f32[256,128]{1,0:T(8,128)S(1)} %get-tuple-element.7), channel_id=1, source_target_pairs={{0,1},{1,0},{2,3},{3,2},{4,5},{5,4},{6,7},{7,6},{8,9},{9,8},{10,11... | collective-permute-start | bytes 393224 | tf_op jit(solution)/shard_map/ppermute | solution.py:265
  10.6 1.3 %collective-permute-done.refs_5_ = f32[256,128]{1,0:T(8,128)S(1)} collective-permute-done((f32[256,128]{1,0:T(8,128)S(1)}, f32[256,128]{1,0:T(8,128)S(1)}, u32[]{:S(2)}, u32[]{:S(2)}) %collective-permute-start) | collective-permute-done | bytes 131104 | tf_op jit(solution)/shard_map/ppermute | solution.py:265
  11.9 2.3 %collective-permute-start.2 = (f32[40,256]{1,0:T(8,128)S(1)}, f32[40,256]{1,0:T(8,128)S(1)}, u32[]{:S(2)}, u32[]{:S(2)}) collective-permute-start(f32[40,256]{1,0:T(8,128)S(1)} %get-tuple-element.12), channel_id=1, source_target_pairs={{2,0},{4,2},{6,4},{8,6},{10,8},{12,10},{14,12},{3,1},{5,3},{7,5},{... | collective-permute-start | bytes 122888 | tf_op jit(solution)/shard_map/ppermute | solution.py:269
  14.3 3.5 %collective-permute-start.1 = (f32[40,256]{1,0:T(8,128)S(1)}, f32[40,256]{1,0:T(8,128)S(1)}, u32[]{:S(2)}, u32[]{:S(2)}) collective-permute-start(f32[40,256]{1,0:T(8,128)S(1)} %get-tuple-element.13), channel_id=1, source_target_pairs={{0,2},{2,4},{4,6},{6,8},{8,10},{10,12},{12,14},{1,3},{3,5},{5,7},{... | collective-permute-start | bytes 122888 | tf_op jit(solution)/shard_map/ppermute | solution.py:270
  17.8 0.0 collective-permute-done.2.refs_7_
  17.8 3.6 %collective-permute-done.1.refs_6_ = f32[40,256]{1,0:T(8,128)S(1)} collective-permute-done((f32[40,256]{1,0:T(8,128)S(1)}, f32[40,256]{1,0:T(8,128)S(1)}, u32[]{:S(2)}, u32[]{:S(2)}) %collective-permute-start.1) | collective-permute-done | bytes 40992 | tf_op jit(solution)/shard_map/ppermute | solution.py:270
  21.4 0.0 copy-start.5
  21.4 0.0 copy-start.6
  21.4 0.7 %copy-done.5 = s32[1,1,1,16]{3,2,1,0:T(1,128)S(1)} copy-done((s32[1,1,1,16]{3,2,1,0:T(1,128)S(1)}, s32[1,1,1,16]{3,2,1,0:T(1,128)}, u32[]{:S(2)}) %copy-start.5) | copy-done | bytes 88
  22.0 0.0 copy-done.6
  22.1 16.7 %steps.1 = (f32[32,16,128]{2,1,0:T(8,128)S(1)}, f32[1,256,256]{2,1,0:T(8,128)}) custom-call(f32[3,1,256,256]{3,2,1,0:T(8,128)S(1)} %copy-done, f32[3,1,256,256]{3,2,1,0:T(8,128)S(1)} %copy-done.1, f32[256,256]{1,0:T(8,128)S(1)} %copy-done.2, f32[256,256]{1,0:T(8,128)S(1)} %copy-done.3, f32[256,256]{1,0:T(8,128)S(1)} %copy-done.4, ...), custom_call_target="tpu_custom_call" | custom-call | flops 14000000 | bytes 2900000 | tf_op jit(solution)/shard_map/steps/pallas_call | solution.py:233
  38.8 24.2 %all_to_all.5 = f32[32,16,128]{2,1,0:T(8,128)S(1)} all-to-all(f32[32,16,128]{2,1,0:T(8,128)S(1)} %get-tuple-element.10), channel_id=1, replica_groups=mesh['emit'=32,'vx'=8,'vy'=2] {'emit'}, dimensions={0} | all-to-all | bytes 524288 | tf_op jit(solution)/shard_map/all_to_all | solution.py:274
  63.0 0.6 reduce_sum.11
  (1 shorter events, 0.0 us)
Async XLA Ops:
  0.6 1.1 %copy-start = (f32[3,1,256,256]{3,2,1,0:T(8,128)S(1)}, f32[3,1,256,256]{3,2,1,0:T(8,128)}, u32[]{:S(2)}) copy-start(f32[3,1,256,256]{3,2,1,0:T(8,128)} %refs_0_.1) | copy-start | bytes 2359300
  1.8 1.1 %copy-start.1 = (f32[3,1,256,256]{3,2,1,0:T(8,128)S(1)}, f32[3,1,256,256]{3,2,1,0:T(8,128)}, u32[]{:S(2)}) copy-start(f32[3,1,256,256]{3,2,1,0:T(8,128)} %refs_1_.1) | copy-start | bytes 2359300
  2.9 0.9 %copy-start.2 = (f32[256,256]{1,0:T(8,128)S(1)}, f32[256,256]{1,0:T(8,128)}, u32[]{:S(2)}) copy-start(f32[256,256]{1,0:T(8,128)} %refs_2_.1) | copy-start | bytes 786436
  3.8 0.9 %copy-start.3 = (f32[256,256]{1,0:T(8,128)S(1)}, f32[256,256]{1,0:T(8,128)}, u32[]{:S(2)}) copy-start(f32[256,256]{1,0:T(8,128)} %refs_3_.1) | copy-start | bytes 786436
  4.8 0.9 %copy-start.4 = (f32[256,256]{1,0:T(8,128)S(1)}, f32[256,256]{1,0:T(8,128)}, u32[]{:S(2)}) copy-start(f32[256,256]{1,0:T(8,128)} %refs_4_.1) | copy-start | bytes 786436
  8.7 3.2 %collective-permute-start = (f32[256,128]{1,0:T(8,128)S(1)}, f32[256,128]{1,0:T(8,128)S(1)}, u32[]{:S(2)}, u32[]{:S(2)}) collective-permute-start(f32[256,128]{1,0:T(8,128)S(1)} %get-tuple-element.7), channel_id=1, source_target_pairs={{0,1},{1,0},{2,3},{3,2},{4,5},{5,4},{6,7},{7,6},{8,9},{9,8},{10,11... | collective-permute-start | bytes 393224 | tf_op jit(solution)/shard_map/ppermute | solution.py:265
  11.9 5.9 %collective-permute-start.2 = (f32[40,256]{1,0:T(8,128)S(1)}, f32[40,256]{1,0:T(8,128)S(1)}, u32[]{:S(2)}, u32[]{:S(2)}) collective-permute-start(f32[40,256]{1,0:T(8,128)S(1)} %get-tuple-element.12), channel_id=1, source_target_pairs={{2,0},{4,2},{6,4},{8,6},{10,8},{12,10},{14,12},{3,1},{5,3},{7,5},{... | collective-permute-start | bytes 122888 | tf_op jit(solution)/shard_map/ppermute | solution.py:269
  14.3 7.1 %collective-permute-start.1 = (f32[40,256]{1,0:T(8,128)S(1)}, f32[40,256]{1,0:T(8,128)S(1)}, u32[]{:S(2)}, u32[]{:S(2)}) collective-permute-start(f32[40,256]{1,0:T(8,128)S(1)} %get-tuple-element.13), channel_id=1, source_target_pairs={{0,2},{2,4},{4,6},{6,8},{8,10},{10,12},{12,14},{1,3},{3,5},{5,7},{... | collective-permute-start | bytes 122888 | tf_op jit(solution)/shard_map/ppermute | solution.py:270
  21.4 0.7 %copy-start.5 = (s32[1,1,1,16]{3,2,1,0:T(1,128)S(1)}, s32[1,1,1,16]{3,2,1,0:T(1,128)}, u32[]{:S(2)}) copy-start(s32[1,1,1,16]{3,2,1,0:T(1,128)} %param.12) | copy-start | bytes 196
  21.4 0.7 %copy-start.6 = (s32[1,1,32]{2,1,0:T(1,128)S(1)}, s32[1,1,32]{2,1,0:T(1,128)}, u32[]{:S(2)}) copy-start(s32[1,1,32]{2,1,0:T(1,128)} %param.13) | copy-start | bytes 388

commit v2 on v1

v2 whole, which is shorter than its diff:
```python
import jax
import jax.numpy as jnp
from jax import lax
from jax.experimental import pallas as pl
from jax.experimental.pallas import tpu as pltpu
from jax.sharding import PartitionSpec as P

BR = 16
BC = 128
STEPS = 4
HALO = 4
SUB = 8
LANES = 128
FIELDS = 9
TILE_AT = 2 * SUB
VMEM_LIMIT = 48 * 1024 * 1024
GROUP = (13, 37, 35, 33)


def pack_kernel(fwd, adj, courant, decay, strength, side_out, top_out, low_out, cols, tops, lows, sem):
    rows = courant.shape[0]
    vy = lax.axis_index("vy")
    edge = pl.ds(pl.multiple_of((1 - vy) * LANES, LANES), LANES)
    copies = []
    for number, state in enumerate((fwd, adj)):
        at = pl.ds(3 * number, 3)
        copies.append((state.at[:, 0, :, edge], cols.at[at]))
        copies.append((state.at[:, 0, pl.ds(0, SUB), :], tops.at[at]))
        copies.append((state.at[:, 0, pl.ds(rows - SUB, SUB), :], lows.at[at]))
    for number, field in enumerate((courant, decay, strength)):
        copies.append((field.at[:, edge], cols.at[6 + number]))
        copies.append((field.at[pl.ds(0, SUB), :], tops.at[6 + number]))
        copies.append((field.at[pl.ds(rows - SUB, SUB), :], lows.at[6 + number]))
    started = [pltpu.make_async_copy(src, dst, sem.at[n]) for n, (src, dst) in enumerate(copies)]
    for copy in started:
        copy.start()
    for copy in started:
        copy.wait()
    lane = lax.broadcasted_iota(jnp.int32, (SUB, LANES), 1)

    for at in range(0, rows, SUB):
        packed = jnp.zeros((SUB, LANES), jnp.float32)
        for field in range(FIELDS):
            moved = pltpu.roll(cols[field, at : at + SUB, :], HALO * field + HALO * (1 - vy), 1)
            here = (lane >= HALO * field) & (lane < HALO * (field + 1))
            packed = jnp.where(here, moved, packed)
        side_out[at : at + SUB, :] = packed
    for out, edges, first in ((top_out, tops, 0), (low_out, lows, SUB - HALO)):
        for field in range(FIELDS):
            out[HALO * field : HALO * (field + 1), :] = edges[field, first : first + HALO, :]
        out[HALO * FIELDS : HALO * (FIELDS + 1), :] = jnp.zeros((HALO, 2 * LANES), jnp.float32)


def pack(fwd_state, adj_state, courant, decay_rate, strength):
    rows, columns = courant.shape
    edge = jax.ShapeDtypeStruct((HALO * (FIELDS + 1), columns), jnp.float32)
    return pl.pallas_call(
        pack_kernel,
        out_shape=(jax.ShapeDtypeStruct((rows, LANES), jnp.float32), edge, edge),
        in_specs=[pl.BlockSpec(memory_space=pltpu.HBM)] * 5,
        out_specs=[pl.BlockSpec(memory_space=pltpu.VMEM)] * 3,
        scratch_shapes=[
            pltpu.VMEM((FIELDS, rows, LANES), jnp.float32),
            pltpu.VMEM((FIELDS, SUB, columns), jnp.float32),
            pltpu.VMEM((FIELDS, SUB, columns), jnp.float32),
            pltpu.SemaphoreType.DMA((15,)),
        ],
        compiler_params=pltpu.CompilerParams(vmem_limit_bytes=VMEM_LIMIT),
        cost_estimate=pl.CostEstimate(flops=600000, bytes_accessed=1500000, transcendentals=0),
        name="pack",
    )(fwd_state, adj_state, courant, decay_rate, strength)


def steps_kernel(
    scale, fwd, adj, courant, decay, strength, side, above, below, footprint, owner,
    ordered, pressure, held, coefs, starts, memories, fore, back, curves, partial, found_g, found_p,
    slot_of, gain_of, sem, out_sem,
):
    rows = courant.shape[0]
    vy = lax.axis_index("vy")
    copies = []
    for half in range(2):
        columns = pl.ds(half * LANES, LANES)
        for number, state in enumerate((fwd, adj)):
            copies.append((state.at[:, 0, :, columns], held.at[pl.ds(3 * number, 3), half, pl.ds(TILE_AT, rows), :]))
        for number, field in enumerate((courant, decay, strength)):
            copies.append((field.at[:, columns], held.at[6 + number, half, pl.ds(TILE_AT, rows), :]))
    started = [pltpu.make_async_copy(src, dst, sem.at[n]) for n, (src, dst) in enumerate(copies)]
    for copy in started:
        copy.start()

    lane = lax.broadcasted_iota(jnp.int32, (SUB, LANES), 1)
    sub = lax.broadcasted_iota(jnp.int32, (SUB, LANES), 0)
    beside = (lane >= (LANES - HALO) * vy) & (lane < (LANES - HALO) * vy + HALO)
    zero = jnp.zeros((SUB, LANES), jnp.float32)
    lane_first, lane_last = lane == 0, lane == LANES - 1

    def spread(strip, field):
        shift = lax.rem(LANES - HALO * field + (LANES - HALO) * vy, LANES)
        return jnp.where(beside, pltpu.roll(strip, shift, 1), zero)

    for block in range(gain_of.shape[0]):
        gain_of[block] = jnp.float32(0.0)
    for number in range(footprint.shape[0]):
        gain_of[footprint[number]] = jnp.float32(scale)
    for number in range(owner.shape[0]):
        slot_of[owner[number]] = number

    corner_above = above[HALO * (FIELDS - 1) : HALO * (FIELDS + 1), 0:LANES]
    corner_below = pltpu.roll(below[HALO * (FIELDS - 1) : HALO * (FIELDS + 1), 0:LANES], HALO, 0)
    upper, lower = sub >= HALO, sub < HALO
    for field in range(FIELDS):
        at = (field // 2) * SUB
        for half in range(2):
            columns = slice(half * LANES, (half + 1) * LANES)
            value = above[at : at + SUB, columns]
            if field % 2 == 0:
                value = pltpu.roll(value, HALO, 0)
            held[field, half, SUB : 2 * SUB, :] = jnp.where(upper, value, zero)
            value = below[at : at + SUB, columns]
            if field % 2 == 1:
                value = pltpu.roll(value, HALO, 0)
            held[field, half, rows + 2 * SUB : rows + 3 * SUB, :] = jnp.where(lower, value, zero)
        held[field, 2, SUB : 2 * SUB, :] = jnp.where(upper, spread(corner_above, field), zero)
        held[field, 2, rows + 2 * SUB : rows + 3 * SUB, :] = jnp.where(lower, spread(corner_below, field), zero)
    for at in range(0, rows, SUB):
        strip = side[at : at + SUB, :]
        for field in range(FIELDS):
            held[field, 2, TILE_AT + at : TILE_AT + at + SUB, :] = spread(strip, field)
    for copy in started:
        copy.wait()

    pitch = rows // SUB + 1

    def strips(field, part, t):
        return held[field, part, pl.ds(TILE_AT - HALO + t, SUB, stride=pitch), :]

    def advance(step, base_t, group):
        final = step == STEPS
        parts = range(2) if final else range(3)
        ts = [base_t + g for g in range(group)]
        stores = []
        speed, keep, loss = {}, {}, {}
        for part in parts:
            for g, t in enumerate(ts):
                for number, of in enumerate((speed, keep, loss)):
                    if step == 1:
                        of[part, g] = strips(6 + number, part, t)
                        stores.append((coefs, (number, part, SUB + t), of[part, g]))
                    else:
                        of[part, g] = coefs[number, part, SUB + t]
        results = []
        for own, state in ((fore, 0), (back, 1)):

            def level(number, part, t, own=own, state=state):
                if number >= 2:
                    return own[number - 2, part, SUB + t]
                if step == 1:
                    return strips(3 * state + number, part, t)
                return starts[state, part, SUB + t]

            centre = {
                (part, g): level(step, part, base_t + g)
                for part in range(3)
                for g in range(-1, group + 1)
                if part in parts or 0 <= g < group
            }
            seconds, nexts = {}, {}
            for g, t in enumerate(ts):
                right = [pltpu.roll(centre[part, g], LANES - 1, 1) for part in range(3)]
                left = [pltpu.roll(centre[part, g], 1, 1) for part in range(3)]
                for part in parts:
                    west = jnp.where(lane_first, left[(part + 2) % 3], left[part])
                    east = jnp.where(lane_last, right[(part + 1) % 3], right[part])
                    now = centre[part, g]
                    curve = (centre[part, g - 1] + centre[part, g + 1]) + (east + west) - 4.0 * now
                    memory = strips(3 * state + 2, part, t) if step == 1 else memories[state, part, SUB + t]
                    memory = keep[part, g] * memory + loss[part, g] * curve
                    second = speed[part, g] * (curve - memory)
                    following = 2.0 * now - level(step - 1, part, t) + second
                    if step == 1:
                        stores.append((starts, (state, part, SUB + t), now))
                    if not final:
                        stores.append((memories, (state, part, SUB + t), memory))
                        stores.append((own, (step - 1, part, SUB + t), following))
                    seconds[part, g] = second
                    nexts[part, g] = following
            results.append((seconds, nexts))
        (seconds, nexts), (_, adjoint) = results
        for part in range(2):
            for g, t in enumerate(ts):
                if step <= 2:
                    stores.append((curves, (step - 1, part, SUB + t), seconds[part, g]))
                    continue
                other = 4 - step
                value = (
                    seconds[part, g] * back[other, part, SUB + t] + curves[other, part, SUB + t] * adjoint[part, g]
                )
                if step == 3:
                    stores.append((partial, (part, SUB + t), value))
                else:
                    rows_at = pl.ds(HALO + t, SUB, stride=pitch)
                    stores.append((found_g, (part, rows_at), partial[part, SUB + t] + value))
                    stores.append((found_p, (part, rows_at), nexts[part, g]))
        for ref, index, value in stores:
            ref[index] = value

    for step in range(1, STEPS + 1):
        margin = STEPS - step
        count = pitch + 2 * margin
        group = GROUP[step - 1]
        if count == group:
            advance(step, -margin, group)
        else:

            def turn(number, carry, step=step, margin=margin, group=group):
                advance(step, number * group - margin, group)
                return carry

            lax.fori_loop(0, count // group, turn, 0)

    leaving = [
        pltpu.make_async_copy(
            found_p.at[half, pl.ds(SUB, rows), :], pressure.at[0, :, pl.ds(half * LANES, LANES)], out_sem.at[half]
        )
        for half in range(2)
    ]
    for copy in leaving:
        copy.start()
    for block in range(gain_of.shape[0]):
        at = SUB + (block // 2) * BR
        ordered[slot_of[block]] = found_g[block % 2, at : at + BR, :] * gain_of[block]
    for copy in leaving:
        copy.wait()


def run_steps(scale, fwd_state, adj_state, courant, decay_rate, strength, side, above, below, footprint, owner_map):
    rows, columns = courant.shape
    blocks = owner_map.shape[0]
    strip = (3, rows // SUB + 16, SUB, LANES)
    found = (2, rows + 6 * SUB, LANES)
    return pl.pallas_call(
        lambda *refs: steps_kernel(scale, *refs),
        out_shape=(
            jax.ShapeDtypeStruct((blocks, BR, BC), jnp.float32),
            jax.ShapeDtypeStruct((1, rows, columns), jnp.float32),
        ),
        in_specs=[pl.BlockSpec(memory_space=pltpu.HBM)] * 5
        + [pl.BlockSpec(memory_space=pltpu.VMEM)] * 3
        + [pl.BlockSpec(memory_space=pltpu.SMEM)] * 2,
        out_specs=[pl.BlockSpec(memory_space=pltpu.VMEM), pl.BlockSpec(memory_space=pltpu.HBM)],
        scratch_shapes=[
            pltpu.VMEM((FIELDS, 3, rows + 7 * SUB, LANES), jnp.float32),
            pltpu.VMEM((3,) + strip, jnp.float32),
            pltpu.VMEM((2,) + strip, jnp.float32),
            pltpu.VMEM((2,) + strip, jnp.float32),
            pltpu.VMEM((STEPS - 1,) + strip, jnp.float32),
            pltpu.VMEM((STEPS - 1,) + strip, jnp.float32),
            pltpu.VMEM((2,) + strip, jnp.float32),
            pltpu.VMEM(strip, jnp.float32),
            pltpu.VMEM(found, jnp.float32),
            pltpu.VMEM(found, jnp.float32),
            pltpu.SMEM((blocks,), jnp.int32),
            pltpu.SMEM((blocks,), jnp.float32),
            pltpu.SemaphoreType.DMA((10,)),
            pltpu.SemaphoreType.DMA((2,)),
        ],
        compiler_params=pltpu.CompilerParams(vmem_limit_bytes=VMEM_LIMIT),
        cost_estimate=pl.CostEstimate(flops=14000000, bytes_accessed=2900000, transcendentals=0),
        name="steps",
    )(fwd_state, adj_state, courant, decay_rate, strength, side, above, below, footprint, owner_map)


def shards(fwd_state, adj_state, courant, decay_rate, strength, footprint, owner_map):
    groups = lax.axis_size("emit")
    tiles = lax.axis_size("vx")
    rows = courant.shape[0]
    fields = (fwd_state, adj_state, courant, decay_rate, strength)
    side, top, low = pack(*fields)
    side = lax.ppermute(side, "vy", [(0, 1), (1, 0)])
    corners = (HALO * FIELDS, 0)
    top = lax.dynamic_update_slice(top, side[:HALO], corners)
    low = lax.dynamic_update_slice(low, side[rows - HALO :], corners)
    below = lax.ppermute(top, "vx", [(i + 1, i) for i in range(tiles - 1)])
    above = lax.ppermute(low, "vx", [(i, i + 1) for i in range(tiles - 1)])
    ordered, pressure = run_steps(
        1.0 / groups, *fields, side, above, below, footprint.reshape(-1), owner_map.reshape(-1)
    )
    sent = lax.all_to_all(ordered, "emit", 0, 0, tiled=True)
    gradient = jnp.sum(sent.reshape(groups, -1, BR, BC), axis=0)
    return gradient, pressure


def solution(mesh):
    in_specs = (
        P(None, "emit", "vx", "vy"),
        P(None, "emit", "vx", "vy"),
        P("vx", "vy"),
        P("vx", "vy"),
        P("vx", "vy"),
        P("emit", "vx", "vy", None),
        P("vx", "vy", None),
    )
    out_specs = (P("emit", "vx", "vy"), P("emit", "vx", "vy"))
    return jax.shard_map(shards, mesh=mesh, in_specs=in_specs, out_specs=out_specs, check_vma=False)
```

time: 64 us -> 49.3 us (0.77)
  Pallas kernels: 19.6 us -> 4.92 us
    pallas_call x1, Pallas kernels: 16.7 us -> 4.19 us  [run_steps(): pl.pallas_call(lambda *refs: steps_kernel(scale, *refs), out_shape=(jax.S...]
    pallas_call x1, Pallas kernels: 2.91 us -> 0.72 us  [pack(): pl.pallas_call(pack_kernel, out_shape=(jax.ShapeDtypeStruct((rows, LANES)...]
where the time goes in v2:
time: 49.3 us; the launch traced here: 48.9 us
  blocking collectives  24.2 us (49%)
  starting transfers between devices  7.75 us (16%)
  local copies, waits for them, and re-layouts  5.79 us (12%)
  waiting for transfers between devices  4.93 us (10%)
  Pallas kernels  4.92 us (10%)
  between operations  0.69 us (1%)
  other arithmetic  0.63 us (1%)
    all_to_all x1, blocking collectives, shards(): sent = lax.all_to_all(ordered, 'emit', 0, 0, tiled=True)  24.2 us
    unnamed x14, local copies, waits for them, and re-layouts  5.78 us
    pallas_call x1, Pallas kernels, run_steps(): pl.pallas_call(lambda *refs: steps_kernel(scale, *refs), out_shape=(jax.S...  4.19 us
    ppermute x1, waiting for transfers between devices, shards(): above = lax.ppermute(low, 'vx', [(i, i + 1) for i in range(tiles - 1)])  3.58 us
    ppermute x1, starting transfers between devices, shards(): above = lax.ppermute(low, 'vx', [(i, i + 1) for i in range(tiles - 1)])  3.48 us
    ppermute x1, starting transfers between devices, shards(): below = lax.ppermute(top, 'vx', [(i + 1, i) for i in range(tiles - 1)])  2.35 us
    ppermute x1, starting transfers between devices, shards(): side = lax.ppermute(side, 'vy', [(0, 1), (1, 0)])  1.92 us
    ppermute x1, waiting for transfers between devices, shards(): side = lax.ppermute(side, 'vy', [(0, 1), (1, 0)])  1.31 us
  transfers between devices with their start and end apart: 3, of which 2 were waited for; matrix products, arithmetic and copies ran while one was open for 0% of the time, Pallas kernels for 0%

profile of v2, /device:TPU:32, one launch (start us, length us, event | category | flops | bytes accessed | tf_op | source)
XLA Modules:
  0.0 48.9 jit_solution(2886827745613651516)
XLA Ops:
  0.6 0.0 copy-start
  0.6 1.1 %copy-done = f32[3,1,256,256]{3,2,1,0:T(8,128)S(1)} copy-done((f32[3,1,256,256]{3,2,1,0:T(8,128)S(1)}, f32[3,1,256,256]{3,2,1,0:T(8,128)}, u32[]{:S(2)}) %copy-start) | copy-done | bytes 786456
  1.8 0.0 copy-start.1
  1.8 1.1 %copy-done.1 = f32[3,1,256,256]{3,2,1,0:T(8,128)S(1)} copy-done((f32[3,1,256,256]{3,2,1,0:T(8,128)S(1)}, f32[3,1,256,256]{3,2,1,0:T(8,128)}, u32[]{:S(2)}) %copy-start.1) | copy-done | bytes 786456
  2.9 0.0 copy-start.2
  2.9 0.9 %copy-done.2 = f32[256,256]{1,0:T(8,128)S(1)} copy-done((f32[256,256]{1,0:T(8,128)S(1)}, f32[256,256]{1,0:T(8,128)}, u32[]{:S(2)}) %copy-start.2) | copy-done | bytes 262168
  3.8 0.0 copy-start.3
  3.9 0.9 %copy-done.3 = f32[256,256]{1,0:T(8,128)S(1)} copy-done((f32[256,256]{1,0:T(8,128)S(1)}, f32[256,256]{1,0:T(8,128)}, u32[]{:S(2)}) %copy-start.3) | copy-done | bytes 262168
  4.8 0.0 copy-start.4
  4.8 0.9 %copy-done.4 = f32[256,256]{1,0:T(8,128)S(1)} copy-done((f32[256,256]{1,0:T(8,128)S(1)}, f32[256,256]{1,0:T(8,128)}, u32[]{:S(2)}) %copy-start.4) | copy-done | bytes 262168
  5.8 0.7 %pack.1 = (f32[256,128]{1,0:T(8,128)S(1)}, f32[40,256]{1,0:T(8,128)S(1)}, f32[40,256]{1,0:T(8,128)S(1)}) custom-call(f32[3,1,256,256]{3,2,1,0:T(8,128)S(1)} %copy-done, f32[3,1,256,256]{3,2,1,0:T(8,128)S(1)} %copy-done.1, f32[256,256]{1,0:T(8,128)S(1)} %copy-done.2, f32[256,256]{1,0:T(8,128)S(1)} %copy-done.3, f32[256,256]{1,0:T(8,128)S(1)} %copy-done.4), custom_call_target="tpu_custom_call" | custom-call | flops 600000 | bytes 1500000 | tf_op jit(solution)/shard_map/pack/pallas_call | solution.py:57
  6.5 1.9 %collective-permute-start = (f32[256,128]{1,0:T(8,128)S(1)}, f32[256,128]{1,0:T(8,128)S(1)}, u32[]{:S(2)}, u32[]{:S(2)}) collective-permute-start(f32[256,128]{1,0:T(8,128)S(1)} %get-tuple-element.7), channel_id=1, source_target_pairs={{0,1},{1,0},{2,3},{3,2},{4,5},{5,4},{6,7},{7,6},{8,9},{9,8},{10,11... | collective-permute-start | bytes 393224 | tf_op jit(solution)/shard_map/ppermute | solution.py:280
  8.4 1.3 %collective-permute-done.refs_5_ = f32[256,128]{1,0:T(8,128)S(1)} collective-permute-done((f32[256,128]{1,0:T(8,128)S(1)}, f32[256,128]{1,0:T(8,128)S(1)}, u32[]{:S(2)}, u32[]{:S(2)}) %collective-permute-start) | collective-permute-done | bytes 131104 | tf_op jit(solution)/shard_map/ppermute | solution.py:280
  9.7 2.3 %collective-permute-start.2 = (f32[40,256]{1,0:T(8,128)S(1)}, f32[40,256]{1,0:T(8,128)S(1)}, u32[]{:S(2)}, u32[]{:S(2)}) collective-permute-start(f32[40,256]{1,0:T(8,128)S(1)} %get-tuple-element.12), channel_id=1, source_target_pairs={{2,0},{4,2},{6,4},{8,6},{10,8},{12,10},{14,12},{3,1},{5,3},{7,5},{... | collective-permute-start | bytes 122888 | tf_op jit(solution)/shard_map/ppermute | solution.py:284
  12.1 3.5 %collective-permute-start.1 = (f32[40,256]{1,0:T(8,128)S(1)}, f32[40,256]{1,0:T(8,128)S(1)}, u32[]{:S(2)}, u32[]{:S(2)}) collective-permute-start(f32[40,256]{1,0:T(8,128)S(1)} %get-tuple-element.13), channel_id=1, source_target_pairs={{0,2},{2,4},{4,6},{6,8},{8,10},{10,12},{12,14},{1,3},{3,5},{5,7},{... | collective-permute-start | bytes 122888 | tf_op jit(solution)/shard_map/ppermute | solution.py:285
  15.6 0.0 collective-permute-done.2.refs_7_
  15.6 3.6 %collective-permute-done.1.refs_6_ = f32[40,256]{1,0:T(8,128)S(1)} collective-permute-done((f32[40,256]{1,0:T(8,128)S(1)}, f32[40,256]{1,0:T(8,128)S(1)}, u32[]{:S(2)}, u32[]{:S(2)}) %collective-permute-start.1) | collective-permute-done | bytes 40992 | tf_op jit(solution)/shard_map/ppermute | solution.py:285
  19.2 0.0 copy-start.5
  19.2 0.0 copy-start.6
  19.2 0.7 %copy-done.5 = s32[1,1,1,16]{3,2,1,0:T(1,128)S(1)} copy-done((s32[1,1,1,16]{3,2,1,0:T(1,128)S(1)}, s32[1,1,1,16]{3,2,1,0:T(1,128)}, u32[]{:S(2)}) %copy-start.5) | copy-done | bytes 88
  19.9 0.0 copy-done.6
  19.9 4.2 %steps.1 = (f32[32,16,128]{2,1,0:T(8,128)S(1)}, f32[1,256,256]{2,1,0:T(8,128)}) custom-call(f32[3,1,256,256]{3,2,1,0:T(8,128)S(1)} %copy-done, f32[3,1,256,256]{3,2,1,0:T(8,128)S(1)} %copy-done.1, f32[256,256]{1,0:T(8,128)S(1)} %copy-done.2, f32[256,256]{1,0:T(8,128)S(1)} %copy-done.3, f32[256,256]{1,0:T(8,128)S(1)} %copy-done.4, ...), custom_call_target="tpu_custom_call" | custom-call | flops 14000000 | bytes 2900000 | tf_op jit(solution)/shard_map/steps/pallas_call | solution.py:242
  24.1 24.2 %all_to_all.5 = f32[32,16,128]{2,1,0:T(8,128)S(1)} all-to-all(f32[32,16,128]{2,1,0:T(8,128)S(1)} %get-tuple-element.10), channel_id=1, replica_groups=mesh['emit'=32,'vx'=8,'vy'=2] {'emit'}, dimensions={0} | all-to-all | bytes 524288 | tf_op jit(solution)/shard_map/all_to_all | solution.py:289
  48.3 0.6 %reduce_sum.11 = f32[16,128]{1,0:T(8,128)} reduce(f32[32,16,128]{2,1,0:T(8,128)S(1)} %all_to_all.5, f32[]{:T(128)} %constant.2.clone.1), dimensions={0}, to_apply=%region_0.0 | reduce | flops 63488 | bytes 270340 | tf_op jit(solution)/shard_map/reduce_sum | solution.py:290
  (1 shorter events, 0.0 us)
Async XLA Ops:
  0.6 1.1 %copy-start = (f32[3,1,256,256]{3,2,1,0:T(8,128)S(1)}, f32[3,1,256,256]{3,2,1,0:T(8,128)}, u32[]{:S(2)}) copy-start(f32[3,1,256,256]{3,2,1,0:T(8,128)} %refs_0_.1) | copy-start | bytes 2359300
  1.8 1.1 %copy-start.1 = (f32[3,1,256,256]{3,2,1,0:T(8,128)S(1)}, f32[3,1,256,256]{3,2,1,0:T(8,128)}, u32[]{:S(2)}) copy-start(f32[3,1,256,256]{3,2,1,0:T(8,128)} %refs_1_.1) | copy-start | bytes 2359300
  2.9 0.9 %copy-start.2 = (f32[256,256]{1,0:T(8,128)S(1)}, f32[256,256]{1,0:T(8,128)}, u32[]{:S(2)}) copy-start(f32[256,256]{1,0:T(8,128)} %refs_2_.1) | copy-start | bytes 786436
  3.8 0.9 %copy-start.3 = (f32[256,256]{1,0:T(8,128)S(1)}, f32[256,256]{1,0:T(8,128)}, u32[]{:S(2)}) copy-start(f32[256,256]{1,0:T(8,128)} %refs_3_.1) | copy-start | bytes 786436
  4.8 0.9 %copy-start.4 = (f32[256,256]{1,0:T(8,128)S(1)}, f32[256,256]{1,0:T(8,128)}, u32[]{:S(2)}) copy-start(f32[256,256]{1,0:T(8,128)} %refs_4_.1) | copy-start | bytes 786436
  6.5 3.2 %collective-permute-start = (f32[256,128]{1,0:T(8,128)S(1)}, f32[256,128]{1,0:T(8,128)S(1)}, u32[]{:S(2)}, u32[]{:S(2)}) collective-permute-start(f32[256,128]{1,0:T(8,128)S(1)} %get-tuple-element.7), channel_id=1, source_target_pairs={{0,1},{1,0},{2,3},{3,2},{4,5},{5,4},{6,7},{7,6},{8,9},{9,8},{10,11... | collective-permute-start | bytes 393224 | tf_op jit(solution)/shard_map/ppermute | solution.py:280
  9.7 5.9 %collective-permute-start.2 = (f32[40,256]{1,0:T(8,128)S(1)}, f32[40,256]{1,0:T(8,128)S(1)}, u32[]{:S(2)}, u32[]{:S(2)}) collective-permute-start(f32[40,256]{1,0:T(8,128)S(1)} %get-tuple-element.12), channel_id=1, source_target_pairs={{2,0},{4,2},{6,4},{8,6},{10,8},{12,10},{14,12},{3,1},{5,3},{7,5},{... | collective-permute-start | bytes 122888 | tf_op jit(solution)/shard_map/ppermute | solution.py:284
  12.1 7.1 %collective-permute-start.1 = (f32[40,256]{1,0:T(8,128)S(1)}, f32[40,256]{1,0:T(8,128)S(1)}, u32[]{:S(2)}, u32[]{:S(2)}) collective-permute-start(f32[40,256]{1,0:T(8,128)S(1)} %get-tuple-element.13), channel_id=1, source_target_pairs={{0,2},{2,4},{4,6},{6,8},{8,10},{10,12},{12,14},{1,3},{3,5},{5,7},{... | collective-permute-start | bytes 122888 | tf_op jit(solution)/shard_map/ppermute | solution.py:285
  19.2 0.7 %copy-start.5 = (s32[1,1,1,16]{3,2,1,0:T(1,128)S(1)}, s32[1,1,1,16]{3,2,1,0:T(1,128)}, u32[]{:S(2)}) copy-start(s32[1,1,1,16]{3,2,1,0:T(1,128)} %param.12) | copy-start | bytes 196
  19.2 0.7 %copy-start.6 = (s32[1,1,32]{2,1,0:T(1,128)S(1)}, s32[1,1,32]{2,1,0:T(1,128)}, u32[]{:S(2)}) copy-start(s32[1,1,32]{2,1,0:T(1,128)} %param.13) | copy-start | bytes 388

commit v3 on v2

--- a/solution.py
+++ b/solution.py
@@ -15,6 +15,10 @@
 TILE_AT = 2 * SUB
 VMEM_LIMIT = 48 * 1024 * 1024
 GROUP = (13, 37, 35, 33)
+
+
+def in_hbm(array):
+    return pltpu.with_memory_space_constraint(array, pltpu.HBM)
 
 
 def pack_kernel(fwd, adj, courant, decay, strength, side_out, top_out, low_out, cols, tops, lows, sem):
@@ -72,9 +76,9 @@
 
 
 def steps_kernel(
-    scale, fwd, adj, courant, decay, strength, side, above, below, footprint, owner,
+    scale, fwd, adj, courant, decay, strength, side, above, below, footprint_in, owner_in,
     ordered, pressure, held, coefs, starts, memories, fore, back, curves, partial, found_g, found_p,
-    slot_of, gain_of, sem, out_sem,
+    footprint, owner, slot_of, gain_of, sem, list_sem, out_sem,
 ):
     rows = courant.shape[0]
     vy = lax.axis_index("vy")
@@ -88,6 +92,12 @@
     started = [pltpu.make_async_copy(src, dst, sem.at[n]) for n, (src, dst) in enumerate(copies)]
     for copy in started:
         copy.start()
+    lists = [
+        pltpu.make_async_copy(footprint_in, footprint, list_sem.at[0]),
+        pltpu.make_async_copy(owner_in, owner, list_sem.at[1]),
+    ]
+    for copy in lists:
+        copy.start()
 
     lane = lax.broadcasted_iota(jnp.int32, (SUB, LANES), 1)
     sub = lax.broadcasted_iota(jnp.int32, (SUB, LANES), 0)
@@ -98,13 +108,6 @@
     def spread(strip, field):
         shift = lax.rem(LANES - HALO * field + (LANES - HALO) * vy, LANES)
         return jnp.where(beside, pltpu.roll(strip, shift, 1), zero)
-
-    for block in range(gain_of.shape[0]):
-        gain_of[block] = jnp.float32(0.0)
-    for number in range(footprint.shape[0]):
-        gain_of[footprint[number]] = jnp.float32(scale)
-    for number in range(owner.shape[0]):
-        slot_of[owner[number]] = number
 
     corner_above = above[HALO * (FIELDS - 1) : HALO * (FIELDS + 1), 0:LANES]
     corner_below = pltpu.roll(below[HALO * (FIELDS - 1) : HALO * (FIELDS + 1), 0:LANES], HALO, 0)
@@ -127,6 +130,14 @@
         strip = side[at : at + SUB, :]
         for field in range(FIELDS):
             held[field, 2, TILE_AT + at : TILE_AT + at + SUB, :] = spread(strip, field)
+    for copy in lists:
+        copy.wait()
+    for block in range(gain_of.shape[0]):
+        gain_of[block] = jnp.float32(0.0)
+    for number in range(footprint.shape[0]):
+        gain_of[footprint[number]] = jnp.float32(scale)
+    for number in range(owner.shape[0]):
+        slot_of[owner[number]] = number
     for copy in started:
         copy.wait()
 
@@ -247,7 +258,7 @@
         ),
         in_specs=[pl.BlockSpec(memory_space=pltpu.HBM)] * 5
         + [pl.BlockSpec(memory_space=pltpu.VMEM)] * 3
-        + [pl.BlockSpec(memory_space=pltpu.SMEM)] * 2,
+        + [pl.BlockSpec(memory_space=pltpu.HBM)] * 2,
         out_specs=[pl.BlockSpec(memory_space=pltpu.VMEM), pl.BlockSpec(memory_space=pltpu.HBM)],
         scratch_shapes=[
             pltpu.VMEM((FIELDS, 3, rows + 7 * SUB, LANES), jnp.float32),
@@ -260,9 +271,12 @@
             pltpu.VMEM(strip, jnp.float32),
             pltpu.VMEM(found, jnp.float32),
             pltpu.VMEM(found, jnp.float32),
+            pltpu.SMEM(footprint.shape, jnp.int32),
+            pltpu.SMEM((blocks,), jnp.int32),
             pltpu.SMEM((blocks,), jnp.int32),
             pltpu.SMEM((blocks,), jnp.float32),
             pltpu.SemaphoreType.DMA((10,)),
+            pltpu.SemaphoreType.DMA((2,)),
             pltpu.SemaphoreType.DMA((2,)),
         ],
         compiler_params=pltpu.CompilerParams(vmem_limit_bytes=VMEM_LIMIT),
@@ -275,7 +289,7 @@
     groups = lax.axis_size("emit")
     tiles = lax.axis_size("vx")
     rows = courant.shape[0]
-    fields = (fwd_state, adj_state, courant, decay_rate, strength)
+    fields = [in_hbm(field) for field in (fwd_state, adj_state, courant, decay_rate, strength)]
     side, top, low = pack(*fields)
     side = lax.ppermute(side, "vy", [(0, 1), (1, 0)])
     corners = (HALO * FIELDS, 0)
@@ -284,7 +298,7 @@
     below = lax.ppermute(top, "vx", [(i + 1, i) for i in range(tiles - 1)])
     above = lax.ppermute(low, "vx", [(i, i + 1) for i in range(tiles - 1)])
     ordered, pressure = run_steps(
-        1.0 / groups, *fields, side, above, below, footprint.reshape(-1), owner_map.reshape(-1)
+        1.0 / groups, *fields, side, above, below, in_hbm(footprint.reshape(-1)), in_hbm(owner_map.reshape(-1))
     )
     sent = lax.all_to_all(ordered, "emit", 0, 0, tiled=True)
     gradient = jnp.sum(sent.reshape(groups, -1, BR, BC), axis=0)

time: 49.3 us -> 45 us (0.913)
  local copies, waits for them, and re-layouts: 5.79 us -> 0.01 us
  Pallas kernels: 4.92 us -> 6.52 us
    unnamed x14 -> x0, local copies, waits for them, and re-layouts: 5.78 us -> none
    pallas_call x1, Pallas kernels: 0.72 us -> 1.84 us  [pack(): pl.pallas_call(pack_kernel, out_shape=(jax.ShapeDtypeStruct((rows, LANES)...]
where the time goes in v3:
time: 45 us; the launch traced here: 44.7 us
  blocking collectives  24.2 us (54%)
  starting transfers between devices  7.75 us (17%)
  Pallas kernels  6.52 us (14%)
  waiting for transfers between devices  4.93 us (11%)
  between operations  0.67 us (1%)
  other arithmetic  0.63 us (1%)
    all_to_all x1, blocking collectives, shards(): sent = lax.all_to_all(ordered, 'emit', 0, 0, tiled=True)  24.2 us
    pallas_call x1, Pallas kernels, run_steps(): pl.pallas_call(lambda *refs: steps_kernel(scale, *refs), out_shape=(jax.S...  4.69 us
    ppermute x1, waiting for transfers between devices, shards(): above = lax.ppermute(low, 'vx', [(i, i + 1) for i in range(tiles - 1)])  3.58 us
    ppermute x1, starting transfers between devices, shards(): above = lax.ppermute(low, 'vx', [(i, i + 1) for i in range(tiles - 1)])  3.48 us
    ppermute x1, starting transfers between devices, shards(): below = lax.ppermute(top, 'vx', [(i + 1, i) for i in range(tiles - 1)])  2.35 us
    ppermute x1, starting transfers between devices, shards(): side = lax.ppermute(side, 'vy', [(0, 1), (1, 0)])  1.92 us
    pallas_call x1, Pallas kernels, pack(): pl.pallas_call(pack_kernel, out_shape=(jax.ShapeDtypeStruct((rows, LANES)...  1.84 us
    ppermute x1, waiting for transfers between devices, shards(): side = lax.ppermute(side, 'vy', [(0, 1), (1, 0)])  1.31 us
  transfers between devices with their start and end apart: 3, of which 2 were waited for; matrix products, arithmetic and copies ran while one was open for 0% of the time, Pallas kernels for 0%

profile of v3, /device:TPU:32, one launch (start us, length us, event | category | flops | bytes accessed | tf_op | source)
XLA Modules:
  0.0 44.7 jit_solution(15640491255651007062)
XLA Ops:
  0.6 1.8 %pack.1 = (f32[256,128]{1,0:T(8,128)S(1)}, f32[40,256]{1,0:T(8,128)S(1)}, f32[40,256]{1,0:T(8,128)S(1)}) custom-call(f32[3,1,256,256]{3,2,1,0:T(8,128)} %refs_0_.1, f32[3,1,256,256]{3,2,1,0:T(8,128)} %refs_1_.1, f32[256,256]{1,0:T(8,128)} %refs_2_.1, f32[256,256]{1,0:T(8,128)} %refs_3_.1, f32[256,256]{1,0:T(8,128)} %refs_4_.1), custom_call_target="tpu_custom_call" | custom-call | flops 600000 | bytes 1500000 | tf_op jit(solution)/shard_map/pack/pallas_call | solution.py:61
  2.5 1.9 %collective-permute-start = (f32[256,128]{1,0:T(8,128)S(1)}, f32[256,128]{1,0:T(8,128)S(1)}, u32[]{:S(2)}, u32[]{:S(2)}) collective-permute-start(f32[256,128]{1,0:T(8,128)S(1)} %get-tuple-element.7), channel_id=1, source_target_pairs={{0,1},{1,0},{2,3},{3,2},{4,5},{5,4},{6,7},{7,6},{8,9},{9,8},{10,11... | collective-permute-start | bytes 393224 | tf_op jit(solution)/shard_map/ppermute | solution.py:294
  4.4 1.3 %collective-permute-done.refs_5_ = f32[256,128]{1,0:T(8,128)S(1)} collective-permute-done((f32[256,128]{1,0:T(8,128)S(1)}, f32[256,128]{1,0:T(8,128)S(1)}, u32[]{:S(2)}, u32[]{:S(2)}) %collective-permute-start) | collective-permute-done | bytes 131104 | tf_op jit(solution)/shard_map/ppermute | solution.py:294
  5.7 2.3 %collective-permute-start.2 = (f32[40,256]{1,0:T(8,128)S(1)}, f32[40,256]{1,0:T(8,128)S(1)}, u32[]{:S(2)}, u32[]{:S(2)}) collective-permute-start(f32[40,256]{1,0:T(8,128)S(1)} %get-tuple-element.12), channel_id=1, source_target_pairs={{2,0},{4,2},{6,4},{8,6},{10,8},{12,10},{14,12},{3,1},{5,3},{7,5},{... | collective-permute-start | bytes 122888 | tf_op jit(solution)/shard_map/ppermute | solution.py:298
  8.1 3.5 %collective-permute-start.1 = (f32[40,256]{1,0:T(8,128)S(1)}, f32[40,256]{1,0:T(8,128)S(1)}, u32[]{:S(2)}, u32[]{:S(2)}) collective-permute-start(f32[40,256]{1,0:T(8,128)S(1)} %get-tuple-element.13), channel_id=1, source_target_pairs={{0,2},{2,4},{4,6},{6,8},{8,10},{10,12},{12,14},{1,3},{3,5},{5,7},{... | collective-permute-start | bytes 122888 | tf_op jit(solution)/shard_map/ppermute | solution.py:299
  11.6 0.0 collective-permute-done.2.refs_7_
  11.6 3.6 %collective-permute-done.1.refs_6_ = f32[40,256]{1,0:T(8,128)S(1)} collective-permute-done((f32[40,256]{1,0:T(8,128)S(1)}, f32[40,256]{1,0:T(8,128)S(1)}, u32[]{:S(2)}, u32[]{:S(2)}) %collective-permute-start.1) | collective-permute-done | bytes 40992 | tf_op jit(solution)/shard_map/ppermute | solution.py:299
  15.2 4.7 %steps.1 = (f32[32,16,128]{2,1,0:T(8,128)S(1)}, f32[1,256,256]{2,1,0:T(8,128)}) custom-call(f32[3,1,256,256]{3,2,1,0:T(8,128)} %refs_0_.1, f32[3,1,256,256]{3,2,1,0:T(8,128)} %refs_1_.1, f32[256,256]{1,0:T(8,128)} %refs_2_.1, f32[256,256]{1,0:T(8,128)} %refs_3_.1, f32[256,256]{1,0:T(8,128)} %refs_4_.1, f32[256,128]{1,0:T(8,128)S(1)} %collective-permute-done.refs_5_, ...), custom_call_target="tpu_custom_call" | custom-call | flops 14000000 | bytes 2900000 | tf_op jit(solution)/shard_map/steps/pallas_call | solution.py:253
  19.9 24.2 %all_to_all.5 = f32[32,16,128]{2,1,0:T(8,128)S(1)} all-to-all(f32[32,16,128]{2,1,0:T(8,128)S(1)} %get-tuple-element.10), channel_id=1, replica_groups=mesh['emit'=32,'vx'=8,'vy'=2] {'emit'}, dimensions={0} | all-to-all | bytes 524288 | tf_op jit(solution)/shard_map/all_to_all | solution.py:303
  44.1 0.6 %reduce_sum.11 = f32[16,128]{1,0:T(8,128)} reduce(f32[32,16,128]{2,1,0:T(8,128)S(1)} %all_to_all.5, f32[]{:T(128)} %constant.2.clone.1), dimensions={0}, to_apply=%region_0.0 | reduce | flops 63488 | bytes 270340 | tf_op jit(solution)/shard_map/reduce_sum | solution.py:304
  (1 shorter events, 0.0 us)
Async XLA Ops:
  2.5 3.2 %collective-permute-start = (f32[256,128]{1,0:T(8,128)S(1)}, f32[256,128]{1,0:T(8,128)S(1)}, u32[]{:S(2)}, u32[]{:S(2)}) collective-permute-start(f32[256,128]{1,0:T(8,128)S(1)} %get-tuple-element.7), channel_id=1, source_target_pairs={{0,1},{1,0},{2,3},{3,2},{4,5},{5,4},{6,7},{7,6},{8,9},{9,8},{10,11... | collective-permute-start | bytes 393224 | tf_op jit(solution)/shard_map/ppermute | solution.py:294
  5.7 5.9 %collective-permute-start.2 = (f32[40,256]{1,0:T(8,128)S(1)}, f32[40,256]{1,0:T(8,128)S(1)}, u32[]{:S(2)}, u32[]{:S(2)}) collective-permute-start(f32[40,256]{1,0:T(8,128)S(1)} %get-tuple-element.12), channel_id=1, source_target_pairs={{2,0},{4,2},{6,4},{8,6},{10,8},{12,10},{14,12},{3,1},{5,3},{7,5},{... | collective-permute-start | bytes 122888 | tf_op jit(solution)/shard_map/ppermute | solution.py:298
  8.1 7.1 %collective-permute-start.1 = (f32[40,256]{1,0:T(8,128)S(1)}, f32[40,256]{1,0:T(8,128)S(1)}, u32[]{:S(2)}, u32[]{:S(2)}) collective-permute-start(f32[40,256]{1,0:T(8,128)S(1)} %get-tuple-element.13), channel_id=1, source_target_pairs={{0,2},{2,4},{4,6},{6,8},{8,10},{10,12},{12,14},{1,3},{3,5},{5,7},{... | collective-permute-start | bytes 122888 | tf_op jit(solution)/shard_map/ppermute | solution.py:299

commit v4 on v2

--- a/solution.py
+++ b/solution.py
@@ -13,8 +13,11 @@
 LANES = 128
 FIELDS = 9
 TILE_AT = 2 * SUB
-VMEM_LIMIT = 48 * 1024 * 1024
-GROUP = (13, 37, 35, 33)
+VMEM_LIMIT = 40 * 1024 * 1024
+
+
+def in_hbm(array):
+    return pltpu.with_memory_space_constraint(array, pltpu.HBM)
 
 
 def pack_kernel(fwd, adj, courant, decay, strength, side_out, top_out, low_out, cols, tops, lows, sem):
@@ -71,64 +74,46 @@
     )(fwd_state, adj_state, courant, decay_rate, strength)
 
 
-def steps_kernel(
-    scale, fwd, adj, courant, decay, strength, side, above, below, footprint, owner,
-    ordered, pressure, held, coefs, starts, memories, fore, back, curves, partial, found_g, found_p,
-    slot_of, gain_of, sem, out_sem,
+def half_kernel(
+    lower_half, fwd, adj, courant, decay, strength, side,
+    found_g, found_p, rim, held, coefs, starts, memories, fore, back, curves, partial, sem,
 ):
-    rows = courant.shape[0]
+    whole = courant.shape[0]
+    rows = whole // 2
+    first_row = rows - SUB if lower_half else 0
+    first_at = TILE_AT - SUB if lower_half else TILE_AT
+    amount = rows + SUB
     vy = lax.axis_index("vy")
     copies = []
     for half in range(2):
         columns = pl.ds(half * LANES, LANES)
+        source, target = pl.ds(first_row, amount), pl.ds(first_at, amount)
         for number, state in enumerate((fwd, adj)):
-            copies.append((state.at[:, 0, :, columns], held.at[pl.ds(3 * number, 3), half, pl.ds(TILE_AT, rows), :]))
+            copies.append((state.at[:, 0, source, columns], held.at[pl.ds(3 * number, 3), half, target, :]))
         for number, field in enumerate((courant, decay, strength)):
-            copies.append((field.at[:, columns], held.at[6 + number, half, pl.ds(TILE_AT, rows), :]))
+            copies.append((field.at[source, columns], held.at[6 + number, half, target, :]))
     started = [pltpu.make_async_copy(src, dst, sem.at[n]) for n, (src, dst) in enumerate(copies)]
     for copy in started:
         copy.start()
 
     lane = lax.broadcasted_iota(jnp.int32, (SUB, LANES), 1)
-    sub = lax.broadcasted_iota(jnp.int32, (SUB, LANES), 0)
     beside = (lane >= (LANES - HALO) * vy) & (lane < (LANES - HALO) * vy + HALO)
     zero = jnp.zeros((SUB, LANES), jnp.float32)
     lane_first, lane_last = lane == 0, lane == LANES - 1
-
-    def spread(strip, field):
+    empty = rows + TILE_AT if lower_half else SUB
+    for field in range(FIELDS):
         shift = lax.rem(LANES - HALO * field + (LANES - HALO) * vy, LANES)
-        return jnp.where(beside, pltpu.roll(strip, shift, 1), zero)
-
-    for block in range(gain_of.shape[0]):
-        gain_of[block] = jnp.float32(0.0)
-    for number in range(footprint.shape[0]):
-        gain_of[footprint[number]] = jnp.float32(scale)
-    for number in range(owner.shape[0]):
-        slot_of[owner[number]] = number
-
-    corner_above = above[HALO * (FIELDS - 1) : HALO * (FIELDS + 1), 0:LANES]
-    corner_below = pltpu.roll(below[HALO * (FIELDS - 1) : HALO * (FIELDS + 1), 0:LANES], HALO, 0)
-    upper, lower = sub >= HALO, sub < HALO
-    for field in range(FIELDS):
-        at = (field // 2) * SUB
-        for half in range(2):
-            columns = slice(half * LANES, (half + 1) * LANES)
-            value = above[at : at + SUB, columns]
-            if field % 2 == 0:
-                value = pltpu.roll(value, HALO, 0)
-            held[field, half, SUB : 2 * SUB, :] = jnp.where(upper, value, zero)
-            value = below[at : at + SUB, columns]
-            if field % 2 == 1:
-                value = pltpu.roll(value, HALO, 0)
-            held[field, half, rows + 2 * SUB : rows + 3 * SUB, :] = jnp.where(lower, value, zero)
-        held[field, 2, SUB : 2 * SUB, :] = jnp.where(upper, spread(corner_above, field), zero)
-        held[field, 2, rows + 2 * SUB : rows + 3 * SUB, :] = jnp.where(lower, spread(corner_below, field), zero)
-    for at in range(0, rows, SUB):
-        strip = side[at : at + SUB, :]
-        for field in range(FIELDS):
-            held[field, 2, TILE_AT + at : TILE_AT + at + SUB, :] = spread(strip, field)
+        for at in range(0, amount, SUB):
+            strip = pltpu.roll(side[first_row + at : first_row + at + SUB, :], shift, 1)
+            held[field, 2, first_at + at : first_at + at + SUB, :] = jnp.where(beside, strip, zero)
+        for part in range(3):
+            held[field, part, empty : empty + SUB, :] = zero
     for copy in started:
         copy.wait()
+    rim_at = rows if lower_half else TILE_AT
+    for field in range(FIELDS):
+        for part in range(3):
+            rim[field, part] = held[field, part, rim_at : rim_at + 2 * SUB, :]
 
     pitch = rows // SUB + 1
 
@@ -208,49 +193,20 @@
     for step in range(1, STEPS + 1):
         margin = STEPS - step
         count = pitch + 2 * margin
-        group = GROUP[step - 1]
-        if count == group:
-            advance(step, -margin, group)
-        else:
-
-            def turn(number, carry, step=step, margin=margin, group=group):
-                advance(step, number * group - margin, group)
-                return carry
-
-            lax.fori_loop(0, count // group, turn, 0)
-
-    leaving = [
-        pltpu.make_async_copy(
-            found_p.at[half, pl.ds(SUB, rows), :], pressure.at[0, :, pl.ds(half * LANES, LANES)], out_sem.at[half]
-        )
-        for half in range(2)
-    ]
-    for copy in leaving:
-        copy.start()
-    for block in range(gain_of.shape[0]):
-        at = SUB + (block // 2) * BR
-        ordered[slot_of[block]] = found_g[block % 2, at : at + BR, :] * gain_of[block]
-    for copy in leaving:
-        copy.wait()
-
-
-def run_steps(scale, fwd_state, adj_state, courant, decay_rate, strength, side, above, below, footprint, owner_map):
-    rows, columns = courant.shape
-    blocks = owner_map.shape[0]
+        advance(step, -margin, count)
+
+
+def run_half(lower_half, fwd_state, adj_state, courant, decay_rate, strength, side):
+    rows = courant.shape[0] // 2
     strip = (3, rows // SUB + 16, SUB, LANES)
-    found = (2, rows + 6 * SUB, LANES)
+    found = jax.ShapeDtypeStruct((2, rows + 4 * SUB, LANES), jnp.float32)
     return pl.pallas_call(
-        lambda *refs: steps_kernel(scale, *refs),
-        out_shape=(
-            jax.ShapeDtypeStruct((blocks, BR, BC), jnp.float32),
-            jax.ShapeDtypeStruct((1, rows, columns), jnp.float32),
-        ),
-        in_specs=[pl.BlockSpec(memory_space=pltpu.HBM)] * 5
-        + [pl.BlockSpec(memory_space=pltpu.VMEM)] * 3
-        + [pl.BlockSpec(memory_space=pltpu.SMEM)] * 2,
-        out_specs=[pl.BlockSpec(memory_space=pltpu.VMEM), pl.BlockSpec(memory_space=pltpu.HBM)],
+        lambda *refs: half_kernel(lower_half, *refs),
+        out_shape=(found, found, jax.ShapeDtypeStruct((FIELDS, 3, 2 * SUB, LANES), jnp.float32)),
+        in_specs=[pl.BlockSpec(memory_space=pltpu.HBM)] * 5 + [pl.BlockSpec(memory_space=pltpu.VMEM)],
+        out_specs=[pl.BlockSpec(memory_space=pltpu.VMEM)] * 3,
         scratch_shapes=[
-            pltpu.VMEM((FIELDS, 3, rows + 7 * SUB, LANES), jnp.float32),
+            pltpu.VMEM((FIELDS, 3, rows + 5 * SUB, LANES), jnp.float32),
             pltpu.VMEM((3,) + strip, jnp.float32),
             pltpu.VMEM((2,) + strip, jnp.float32),
             pltpu.VMEM((2,) + strip, jnp.float32),
@@ -258,33 +214,183 @@
             pltpu.VMEM((STEPS - 1,) + strip, jnp.float32),
             pltpu.VMEM((2,) + strip, jnp.float32),
             pltpu.VMEM(strip, jnp.float32),
-            pltpu.VMEM(found, jnp.float32),
-            pltpu.VMEM(found, jnp.float32),
+            pltpu.SemaphoreType.DMA((10,)),
+        ],
+        compiler_params=pltpu.CompilerParams(vmem_limit_bytes=VMEM_LIMIT),
+        cost_estimate=pl.CostEstimate(flops=8000000, bytes_accessed=1800000, transcendentals=0),
+        name="lower_half" if lower_half else "upper_half",
+    )(fwd_state, adj_state, courant, decay_rate, strength, side)
+
+
+def rim_kernel(
+    scale, upper_g, upper_p, upper_rim, lower_g, lower_p, lower_rim, above, below, footprint_in, owner_in,
+    ordered, pressure, edges, footprint, owner, slot_of, gain_of, list_sem, out_sem,
+):
+    rows = pressure.shape[1]
+    half_rows = rows // 2
+    vy = lax.axis_index("vy")
+    lists = [
+        pltpu.make_async_copy(footprint_in, footprint, list_sem.at[0]),
+        pltpu.make_async_copy(owner_in, owner, list_sem.at[1]),
+    ]
+    for copy in lists:
+        copy.start()
+    inner = half_rows - SUB
+    leaving = []
+    for half in range(2):
+        columns = pl.ds(half * LANES, LANES)
+        leaving.append((upper_p.at[half, pl.ds(2 * SUB, inner), :], pressure.at[0, pl.ds(SUB, inner), columns]))
+        leaving.append((lower_p.at[half, pl.ds(SUB, inner), :], pressure.at[0, pl.ds(half_rows, inner), columns]))
+    leaving = [pltpu.make_async_copy(src, dst, out_sem.at[n]) for n, (src, dst) in enumerate(leaving)]
+    for copy in leaving:
+        copy.start()
+
+    lane = lax.broadcasted_iota(jnp.int32, (SUB, LANES), 1)
+    sub = lax.broadcasted_iota(jnp.int32, (SUB, LANES), 0)
+    beside = (lane >= (LANES - HALO) * vy) & (lane < (LANES - HALO) * vy + HALO)
+    zero = jnp.zeros((SUB, LANES), jnp.float32)
+    lane_first, lane_last = lane == 0, lane == LANES - 1
+    first, last = sub == 0, sub == SUB - 1
+
+    def halo_of(field, part, low):
+        source = below if low else above
+        last_pair = HALO * (FIELDS - 1)
+        at = last_pair if part == 2 else (field // 2) * SUB
+        value = source[at : at + SUB, (part % 2) * LANES : (part % 2 + 1) * LANES]
+        in_lower_rows = part == 2 or field % 2 == 1
+        if in_lower_rows == low:
+            value = pltpu.roll(value, HALO, 0)
+        value = jnp.where((sub < HALO) if low else (sub >= HALO), value, zero)
+        if part == 2:
+            shift = lax.rem(LANES - HALO * field + (LANES - HALO) * vy, LANES)
+            value = jnp.where(beside, pltpu.roll(value, shift, 1), zero)
+        return value
+
+    def window(field, low):
+        result = []
+        for chunk in range(3):
+            if low:
+                row = [halo_of(field, p, True) if chunk == 2 else lower_rim[field, p, chunk * SUB : (chunk + 1) * SUB, :] for p in range(3)]
+            else:
+                row = [halo_of(field, p, False) if chunk == 0 else upper_rim[field, p, (chunk - 1) * SUB : chunk * SUB, :] for p in range(3)]
+            result.append(row)
+        return result
+
+    for low in (False, True):
+        speed, keep, loss = (window(field, low) for field in (6, 7, 8))
+        states = [[window(3 * state + field, low) for field in range(3)] for state in range(2)]
+        levels = ([], [])
+        curves = []
+        for step in range(1, STEPS + 1):
+            chunks = (1,) if step == STEPS else (0, 1, 2)
+            for state in range(2):
+                old, new, memory = states[state]
+                up = [[pltpu.roll(value, 1, 0) for value in row] for row in new]
+                down = [[pltpu.roll(value, SUB - 1, 0) for value in row] for row in new]
+                memories = [list(row) for row in memory]
+                nexts = [list(row) for row in new]
+                for chunk in chunks:
+                    right = [pltpu.roll(value, LANES - 1, 1) for value in new[chunk]]
+                    left = [pltpu.roll(value, 1, 1) for value in new[chunk]]
+                    for part in range(2) if step == STEPS else range(3):
+                        now = new[chunk][part]
+                        north = jnp.where(first, up[chunk - 1][part] if chunk > 0 else zero, up[chunk][part])
+                        south = jnp.where(last, down[chunk + 1][part] if chunk < 2 else zero, down[chunk][part])
+                        west = jnp.where(lane_first, left[(part + 2) % 3], left[part])
+                        east = jnp.where(lane_last, right[(part + 1) % 3], right[part])
+                        curve = (north + south) + (east + west) - 4.0 * now
+                        held = keep[chunk][part] * memory[chunk][part] + loss[chunk][part] * curve
+                        second = speed[chunk][part] * (curve - held)
+                        memories[chunk][part] = held
+                        nexts[chunk][part] = 2.0 * now - old[chunk][part] + second
+                        if state == 0 and chunk == 1 and part < 2:
+                            curves.append(second)
+                levels[state].append(nexts[1])
+                states[state] = [new, nexts, memories]
+        at = slice(SUB, 2 * SUB) if low else slice(0, SUB)
+        for part in range(2):
+            adjoint = [level[part] for level in levels[1]]
+            seconds = curves[part::2]
+            value = seconds[2] * adjoint[1] + seconds[1] * adjoint[2]
+            value = value + (seconds[3] * adjoint[0] + seconds[0] * adjoint[3])
+            edges[0, at, part * LANES : (part + 1) * LANES] = levels[0][STEPS - 1][part]
+            edges[1, at, part * LANES : (part + 1) * LANES] = value
+    outer = [
+        pltpu.make_async_copy(edges.at[0, pl.ds(0, SUB), :], pressure.at[0, pl.ds(0, SUB), :], out_sem.at[4]),
+        pltpu.make_async_copy(edges.at[0, pl.ds(SUB, SUB), :], pressure.at[0, pl.ds(rows - SUB, SUB), :], out_sem.at[5]),
+    ]
+    for copy in outer:
+        copy.start()
+
+    for copy in lists:
+        copy.wait()
+    blocks = gain_of.shape[0]
+    for block in range(blocks):
+        gain_of[block] = jnp.float32(0.0)
+    for number in range(footprint.shape[0]):
+        gain_of[footprint[number]] = jnp.float32(scale)
+    for number in range(owner.shape[0]):
+        slot_of[owner[number]] = number
+    for block in range(blocks):
+        source = upper_g if block < blocks // 2 else lower_g
+        part = block % 2
+        at = SUB + (block % (blocks // 2)) // 2 * BR
+        slot, gain = slot_of[block], gain_of[block]
+        high, low = source[part, at : at + SUB, :], source[part, at + SUB : at + BR, :]
+        if block < 2:
+            high = edges[1, 0:SUB, part * LANES : (part + 1) * LANES]
+        if block >= blocks - 2:
+            low = edges[1, SUB : 2 * SUB, part * LANES : (part + 1) * LANES]
+        ordered[slot, 0:SUB, :] = high * gain
+        ordered[slot, SUB:BR, :] = low * gain
+    for copy in leaving + outer:
+        copy.wait()
+
+
+def run_rim(scale, upper, lower, above, below, footprint, owner_map):
+    columns = above.shape[1]
+    rows = 2 * (upper[0].shape[1] - 4 * SUB)
+    blocks = owner_map.shape[0]
+    return pl.pallas_call(
+        lambda *refs: rim_kernel(scale, *refs),
+        out_shape=(
+            jax.ShapeDtypeStruct((blocks, BR, BC), jnp.float32),
+            jax.ShapeDtypeStruct((1, rows, columns), jnp.float32),
+        ),
+        in_specs=[pl.BlockSpec(memory_space=pltpu.VMEM)] * 8 + [pl.BlockSpec(memory_space=pltpu.HBM)] * 2,
+        out_specs=[pl.BlockSpec(memory_space=pltpu.VMEM), pl.BlockSpec(memory_space=pltpu.HBM)],
+        scratch_shapes=[
+            pltpu.VMEM((2, 2 * SUB, columns), jnp.float32),
+            pltpu.SMEM(footprint.shape, jnp.int32),
+            pltpu.SMEM((blocks,), jnp.int32),
             pltpu.SMEM((blocks,), jnp.int32),
             pltpu.SMEM((blocks,), jnp.float32),
-            pltpu.SemaphoreType.DMA((10,)),
             pltpu.SemaphoreType.DMA((2,)),
+            pltpu.SemaphoreType.DMA((6,)),
         ],
         compiler_params=pltpu.CompilerParams(vmem_limit_bytes=VMEM_LIMIT),
-        cost_estimate=pl.CostEstimate(flops=14000000, bytes_accessed=2900000, transcendentals=0),
-        name="steps",
-    )(fwd_state, adj_state, courant, decay_rate, strength, side, above, below, footprint, owner_map)
+        cost_estimate=pl.CostEstimate(flops=2000000, bytes_accessed=1500000, transcendentals=0),
+        name="rim",
+    )(*upper, *lower, above, below, footprint, owner_map)
 
 
 def shards(fwd_state, adj_state, courant, decay_rate, strength, footprint, owner_map):
     groups = lax.axis_size("emit")
     tiles = lax.axis_size("vx")
     rows = courant.shape[0]
-    fields = (fwd_state, adj_state, courant, decay_rate, strength)
+    fields = [in_hbm(field) for field in (fwd_state, adj_state, courant, decay_rate, strength)]
     side, top, low = pack(*fields)
     side = lax.ppermute(side, "vy", [(0, 1), (1, 0)])
     corners = (HALO * FIELDS, 0)
     top = lax.dynamic_update_slice(top, side[:HALO], corners)
     low = lax.dynamic_update_slice(low, side[rows - HALO :], corners)
     below = lax.ppermute(top, "vx", [(i + 1, i) for i in range(tiles - 1)])
+    upper = run_half(False, *fields, side)
+    low, upper = lax.optimization_barrier((low, upper))
     above = lax.ppermute(low, "vx", [(i, i + 1) for i in range(tiles - 1)])
-    ordered, pressure = run_steps(
-        1.0 / groups, *fields, side, above, below, footprint.reshape(-1), owner_map.reshape(-1)
+    lower = run_half(True, *fields, side)
+    ordered, pressure = run_rim(
+        1.0 / groups, upper, lower, above, below, in_hbm(footprint.reshape(-1)), in_hbm(owner_map.reshape(-1))
     )
     sent = lax.all_to_all(ordered, "emit", 0, 0, tiled=True)
     gradient = jnp.sum(sent.reshape(groups, -1, BR, BC), axis=0)

time: 49.3 us -> 46 us (0.933)
  the two profiles are of different devices: /device:TPU:32 before, /device:TPU:24 now
where the time goes in v4:
time: 46 us; the launch traced here: 45.7 us
  blocking collectives  25 us (54%)
  Pallas kernels  9.01 us (20%)
  starting transfers between devices  8.96 us (19%)
  waiting for transfers between devices  1.32 us (3%)
  between operations  0.7 us (2%)
  other arithmetic  0.63 us (1%)
    all_to_all x1, blocking collectives, shards(): sent = lax.all_to_all(ordered, 'emit', 0, 0, tiled=True)  25 us
    pallas_call x2, Pallas kernels, run_half(): pl.pallas_call(lambda *refs: half_kernel(lower_half, *refs), out_shape=(f...  6 us
    ppermute x1, starting transfers between devices, shards(): above = lax.ppermute(low, 'vx', [(i, i + 1) for i in range(tiles - 1)])  4.7 us
    ppermute x1, starting transfers between devices, shards(): below = lax.ppermute(top, 'vx', [(i + 1, i) for i in range(tiles - 1)])  2.35 us
    ppermute x1, starting transfers between devices, shards(): side = lax.ppermute(side, 'vy', [(0, 1), (1, 0)])  1.92 us
    pallas_call x1, Pallas kernels, pack(): pl.pallas_call(pack_kernel, out_shape=(jax.ShapeDtypeStruct((rows, LANES)...  1.84 us
    ppermute x1, waiting for transfers between devices, shards(): side = lax.ppermute(side, 'vy', [(0, 1), (1, 0)])  1.31 us
    pallas_call x1, Pallas kernels, run_rim(): pl.pallas_call(lambda *refs: rim_kernel(scale, *refs), out_shape=(jax.Sha...  1.17 us
  transfers between devices with their start and end apart: 3, of which 1 were waited for; matrix products, arithmetic and copies ran while one was open for 0% of the time, Pallas kernels for 13%

profile of v4, /device:TPU:24, one launch (start us, length us, event | category | flops | bytes accessed | tf_op | source)
XLA Modules:
  0.0 45.7 jit_solution(14204052041357813963)
XLA Ops:
  0.6 1.8 %pack.1 = (f32[256,128]{1,0:T(8,128)S(1)}, f32[40,256]{1,0:T(8,128)S(1)}, f32[40,256]{1,0:T(8,128)S(1)}) custom-call(f32[3,1,256,256]{3,2,1,0:T(8,128)} %refs_0_.3, f32[3,1,256,256]{3,2,1,0:T(8,128)} %refs_1_.3, f32[256,256]{1,0:T(8,128)} %refs_2_.3, f32[256,256]{1,0:T(8,128)} %refs_3_.3, f32[256,256]{1,0:T(8,128)} %refs_4_.3), custom_call_target="tpu_custom_call" | custom-call | flops 600000 | bytes 1500000 | tf_op jit(solution)/shard_map/pack/pallas_call | solution.py:60
  2.5 1.9 %collective-permute-start = (f32[256,128]{1,0:T(8,128)S(1)}, f32[256,128]{1,0:T(8,128)S(1)}, u32[]{:S(2)}, u32[]{:S(2)}) collective-permute-start(f32[256,128]{1,0:T(8,128)S(1)} %get-tuple-element.18), channel_id=1, source_target_pairs={{0,1},{1,0},{2,3},{3,2},{4,5},{5,4},{6,7},{7,6},{8,9},{9,8},{10,11... | collective-permute-start | bytes 393224 | tf_op jit(solution)/shard_map/ppermute | solution.py:383
  4.4 1.3 %collective-permute-done.refs_5_ = f32[256,128]{1,0:T(8,128)S(1)} collective-permute-done((f32[256,128]{1,0:T(8,128)S(1)}, f32[256,128]{1,0:T(8,128)S(1)}, u32[]{:S(2)}, u32[]{:S(2)}) %collective-permute-start) | collective-permute-done | bytes 131104 | tf_op jit(solution)/shard_map/ppermute | solution.py:383
  5.7 2.3 %collective-permute-start.2 = (f32[40,256]{1,0:T(8,128)S(1)}, f32[40,256]{1,0:T(8,128)S(1)}, u32[]{:S(2)}, u32[]{:S(2)}) collective-permute-start(f32[40,256]{1,0:T(8,128)S(1)} %get-tuple-element.32), channel_id=1, source_target_pairs={{2,0},{4,2},{6,4},{8,6},{10,8},{12,10},{14,12},{3,1},{5,3},{7,5},{... | collective-permute-start | bytes 122888 | tf_op jit(solution)/shard_map/ppermute | solution.py:387
  8.1 3.0 %upper_half.1 = (f32[2,160,128]{2,1,0:T(8,128)S(1)}, f32[2,160,128]{2,1,0:T(8,128)S(1)}, f32[9,3,16,128]{3,2,1,0:T(8,128)S(1)}) custom-call(f32[3,1,256,256]{3,2,1,0:T(8,128)} %refs_0_.3, f32[3,1,256,256]{3,2,1,0:T(8,128)} %refs_1_.3, f32[256,256]{1,0:T(8,128)} %refs_2_.3, f32[256,256]{1,0:T(8,128)} %refs_3_.3, f32[256,256]{1,0:T(8,128)} %refs_4_.3, ...), custom_call_target="tpu_custom_call" | custom-call | flops 8000000 | bytes 1800000 | tf_op jit(solution)/shard_map/upper_half/pallas_call | solution.py:203
  11.1 4.7 %collective-permute-start.1 = (f32[40,256]{1,0:T(8,128)S(1)}, f32[40,256]{1,0:T(8,128)S(1)}, u32[]{:S(2)}, u32[]{:S(2)}) collective-permute-start(f32[40,256]{1,0:T(8,128)S(1)} %get-tuple-element.28), channel_id=1, source_target_pairs={{0,2},{2,4},{4,6},{6,8},{8,10},{10,12},{12,14},{1,3},{3,5},{5,7},{... | collective-permute-start | bytes 122888 | tf_op jit(solution)/shard_map/ppermute | solution.py:390
  15.8 3.0 %lower_half.1 = (f32[2,160,128]{2,1,0:T(8,128)S(1)}, f32[2,160,128]{2,1,0:T(8,128)S(1)}, f32[9,3,16,128]{3,2,1,0:T(8,128)S(1)}) custom-call(f32[3,1,256,256]{3,2,1,0:T(8,128)} %refs_0_.3, f32[3,1,256,256]{3,2,1,0:T(8,128)} %refs_1_.3, f32[256,256]{1,0:T(8,128)} %refs_2_.3, f32[256,256]{1,0:T(8,128)} %refs_3_.3, f32[256,256]{1,0:T(8,128)} %refs_4_.3, ...), custom_call_target="tpu_custom_call" | custom-call | flops 8000000 | bytes 1800000 | tf_op jit(solution)/shard_map/lower_half/pallas_call | solution.py:203
  18.8 0.0 collective-permute-done.2.refs_7_
  18.8 0.0 collective-permute-done.1.refs_6_
  18.8 1.2 %rim.1 = (f32[32,16,128]{2,1,0:T(8,128)S(1)}, f32[1,256,256]{2,1,0:T(8,128)}) custom-call(f32[2,160,128]{2,1,0:T(8,128)S(1)} %get-tuple-element.22.refs_0_, f32[2,160,128]{2,1,0:T(8,128)S(1)} %get-tuple-element.23.refs_1_, f32[9,3,16,128]{3,2,1,0:T(8,128)S(1)} %get-tuple-element.24.refs_2_, f32[2,160,128]{2,1,0:T(8,128)S(1)} %get-tuple-element.25.refs_3_, ...), custom_call_target="tpu_custom_call" | custom-call | flops 2000000 | bytes 1500000 | tf_op jit(solution)/shard_map/rim/pallas_call | solution.py:354
  20.0 25.0 %all_to_all.5 = f32[32,16,128]{2,1,0:T(8,128)S(1)} all-to-all(f32[32,16,128]{2,1,0:T(8,128)S(1)} %get-tuple-element.30), channel_id=1, replica_groups=mesh['emit'=32,'vx'=8,'vy'=2] {'emit'}, dimensions={0} | all-to-all | bytes 524288 | tf_op jit(solution)/shard_map/all_to_all | solution.py:395
  45.0 0.6 %reduce_sum.11 = f32[16,128]{1,0:T(8,128)} reduce(f32[32,16,128]{2,1,0:T(8,128)S(1)} %all_to_all.5, f32[]{:T(128)} %constant.2.clone.1), dimensions={0}, to_apply=%region_0.0 | reduce | flops 63488 | bytes 270340 | tf_op jit(solution)/shard_map/reduce_sum | solution.py:396
  (1 shorter events, 0.0 us)
Async XLA Ops:
  2.5 3.2 %collective-permute-start = (f32[256,128]{1,0:T(8,128)S(1)}, f32[256,128]{1,0:T(8,128)S(1)}, u32[]{:S(2)}, u32[]{:S(2)}) collective-permute-start(f32[256,128]{1,0:T(8,128)S(1)} %get-tuple-element.18), channel_id=1, source_target_pairs={{0,1},{1,0},{2,3},{3,2},{4,5},{5,4},{6,7},{7,6},{8,9},{9,8},{10,11... | collective-permute-start | bytes 393224 | tf_op jit(solution)/shard_map/ppermute | solution.py:383
  5.7 13.1 %collective-permute-start.2 = (f32[40,256]{1,0:T(8,128)S(1)}, f32[40,256]{1,0:T(8,128)S(1)}, u32[]{:S(2)}, u32[]{:S(2)}) collective-permute-start(f32[40,256]{1,0:T(8,128)S(1)} %get-tuple-element.32), channel_id=1, source_target_pairs={{2,0},{4,2},{6,4},{8,6},{10,8},{12,10},{14,12},{3,1},{5,3},{7,5},{... | collective-permute-start | bytes 122888 | tf_op jit(solution)/shard_map/ppermute | solution.py:387
  11.1 7.7 %collective-permute-start.1 = (f32[40,256]{1,0:T(8,128)S(1)}, f32[40,256]{1,0:T(8,128)S(1)}, u32[]{:S(2)}, u32[]{:S(2)}) collective-permute-start(f32[40,256]{1,0:T(8,128)S(1)} %get-tuple-element.28), channel_id=1, source_target_pairs={{0,2},{2,4},{4,6},{6,8},{8,10},{10,12},{12,14},{1,3},{3,5},{5,7},{... | collective-permute-start | bytes 122888 | tf_op jit(solution)/shard_map/ppermute | solution.py:390

commit v5 on v4

--- a/solution.py
+++ b/solution.py
@@ -13,7 +13,8 @@
 LANES = 128
 FIELDS = 9
 TILE_AT = 2 * SUB
-VMEM_LIMIT = 40 * 1024 * 1024
+VMEM_LIMIT = 28 * 1024 * 1024
+GROUP = (13, 37, 35, 33)
 
 
 def in_hbm(array):
@@ -37,17 +38,20 @@
     started = [pltpu.make_async_copy(src, dst, sem.at[n]) for n, (src, dst) in enumerate(copies)]
     for copy in started:
         copy.start()
-    for copy in started:
-        copy.wait()
     lane = lax.broadcasted_iota(jnp.int32, (SUB, LANES), 1)
-
-    for at in range(0, rows, SUB):
-        packed = jnp.zeros((SUB, LANES), jnp.float32)
-        for field in range(FIELDS):
-            moved = pltpu.roll(cols[field, at : at + SUB, :], HALO * field + HALO * (1 - vy), 1)
+    packed = [jnp.zeros((SUB, LANES), jnp.float32)] * (rows // SUB)
+    for number, members in enumerate(((0, 1, 2), (3, 4, 5), (6,), (7,), (8,))):
+        started[3 * number].wait()
+        for field in members:
             here = (lane >= HALO * field) & (lane < HALO * (field + 1))
-            packed = jnp.where(here, moved, packed)
-        side_out[at : at + SUB, :] = packed
+            shift = HALO * field + HALO * (1 - vy)
+            for at in range(rows // SUB):
+                packed[at] = jnp.where(here, pltpu.roll(cols[field, at * SUB : (at + 1) * SUB, :], shift, 1), packed[at])
+    for at in range(rows // SUB):
+        side_out[at * SUB : (at + 1) * SUB, :] = packed[at]
+    for number, copy in enumerate(started):
+        if number % 3:
+            copy.wait()
     for out, edges, first in ((top_out, tops, 0), (low_out, lows, SUB - HALO)):
         for field in range(FIELDS):
             out[HALO * field : HALO * (field + 1), :] = edges[field, first : first + HALO, :]
@@ -74,24 +78,19 @@
     )(fwd_state, adj_state, courant, decay_rate, strength)
 
 
-def half_kernel(
-    lower_half, fwd, adj, courant, decay, strength, side,
+def tile_kernel(
+    fwd, adj, courant, decay, strength, side,
     found_g, found_p, rim, held, coefs, starts, memories, fore, back, curves, partial, sem,
 ):
-    whole = courant.shape[0]
-    rows = whole // 2
-    first_row = rows - SUB if lower_half else 0
-    first_at = TILE_AT - SUB if lower_half else TILE_AT
-    amount = rows + SUB
+    rows = courant.shape[0]
     vy = lax.axis_index("vy")
     copies = []
     for half in range(2):
-        columns = pl.ds(half * LANES, LANES)
-        source, target = pl.ds(first_row, amount), pl.ds(first_at, amount)
+        columns, target = pl.ds(half * LANES, LANES), pl.ds(TILE_AT, rows)
         for number, state in enumerate((fwd, adj)):
-            copies.append((state.at[:, 0, source, columns], held.at[pl.ds(3 * number, 3), half, target, :]))
+            copies.append((state.at[:, 0, :, columns], held.at[pl.ds(3 * number, 3), half, target, :]))
         for number, field in enumerate((courant, decay, strength)):
-            copies.append((field.at[source, columns], held.at[6 + number, half, target, :]))
+            copies.append((field.at[:, columns], held.at[6 + number, half, target, :]))
     started = [pltpu.make_async_copy(src, dst, sem.at[n]) for n, (src, dst) in enumerate(copies)]
     for copy in started:
         copy.start()
@@ -100,20 +99,20 @@
     beside = (lane >= (LANES - HALO) * vy) & (lane < (LANES - HALO) * vy + HALO)
     zero = jnp.zeros((SUB, LANES), jnp.float32)
     lane_first, lane_last = lane == 0, lane == LANES - 1
-    empty = rows + TILE_AT if lower_half else SUB
     for field in range(FIELDS):
         shift = lax.rem(LANES - HALO * field + (LANES - HALO) * vy, LANES)
-        for at in range(0, amount, SUB):
-            strip = pltpu.roll(side[first_row + at : first_row + at + SUB, :], shift, 1)
-            held[field, 2, first_at + at : first_at + at + SUB, :] = jnp.where(beside, strip, zero)
+        for at in range(0, rows, SUB):
+            strip = pltpu.roll(side[at : at + SUB, :], shift, 1)
+            held[field, 2, TILE_AT + at : TILE_AT + at + SUB, :] = jnp.where(beside, strip, zero)
         for part in range(3):
-            held[field, part, empty : empty + SUB, :] = zero
+            held[field, part, SUB : 2 * SUB, :] = zero
+            held[field, part, rows + 2 * SUB : rows + 3 * SUB, :] = zero
     for copy in started:
         copy.wait()
-    rim_at = rows if lower_half else TILE_AT
     for field in range(FIELDS):
         for part in range(3):
-            rim[field, part] = held[field, part, rim_at : rim_at + 2 * SUB, :]
+            rim[0, field, part] = held[field, part, TILE_AT : TILE_AT + 2 * SUB, :]
+            rim[1, field, part] = held[field, part, rows : rows + 2 * SUB, :]
 
     pitch = rows // SUB + 1
 
@@ -193,20 +192,29 @@
     for step in range(1, STEPS + 1):
         margin = STEPS - step
         count = pitch + 2 * margin
-        advance(step, -margin, count)
-
-
-def run_half(lower_half, fwd_state, adj_state, courant, decay_rate, strength, side):
-    rows = courant.shape[0] // 2
+        group = GROUP[step - 1]
+        if count == group:
+            advance(step, -margin, group)
+        else:
+
+            def turn(number, carry, step=step, margin=margin, group=group):
+                advance(step, number * group - margin, group)
+                return carry
+
+            lax.fori_loop(0, count // group, turn, 0)
+
+
+def run_tile(fwd_state, adj_state, courant, decay_rate, strength, side):
+    rows = courant.shape[0]
     strip = (3, rows // SUB + 16, SUB, LANES)
-    found = jax.ShapeDtypeStruct((2, rows + 4 * SUB, LANES), jnp.float32)
+    found = jax.ShapeDtypeStruct((2, rows + 6 * SUB, LANES), jnp.float32)
     return pl.pallas_call(
-        lambda *refs: half_kernel(lower_half, *refs),
-        out_shape=(found, found, jax.ShapeDtypeStruct((FIELDS, 3, 2 * SUB, LANES), jnp.float32)),
-        in_specs=[pl.BlockSpec(memory_space=pltpu.HBM)] * 5 + [pl.BlockSpec(memory_space=pltpu.VMEM)],
+        tile_kernel,
+        out_shape=(found, found, jax.ShapeDtypeStruct((2, FIELDS, 3, 2 * SUB, LANES), jnp.float32)),
+        in_specs=[pl.BlockSpec(memory_space=pl.ANY)] * 5 + [pl.BlockSpec(memory_space=pltpu.VMEM)],
         out_specs=[pl.BlockSpec(memory_space=pltpu.VMEM)] * 3,
         scratch_shapes=[
-            pltpu.VMEM((FIELDS, 3, rows + 5 * SUB, LANES), jnp.float32),
+            pltpu.VMEM((FIELDS, 3, rows + 7 * SUB, LANES), jnp.float32),
             pltpu.VMEM((3,) + strip, jnp.float32),
             pltpu.VMEM((2,) + strip, jnp.float32),
             pltpu.VMEM((2,) + strip, jnp.float32),
@@ -217,17 +225,16 @@
             pltpu.SemaphoreType.DMA((10,)),
         ],
         compiler_params=pltpu.CompilerParams(vmem_limit_bytes=VMEM_LIMIT),
-        cost_estimate=pl.CostEstimate(flops=8000000, bytes_accessed=1800000, transcendentals=0),
-        name="lower_half" if lower_half else "upper_half",
+        cost_estimate=pl.CostEstimate(flops=14000000, bytes_accessed=3500000, transcendentals=0),
+        name="tile",
     )(fwd_state, adj_state, courant, decay_rate, strength, side)
 
 
 def rim_kernel(
-    scale, upper_g, upper_p, upper_rim, lower_g, lower_p, lower_rim, above, below, footprint_in, owner_in,
+    scale, found_g, found_p, rim, above, below, footprint_in, owner_in,
     ordered, pressure, edges, footprint, owner, slot_of, gain_of, list_sem, out_sem,
 ):
     rows = pressure.shape[1]
-    half_rows = rows // 2
     vy = lax.axis_index("vy")
     lists = [
         pltpu.make_async_copy(footprint_in, footprint, list_sem.at[0]),
@@ -235,12 +242,11 @@
     ]
     for copy in lists:
         copy.start()
-    inner = half_rows - SUB
+    inner = rows - 2 * SUB
     leaving = []
     for half in range(2):
         columns = pl.ds(half * LANES, LANES)
-        leaving.append((upper_p.at[half, pl.ds(2 * SUB, inner), :], pressure.at[0, pl.ds(SUB, inner), columns]))
-        leaving.append((lower_p.at[half, pl.ds(SUB, inner), :], pressure.at[0, pl.ds(half_rows, inner), columns]))
+        leaving.append((found_p.at[half, pl.ds(2 * SUB, inner), :], pressure.at[0, pl.ds(SUB, inner), columns]))
     leaving = [pltpu.make_async_copy(src, dst, out_sem.at[n]) for n, (src, dst) in enumerate(leaving)]
     for copy in leaving:
         copy.start()
@@ -270,9 +276,9 @@
         result = []
         for chunk in range(3):
             if low:
-                row = [halo_of(field, p, True) if chunk == 2 else lower_rim[field, p, chunk * SUB : (chunk + 1) * SUB, :] for p in range(3)]
+                row = [halo_of(field, p, True) if chunk == 2 else rim[1, field, p, chunk * SUB : (chunk + 1) * SUB, :] for p in range(3)]
             else:
-                row = [halo_of(field, p, False) if chunk == 0 else upper_rim[field, p, (chunk - 1) * SUB : chunk * SUB, :] for p in range(3)]
+                row = [halo_of(field, p, False) if chunk == 0 else rim[0, field, p, (chunk - 1) * SUB : chunk * SUB, :] for p in range(3)]
             result.append(row)
         return result
 
@@ -316,8 +322,8 @@
             edges[0, at, part * LANES : (part + 1) * LANES] = levels[0][STEPS - 1][part]
             edges[1, at, part * LANES : (part + 1) * LANES] = value
     outer = [
-        pltpu.make_async_copy(edges.at[0, pl.ds(0, SUB), :], pressure.at[0, pl.ds(0, SUB), :], out_sem.at[4]),
-        pltpu.make_async_copy(edges.at[0, pl.ds(SUB, SUB), :], pressure.at[0, pl.ds(rows - SUB, SUB), :], out_sem.at[5]),
+        pltpu.make_async_copy(edges.at[0, pl.ds(0, SUB), :], pressure.at[0, pl.ds(0, SUB), :], out_sem.at[2]),
+        pltpu.make_async_copy(edges.at[0, pl.ds(SUB, SUB), :], pressure.at[0, pl.ds(rows - SUB, SUB), :], out_sem.at[3]),
     ]
     for copy in outer:
         copy.start()
@@ -332,11 +338,10 @@
     for number in range(owner.shape[0]):
         slot_of[owner[number]] = number
     for block in range(blocks):
-        source = upper_g if block < blocks // 2 else lower_g
         part = block % 2
-        at = SUB + (block % (blocks // 2)) // 2 * BR
+        at = SUB + block // 2 * BR
         slot, gain = slot_of[block], gain_of[block]
-        high, low = source[part, at : at + SUB, :], source[part, at + SUB : at + BR, :]
+        high, low = found_g[part, at : at + SUB, :], found_g[part, at + SUB : at + BR, :]
         if block < 2:
             high = edges[1, 0:SUB, part * LANES : (part + 1) * LANES]
         if block >= blocks - 2:
@@ -347,9 +352,9 @@
         copy.wait()
 
 
-def run_rim(scale, upper, lower, above, below, footprint, owner_map):
+def run_rim(scale, found, above, below, footprint, owner_map):
     columns = above.shape[1]
-    rows = 2 * (upper[0].shape[1] - 4 * SUB)
+    rows = found[0].shape[1] - 6 * SUB
     blocks = owner_map.shape[0]
     return pl.pallas_call(
         lambda *refs: rim_kernel(scale, *refs),
@@ -357,7 +362,7 @@
             jax.ShapeDtypeStruct((blocks, BR, BC), jnp.float32),
             jax.ShapeDtypeStruct((1, rows, columns), jnp.float32),
         ),
-        in_specs=[pl.BlockSpec(memory_space=pltpu.VMEM)] * 8 + [pl.BlockSpec(memory_space=pltpu.HBM)] * 2,
+        in_specs=[pl.BlockSpec(memory_space=pltpu.VMEM)] * 5 + [pl.BlockSpec(memory_space=pltpu.HBM)] * 2,
         out_specs=[pl.BlockSpec(memory_space=pltpu.VMEM), pl.BlockSpec(memory_space=pltpu.HBM)],
         scratch_shapes=[
             pltpu.VMEM((2, 2 * SUB, columns), jnp.float32),
@@ -366,31 +371,30 @@
             pltpu.SMEM((blocks,), jnp.int32),
             pltpu.SMEM((blocks,), jnp.float32),
             pltpu.SemaphoreType.DMA((2,)),
-            pltpu.SemaphoreType.DMA((6,)),
+            pltpu.SemaphoreType.DMA((4,)),
         ],
         compiler_params=pltpu.CompilerParams(vmem_limit_bytes=VMEM_LIMIT),
         cost_estimate=pl.CostEstimate(flops=2000000, bytes_accessed=1500000, transcendentals=0),
         name="rim",
-    )(*upper, *lower, above, below, footprint, owner_map)
+    )(*found, above, below, footprint, owner_map)
 
 
 def shards(fwd_state, adj_state, courant, decay_rate, strength, footprint, owner_map):
     groups = lax.axis_size("emit")
     tiles = lax.axis_size("vx")
     rows = courant.shape[0]
-    fields = [in_hbm(field) for field in (fwd_state, adj_state, courant, decay_rate, strength)]
-    side, top, low = pack(*fields)
+    fields = (fwd_state, adj_state, courant, decay_rate, strength)
+    side, top, low = pack(*[in_hbm(field) for field in fields])
+    later, side = lax.optimization_barrier((fields, side))
     side = lax.ppermute(side, "vy", [(0, 1), (1, 0)])
     corners = (HALO * FIELDS, 0)
     top = lax.dynamic_update_slice(top, side[:HALO], corners)
     low = lax.dynamic_update_slice(low, side[rows - HALO :], corners)
     below = lax.ppermute(top, "vx", [(i + 1, i) for i in range(tiles - 1)])
-    upper = run_half(False, *fields, side)
-    low, upper = lax.optimization_barrier((low, upper))
     above = lax.ppermute(low, "vx", [(i, i + 1) for i in range(tiles - 1)])
-    lower = run_half(True, *fields, side)
+    found = run_tile(*later, side)
     ordered, pressure = run_rim(
-        1.0 / groups, upper, lower, above, below, in_hbm(footprint.reshape(-1)), in_hbm(owner_map.reshape(-1))
+        1.0 / groups, found, above, below, in_hbm(footprint.reshape(-1)), in_hbm(owner_map.reshape(-1))
     )
     sent = lax.all_to_all(ordered, "emit", 0, 0, tiled=True)
     gradient = jnp.sum(sent.reshape(groups, -1, BR, BC), axis=0)

time: 46 us -> 43.1 us (0.937)
  Pallas kernels: 9.01 us -> 6.1 us
    pallas_call x2 -> x1, Pallas kernels: 6 us -> 2.99 us  [run_tile(): pl.pallas_call(tile_kernel, out_shape=(found, found, jax.ShapeDtypeStruct...]
  transfers between devices with their start and end apart: 3 -> 3, of which waited for: 1 -> 1; matrix products, arithmetic and copies ran while one was open for 0% -> 0% of each run, Pallas kernels for 13% -> 7%
where the time goes in v5:
time: 43.1 us; the launch traced here: 42.8 us
  blocking collectives  25 us (58%)
  starting transfers between devices  8.96 us (21%)
  Pallas kernels  6.1 us (14%)
  waiting for transfers between devices  1.32 us (3%)
  between operations  0.77 us (2%)
  other arithmetic  0.63 us (1%)
    all_to_all x1, blocking collectives, shards(): sent = lax.all_to_all(ordered, 'emit', 0, 0, tiled=True)  25 us
    ppermute x1, starting transfers between devices, shards(): above = lax.ppermute(low, 'vx', [(i, i + 1) for i in range(tiles - 1)])  4.7 us
    pallas_call x1, Pallas kernels, run_tile(): pl.pallas_call(tile_kernel, out_shape=(found, found, jax.ShapeDtypeStruct...  2.99 us
    ppermute x1, starting transfers between devices, shards(): below = lax.ppermute(top, 'vx', [(i + 1, i) for i in range(tiles - 1)])  2.35 us
    pallas_call x1, Pallas kernels, pack(): pl.pallas_call(pack_kernel, out_shape=(jax.ShapeDtypeStruct((rows, LANES)...  1.96 us
    ppermute x1, starting transfers between devices, shards(): side = lax.ppermute(side, 'vy', [(0, 1), (1, 0)])  1.92 us
    ppermute x1, waiting for transfers between devices, shards(): side = lax.ppermute(side, 'vy', [(0, 1), (1, 0)])  1.31 us
    pallas_call x1, Pallas kernels, run_rim(): pl.pallas_call(lambda *refs: rim_kernel(scale, *refs), out_shape=(jax.Sha...  1.15 us
  transfers between devices with their start and end apart: 3, of which 1 were waited for; matrix products, arithmetic and copies ran while one was open for 0% of the time, Pallas kernels for 7%

profile of v5, /device:TPU:24, one launch (start us, length us, event | category | flops | bytes accessed | tf_op | source)
XLA Modules:
  0.0 42.8 jit_solution(2278348787320189287)
XLA Ops:
  0.6 0.0 copy-start.4
  0.6 0.0 copy-start.3
  0.7 0.0 copy-start.2
  0.7 0.0 copy-start.1
  0.7 0.0 copy-start
  0.7 2.0 %pack.1 = (f32[256,128]{1,0:T(8,128)S(1)}, f32[40,256]{1,0:T(8,128)S(1)}, f32[40,256]{1,0:T(8,128)S(1)}) custom-call(f32[3,1,256,256]{3,2,1,0:T(8,128)} %fwd.2, f32[3,1,256,256]{3,2,1,0:T(8,128)} %adj.2, f32[256,256]{1,0:T(8,128)} %courant.2, f32[256,256]{1,0:T(8,128)} %decay.2, f32[256,256]{1,0:T(8,128)} %strength.2), custom_call_target="tpu_custom_call" | custom-call | flops 600000 | bytes 1500000 | tf_op jit(solution)/shard_map/pack/pallas_call | solution.py:64
  2.7 1.9 %collective-permute-start = (f32[256,128]{1,0:T(8,128)S(1)}, f32[256,128]{1,0:T(8,128)S(1)}, u32[]{:S(2)}, u32[]{:S(2)}) collective-permute-start(f32[256,128]{1,0:T(8,128)S(1)} %get-tuple-element.22), channel_id=1, source_target_pairs={{0,1},{1,0},{2,3},{3,2},{4,5},{5,4},{6,7},{7,6},{8,9},{9,8},{10,11... | collective-permute-start | bytes 393224 | tf_op jit(solution)/shard_map/ppermute | solution.py:389
  4.6 1.3 %collective-permute-done.side = f32[256,128]{1,0:T(8,128)S(1)} collective-permute-done((f32[256,128]{1,0:T(8,128)S(1)}, f32[256,128]{1,0:T(8,128)S(1)}, u32[]{:S(2)}, u32[]{:S(2)}) %collective-permute-start) | collective-permute-done | bytes 131104 | tf_op jit(solution)/shard_map/ppermute | solution.py:389
  5.9 2.3 %collective-permute-start.2 = (f32[40,256]{1,0:T(8,128)S(1)}, f32[40,256]{1,0:T(8,128)S(1)}, u32[]{:S(2)}, u32[]{:S(2)}) collective-permute-start(f32[40,256]{1,0:T(8,128)S(1)} %get-tuple-element.30), channel_id=1, source_target_pairs={{2,0},{4,2},{6,4},{8,6},{10,8},{12,10},{14,12},{3,1},{5,3},{7,5},{... | collective-permute-start | bytes 122888 | tf_op jit(solution)/shard_map/ppermute | solution.py:393
  8.3 4.7 %collective-permute-start.1 = (f32[40,256]{1,0:T(8,128)S(1)}, f32[40,256]{1,0:T(8,128)S(1)}, u32[]{:S(2)}, u32[]{:S(2)}) collective-permute-start(f32[40,256]{1,0:T(8,128)S(1)} %get-tuple-element.31), channel_id=1, source_target_pairs={{0,2},{2,4},{4,6},{6,8},{8,10},{10,12},{12,14},{1,3},{3,5},{5,7},{... | collective-permute-start | bytes 122888 | tf_op jit(solution)/shard_map/ppermute | solution.py:394
  13.0 0.0 copy-done.4
  13.0 0.0 copy-done.3
  13.0 0.0 copy-done.2
  13.0 0.0 copy-done.1
  13.0 0.0 copy-done
  13.0 3.0 %tile.1 = (f32[2,304,128]{2,1,0:T(8,128)S(1)}, f32[2,304,128]{2,1,0:T(8,128)S(1)}, f32[2,9,3,16,128]{4,3,2,1,0:T(8,128)S(1)}) custom-call(f32[3,1,256,256]{3,2,1,0:T(8,128)S(1)} %copy-done, f32[3,1,256,256]{3,2,1,0:T(8,128)S(1)} %copy-done.1, f32[256,256]{1,0:T(8,128)S(1)} %copy-done.2, f32[256,256]{1,0:T(8,128)S(1)} %copy-done.3, f32[256,256]{1,0:T(8,128)S(1)} %copy-done.4, ...), custom_call_target="tpu_custom_call" | custom-call | flops 14000000 | bytes 3500000 | tf_op jit(solution)/shard_map/tile/pallas_call | solution.py:211
  16.0 0.0 collective-permute-done.2.refs_4_
  16.0 0.0 collective-permute-done.1.refs_3_
  16.0 1.1 %rim.1 = (f32[32,16,128]{2,1,0:T(8,128)S(1)}, f32[1,256,256]{2,1,0:T(8,128)}) custom-call(f32[2,304,128]{2,1,0:T(8,128)S(1)} %get-tuple-element.23.refs_0_, f32[2,304,128]{2,1,0:T(8,128)S(1)} %get-tuple-element.24.refs_1_, f32[2,9,3,16,128]{4,3,2,1,0:T(8,128)S(1)} %get-tuple-element.25.refs_2_, f32[40,256]{1,0:T(8,128)S(1)} %collective-permute-done.1.refs_3_, ...), custom_call_target="tpu_custom_call" | custom-call | flops 2000000 | bytes 1500000 | tf_op jit(solution)/shard_map/rim/pallas_call | solution.py:359
  17.2 25.0 %all_to_all.5 = f32[32,16,128]{2,1,0:T(8,128)S(1)} all-to-all(f32[32,16,128]{2,1,0:T(8,128)S(1)} %get-tuple-element.28), channel_id=1, replica_groups=mesh['emit'=32,'vx'=8,'vy'=2] {'emit'}, dimensions={0} | all-to-all | bytes 524288 | tf_op jit(solution)/shard_map/all_to_all | solution.py:399
  42.2 0.6 %reduce_sum.11 = f32[16,128]{1,0:T(8,128)} reduce(f32[32,16,128]{2,1,0:T(8,128)S(1)} %all_to_all.5, f32[]{:T(128)} %constant.2.clone.1), dimensions={0}, to_apply=%region_0.0 | reduce | flops 63488 | bytes 270340 | tf_op jit(solution)/shard_map/reduce_sum | solution.py:400
  (1 shorter events, 0.0 us)
Async XLA Ops:
  0.6 12.3 %copy-start.4 = (f32[256,256]{1,0:T(8,128)S(1)}, f32[256,256]{1,0:T(8,128)}, u32[]{:S(2)}) copy-start(f32[256,256]{1,0:T(8,128)} %strength.2) | copy-start | bytes 786436
  0.6 12.3 %copy-start.3 = (f32[256,256]{1,0:T(8,128)S(1)}, f32[256,256]{1,0:T(8,128)}, u32[]{:S(2)}) copy-start(f32[256,256]{1,0:T(8,128)} %decay.2) | copy-start | bytes 786436
  0.7 12.3 %copy-start.2 = (f32[256,256]{1,0:T(8,128)S(1)}, f32[256,256]{1,0:T(8,128)}, u32[]{:S(2)}) copy-start(f32[256,256]{1,0:T(8,128)} %courant.2) | copy-start | bytes 786436
  0.7 12.3 %copy-start.1 = (f32[3,1,256,256]{3,2,1,0:T(8,128)S(1)}, f32[3,1,256,256]{3,2,1,0:T(8,128)}, u32[]{:S(2)}) copy-start(f32[3,1,256,256]{3,2,1,0:T(8,128)} %adj.2) | copy-start | bytes 2359300
  0.7 12.3 %copy-start = (f32[3,1,256,256]{3,2,1,0:T(8,128)S(1)}, f32[3,1,256,256]{3,2,1,0:T(8,128)}, u32[]{:S(2)}) copy-start(f32[3,1,256,256]{3,2,1,0:T(8,128)} %fwd.2) | copy-start | bytes 2359300
  2.7 3.2 %collective-permute-start = (f32[256,128]{1,0:T(8,128)S(1)}, f32[256,128]{1,0:T(8,128)S(1)}, u32[]{:S(2)}, u32[]{:S(2)}) collective-permute-start(f32[256,128]{1,0:T(8,128)S(1)} %get-tuple-element.22), channel_id=1, source_target_pairs={{0,1},{1,0},{2,3},{3,2},{4,5},{5,4},{6,7},{7,6},{8,9},{9,8},{10,11... | collective-permute-start | bytes 393224 | tf_op jit(solution)/shard_map/ppermute | solution.py:389
  5.9 10.1 %collective-permute-start.2 = (f32[40,256]{1,0:T(8,128)S(1)}, f32[40,256]{1,0:T(8,128)S(1)}, u32[]{:S(2)}, u32[]{:S(2)}) collective-permute-start(f32[40,256]{1,0:T(8,128)S(1)} %get-tuple-element.30), channel_id=1, source_target_pairs={{2,0},{4,2},{6,4},{8,6},{10,8},{12,10},{14,12},{3,1},{5,3},{7,5},{... | collective-permute-start | bytes 122888 | tf_op jit(solution)/shard_map/ppermute | solution.py:393
  8.3 7.8 %collective-permute-start.1 = (f32[40,256]{1,0:T(8,128)S(1)}, f32[40,256]{1,0:T(8,128)S(1)}, u32[]{:S(2)}, u32[]{:S(2)}) collective-permute-start(f32[40,256]{1,0:T(8,128)S(1)} %get-tuple-element.31), channel_id=1, source_target_pairs={{0,2},{2,4},{4,6},{6,8},{8,10},{10,12},{12,14},{1,3},{3,5},{5,7},{... | collective-permute-start | bytes 122888 | tf_op jit(solution)/shard_map/ppermute | solution.py:394

commit v6 on v5

--- a/solution.py
+++ b/solution.py
@@ -79,22 +79,18 @@
 
 
 def tile_kernel(
-    fwd, adj, courant, decay, strength, side,
-    found_g, found_p, rim, held, coefs, starts, memories, fore, back, curves, partial, sem,
+    scale, fwd, adj, courant, decay, strength, side, footprint_in, owner_in,
+    ordered, found_p, rim, marks, gains, held, coefs, starts, memories, fore, back, curves, partial, found_g,
+    footprint, owner, slot_of, gain_of, list_sem,
 ):
     rows = courant.shape[0]
+    lists = [
+        pltpu.make_async_copy(footprint_in, footprint, list_sem.at[0]),
+        pltpu.make_async_copy(owner_in, owner, list_sem.at[1]),
+    ]
+    for copy in lists:
+        copy.start()
     vy = lax.axis_index("vy")
-    copies = []
-    for half in range(2):
-        columns, target = pl.ds(half * LANES, LANES), pl.ds(TILE_AT, rows)
-        for number, state in enumerate((fwd, adj)):
-            copies.append((state.at[:, 0, :, columns], held.at[pl.ds(3 * number, 3), half, target, :]))
-        for number, field in enumerate((courant, decay, strength)):
-            copies.append((field.at[:, columns], held.at[6 + number, half, target, :]))
-    started = [pltpu.make_async_copy(src, dst, sem.at[n]) for n, (src, dst) in enumerate(copies)]
-    for copy in started:
-        copy.start()
-
     lane = lax.broadcasted_iota(jnp.int32, (SUB, LANES), 1)
     beside = (lane >= (LANES - HALO) * vy) & (lane < (LANES - HALO) * vy + HALO)
     zero = jnp.zeros((SUB, LANES), jnp.float32)
@@ -107,8 +103,13 @@
         for part in range(3):
             held[field, part, SUB : 2 * SUB, :] = zero
             held[field, part, rows + 2 * SUB : rows + 3 * SUB, :] = zero
-    for copy in started:
-        copy.wait()
+    for half in range(2):
+        columns, target = slice(half * LANES, (half + 1) * LANES), slice(TILE_AT, TILE_AT + rows)
+        for number in range(3):
+            held[number, half, target, :] = fwd[number, 0, :, columns]
+            held[3 + number, half, target, :] = adj[number, 0, :, columns]
+        for number, field in enumerate((courant, decay, strength)):
+            held[6 + number, half, target, :] = field[:, columns]
     for field in range(FIELDS):
         for part in range(3):
             rim[0, field, part] = held[field, part, TILE_AT : TILE_AT + 2 * SUB, :]
@@ -203,16 +204,39 @@
 
             lax.fori_loop(0, count // group, turn, 0)
 
-
-def run_tile(fwd_state, adj_state, courant, decay_rate, strength, side):
+    for copy in lists:
+        copy.wait()
+    blocks = gain_of.shape[0]
+    for block in range(blocks):
+        gain_of[block] = jnp.float32(0.0)
+    for number in range(footprint.shape[0]):
+        gain_of[footprint[number]] = jnp.float32(scale)
+    for number in range(blocks):
+        slot_of[owner[number]] = number
+        marks[number] = jnp.full((SUB, LANES), owner[number], jnp.int32)
+    for number, block in enumerate((0, 1, blocks - 2, blocks - 1)):
+        gains[number] = jnp.full((SUB, LANES), gain_of[block], jnp.float32)
+    for block in range(blocks):
+        at = SUB + block // 2 * BR
+        ordered[slot_of[block]] = found_g[block % 2, at : at + BR, :] * gain_of[block]
+
+
+def run_tile(scale, fwd_state, adj_state, courant, decay_rate, strength, side, footprint, owner_map):
     rows = courant.shape[0]
     strip = (3, rows // SUB + 16, SUB, LANES)
-    found = jax.ShapeDtypeStruct((2, rows + 6 * SUB, LANES), jnp.float32)
+    found = (2, rows + 6 * SUB, LANES)
+    blocks = owner_map.shape[0]
     return pl.pallas_call(
-        tile_kernel,
-        out_shape=(found, found, jax.ShapeDtypeStruct((2, FIELDS, 3, 2 * SUB, LANES), jnp.float32)),
-        in_specs=[pl.BlockSpec(memory_space=pl.ANY)] * 5 + [pl.BlockSpec(memory_space=pltpu.VMEM)],
-        out_specs=[pl.BlockSpec(memory_space=pltpu.VMEM)] * 3,
+        lambda *refs: tile_kernel(scale, *refs),
+        out_shape=(
+            jax.ShapeDtypeStruct((blocks, BR, BC), jnp.float32),
+            jax.ShapeDtypeStruct(found, jnp.float32),
+            jax.ShapeDtypeStruct((2, FIELDS, 3, 2 * SUB, LANES), jnp.float32),
+            jax.ShapeDtypeStruct((blocks, SUB, LANES), jnp.int32),
+            jax.ShapeDtypeStruct((4, SUB, LANES), jnp.float32),
+        ),
+        in_specs=[pl.BlockSpec(memory_space=pltpu.VMEM)] * 6 + [pl.BlockSpec(memory_space=pltpu.HBM)] * 2,
+        out_specs=[pl.BlockSpec(memory_space=pltpu.VMEM)] * 5,
         scratch_shapes=[
             pltpu.VMEM((FIELDS, 3, rows + 7 * SUB, LANES), jnp.float32),
             pltpu.VMEM((3,) + strip, jnp.float32),
@@ -222,35 +246,21 @@
             pltpu.VMEM((STEPS - 1,) + strip, jnp.float32),
             pltpu.VMEM((2,) + strip, jnp.float32),
             pltpu.VMEM(strip, jnp.float32),
-            pltpu.SemaphoreType.DMA((10,)),
+            pltpu.VMEM(found, jnp.float32),
+            pltpu.SMEM(footprint.shape, jnp.int32),
+            pltpu.SMEM((blocks,), jnp.int32),
+            pltpu.SMEM((blocks,), jnp.int32),
+            pltpu.SMEM((blocks,), jnp.float32),
+            pltpu.SemaphoreType.DMA((2,)),
         ],
         compiler_params=pltpu.CompilerParams(vmem_limit_bytes=VMEM_LIMIT),
         cost_estimate=pl.CostEstimate(flops=14000000, bytes_accessed=3500000, transcendentals=0),
         name="tile",
-    )(fwd_state, adj_state, courant, decay_rate, strength, side)
-
-
-def rim_kernel(
-    scale, found_g, found_p, rim, above, below, footprint_in, owner_in,
-    ordered, pressure, edges, footprint, owner, slot_of, gain_of, list_sem, out_sem,
-):
-    rows = pressure.shape[1]
+    )(fwd_state, adj_state, courant, decay_rate, strength, side, footprint, owner_map)
+
+
+def rim_kernel(slots, marks, gains, rim, above, below, ordered, edge_p):
     vy = lax.axis_index("vy")
-    lists = [
-        pltpu.make_async_copy(footprint_in, footprint, list_sem.at[0]),
-        pltpu.make_async_copy(owner_in, owner, list_sem.at[1]),
-    ]
-    for copy in lists:
-        copy.start()
-    inner = rows - 2 * SUB
-    leaving = []
-    for half in range(2):
-        columns = pl.ds(half * LANES, LANES)
-        leaving.append((found_p.at[half, pl.ds(2 * SUB, inner), :], pressure.at[0, pl.ds(SUB, inner), columns]))
-    leaving = [pltpu.make_async_copy(src, dst, out_sem.at[n]) for n, (src, dst) in enumerate(leaving)]
-    for copy in leaving:
-        copy.start()
-
     lane = lax.broadcasted_iota(jnp.int32, (SUB, LANES), 1)
     sub = lax.broadcasted_iota(jnp.int32, (SUB, LANES), 0)
     beside = (lane >= (LANES - HALO) * vy) & (lane < (LANES - HALO) * vy + HALO)
@@ -282,6 +292,7 @@
             result.append(row)
         return result
 
+    edges = {}
     for low in (False, True):
         speed, keep, loss = (window(field, low) for field in (6, 7, 8))
         states = [[window(3 * state + field, low) for field in range(3)] for state in range(2)]
@@ -319,64 +330,78 @@
             seconds = curves[part::2]
             value = seconds[2] * adjoint[1] + seconds[1] * adjoint[2]
             value = value + (seconds[3] * adjoint[0] + seconds[0] * adjoint[3])
-            edges[0, at, part * LANES : (part + 1) * LANES] = levels[0][STEPS - 1][part]
-            edges[1, at, part * LANES : (part + 1) * LANES] = value
-    outer = [
-        pltpu.make_async_copy(edges.at[0, pl.ds(0, SUB), :], pressure.at[0, pl.ds(0, SUB), :], out_sem.at[2]),
-        pltpu.make_async_copy(edges.at[0, pl.ds(SUB, SUB), :], pressure.at[0, pl.ds(rows - SUB, SUB), :], out_sem.at[3]),
+            edge_p[at, part * LANES : (part + 1) * LANES] = levels[0][STEPS - 1][part]
+            edges[low, part] = value * gains[2 * low + part]
+
+    blocks = slots.shape[0]
+    for slot in range(blocks):
+        block = marks[slot]
+        high, low = slots[slot, 0:SUB, :], slots[slot, SUB:BR, :]
+        for part in range(2):
+            high = jnp.where(block == part, edges[False, part], high)
+            low = jnp.where(block == blocks - 2 + part, edges[True, part], low)
+        ordered[slot, 0:SUB, :] = high
+        ordered[slot, SUB:BR, :] = low
+
+
+def run_rim(slots, marks, gains, rim, above, below):
+    return pl.pallas_call(
+        rim_kernel,
+        out_shape=(
+            jax.ShapeDtypeStruct(slots.shape, jnp.float32),
+            jax.ShapeDtypeStruct((2 * SUB, above.shape[1]), jnp.float32),
+        ),
+        in_specs=[pl.BlockSpec(memory_space=pltpu.VMEM)] * 6,
+        out_specs=[pl.BlockSpec(memory_space=pltpu.VMEM)] * 2,
+        compiler_params=pltpu.CompilerParams(vmem_limit_bytes=VMEM_LIMIT),
+        cost_estimate=pl.CostEstimate(flops=2000000, bytes_accessed=1000000, transcendentals=0),
+        name="rim",
+    )(slots, marks, gains, rim, above, below)
+
+
+def finish_kernel(sent, found_p, edge_p, gradient, pressure, total, sem):
+    rows = pressure.shape[1]
+    inner = rows - 2 * SUB
+    copies = [
+        (edge_p.at[pl.ds(0, SUB), :], pressure.at[0, pl.ds(0, SUB), :]),
+        (edge_p.at[pl.ds(SUB, SUB), :], pressure.at[0, pl.ds(rows - SUB, SUB), :]),
     ]
-    for copy in outer:
+    for half in range(2):
+        columns = pl.ds(half * LANES, LANES)
+        copies.append((found_p.at[half, pl.ds(2 * SUB, inner), :], pressure.at[0, pl.ds(SUB, inner), columns]))
+    copies = [pltpu.make_async_copy(src, dst, sem.at[n]) for n, (src, dst) in enumerate(copies)]
+    for copy in copies:
         copy.start()
-
-    for copy in lists:
+    held = gradient.shape[0]
+    for slot in range(held):
+        terms = [sent[number] for number in range(slot, sent.shape[0], held)]
+        while len(terms) > 1:
+            joined = [one + two for one, two in zip(terms[::2], terms[1::2])]
+            terms = joined + terms[2 * len(joined) :]
+        total[slot] = terms[0]
+    last = pltpu.make_async_copy(total, gradient, sem.at[4])
+    last.start()
+    last.wait()
+    for copy in copies:
         copy.wait()
-    blocks = gain_of.shape[0]
-    for block in range(blocks):
-        gain_of[block] = jnp.float32(0.0)
-    for number in range(footprint.shape[0]):
-        gain_of[footprint[number]] = jnp.float32(scale)
-    for number in range(owner.shape[0]):
-        slot_of[owner[number]] = number
-    for block in range(blocks):
-        part = block % 2
-        at = SUB + block // 2 * BR
-        slot, gain = slot_of[block], gain_of[block]
-        high, low = found_g[part, at : at + SUB, :], found_g[part, at + SUB : at + BR, :]
-        if block < 2:
-            high = edges[1, 0:SUB, part * LANES : (part + 1) * LANES]
-        if block >= blocks - 2:
-            low = edges[1, SUB : 2 * SUB, part * LANES : (part + 1) * LANES]
-        ordered[slot, 0:SUB, :] = high * gain
-        ordered[slot, SUB:BR, :] = low * gain
-    for copy in leaving + outer:
-        copy.wait()
-
-
-def run_rim(scale, found, above, below, footprint, owner_map):
-    columns = above.shape[1]
-    rows = found[0].shape[1] - 6 * SUB
-    blocks = owner_map.shape[0]
+
+
+def finish(groups, sent, found_p, edge_p):
+    gradient = (sent.shape[0] // groups, BR, BC)
+    rows, columns = found_p.shape[1] - 6 * SUB, edge_p.shape[1]
     return pl.pallas_call(
-        lambda *refs: rim_kernel(scale, *refs),
+        finish_kernel,
         out_shape=(
-            jax.ShapeDtypeStruct((blocks, BR, BC), jnp.float32),
+            jax.ShapeDtypeStruct(gradient, jnp.float32),
             jax.ShapeDtypeStruct((1, rows, columns), jnp.float32),
         ),
-        in_specs=[pl.BlockSpec(memory_space=pltpu.VMEM)] * 5 + [pl.BlockSpec(memory_space=pltpu.HBM)] * 2,
-        out_specs=[pl.BlockSpec(memory_space=pltpu.VMEM), pl.BlockSpec(memory_space=pltpu.HBM)],
-        scratch_shapes=[
-            pltpu.VMEM((2, 2 * SUB, columns), jnp.float32),
-            pltpu.SMEM(footprint.shape, jnp.int32),
-            pltpu.SMEM((blocks,), jnp.int32),
-            pltpu.SMEM((blocks,), jnp.int32),
-            pltpu.SMEM((blocks,), jnp.float32),
-            pltpu.SemaphoreType.DMA((2,)),
-            pltpu.SemaphoreType.DMA((4,)),
-        ],
+        in_specs=[pl.BlockSpec(memory_space=pltpu.VMEM)] * 3,
+        out_specs=[pl.BlockSpec(memory_space=pltpu.HBM)] * 2,
+        scratch_shapes=[pltpu.VMEM(gradient, jnp.float32), pltpu.SemaphoreType.DMA((5,))],
         compiler_params=pltpu.CompilerParams(vmem_limit_bytes=VMEM_LIMIT),
-        cost_estimate=pl.CostEstimate(flops=2000000, bytes_accessed=1500000, transcendentals=0),
-        name="rim",
-    )(*found, above, below, footprint, owner_map)
+        cost_estimate=pl.CostEstimate(flops=70000, bytes_accessed=800000, transcendentals=0),
+        name="finish",
+    )(sent, found_p, edge_p)
 
 
 def shards(fwd_state, adj_state, courant, decay_rate, strength, footprint, owner_map):
@@ -392,13 +417,12 @@
     low = lax.dynamic_update_slice(low, side[rows - HALO :], corners)
     below = lax.ppermute(top, "vx", [(i + 1, i) for i in range(tiles - 1)])
     above = lax.ppermute(low, "vx", [(i, i + 1) for i in range(tiles - 1)])
-    found = run_tile(*later, side)
-    ordered, pressure = run_rim(
-        1.0 / groups, found, above, below, in_hbm(footprint.reshape(-1)), in_hbm(owner_map.reshape(-1))
+    slots, found_p, rim, marks, gains = run_tile(
+        1.0 / groups, *later, side, in_hbm(footprint.reshape(-1)), in_hbm(owner_map.reshape(-1))
     )
+    ordered, edge_p = run_rim(slots, marks, gains, rim, above, below)
     sent = lax.all_to_all(ordered, "emit", 0, 0, tiled=True)
-    gradient = jnp.sum(sent.reshape(groups, -1, BR, BC), axis=0)
-    return gradient, pressure
+    return finish(groups, sent, found_p, edge_p)
 
 
 def solution(mesh):

time: 43.1 us -> 42.5 us (0.986)
  other arithmetic: 0.63 us -> 0 us
    reduce_sum x1 -> x0, other arithmetic: 0.63 us -> none  [shards(): gradient = jnp.sum(sent.reshape(groups, -1, BR, BC), axis=0)]
    pallas_call x2 -> x3, Pallas kernels: 4.14 us -> 4.19 us  [the longest x1 2.94 us: run_tile(): pl.pallas_call(lambda *refs: tile_kernel(scale, *refs), out_shape=(jax.Sh...]
where the time goes in v6:
time: 42.5 us; the launch traced here: 42.3 us
  blocking collectives  25 us (59%)
  starting transfers between devices  8.96 us (21%)
  Pallas kernels  6.15 us (14%)
  waiting for transfers between devices  1.32 us (3%)
  between operations  0.77 us (2%)
    all_to_all x1, blocking collectives, shards(): sent = lax.all_to_all(ordered, 'emit', 0, 0, tiled=True)  25 us
    ppermute x1, starting transfers between devices, shards(): above = lax.ppermute(low, 'vx', [(i, i + 1) for i in range(tiles - 1)])  4.7 us
    pallas_call x1, Pallas kernels, run_tile(): pl.pallas_call(lambda *refs: tile_kernel(scale, *refs), out_shape=(jax.Sh...  2.94 us
    ppermute x1, starting transfers between devices, shards(): below = lax.ppermute(top, 'vx', [(i + 1, i) for i in range(tiles - 1)])  2.35 us
    pallas_call x1, Pallas kernels, pack(): pl.pallas_call(pack_kernel, out_shape=(jax.ShapeDtypeStruct((rows, LANES)...  1.96 us
    ppermute x1, starting transfers between devices, shards(): side = lax.ppermute(side, 'vy', [(0, 1), (1, 0)])  1.92 us
    ppermute x1, waiting for transfers between devices, shards(): side = lax.ppermute(side, 'vy', [(0, 1), (1, 0)])  1.31 us
  transfers between devices with their start and end apart: 3, of which 1 were waited for; matrix products, arithmetic and copies ran while one was open for 0% of the time, Pallas kernels for 7%

profile of v6, /device:TPU:24, one launch (start us, length us, event | category | flops | bytes accessed | tf_op | source)
XLA Modules:
  0.0 42.3 jit_solution(1321250181026786553)
XLA Ops:
  0.6 0.0 copy-start.4
  0.6 0.0 copy-start.3
  0.7 0.0 copy-start.2
  0.7 0.0 copy-start.1
  0.7 0.0 copy-start
  0.7 2.0 %pack.1 = (f32[256,128]{1,0:T(8,128)S(1)}, f32[40,256]{1,0:T(8,128)S(1)}, f32[40,256]{1,0:T(8,128)S(1)}) custom-call(f32[3,1,256,256]{3,2,1,0:T(8,128)} %refs_0_, f32[3,1,256,256]{3,2,1,0:T(8,128)} %refs_1_, f32[256,256]{1,0:T(8,128)} %refs_2_, f32[256,256]{1,0:T(8,128)} %refs_3_, f32[256,256]{1,0:T(8,128)} %refs_4_), custom_call_target="tpu_custom_call" | custom-call | flops 600000 | bytes 1500000 | tf_op jit(solution)/shard_map/pack/pallas_call | solution.py:64
  2.7 1.9 %collective-permute-start = (f32[256,128]{1,0:T(8,128)S(1)}, f32[256,128]{1,0:T(8,128)S(1)}, u32[]{:S(2)}, u32[]{:S(2)}) collective-permute-start(f32[256,128]{1,0:T(8,128)S(1)} %get-tuple-element.24), channel_id=1, source_target_pairs={{0,1},{1,0},{2,3},{3,2},{4,5},{5,4},{6,7},{7,6},{8,9},{9,8},{10,11... | collective-permute-start | bytes 393224 | tf_op jit(solution)/shard_map/ppermute | solution.py:414
  4.6 1.3 %collective-permute-done.refs_5_ = f32[256,128]{1,0:T(8,128)S(1)} collective-permute-done((f32[256,128]{1,0:T(8,128)S(1)}, f32[256,128]{1,0:T(8,128)S(1)}, u32[]{:S(2)}, u32[]{:S(2)}) %collective-permute-start) | collective-permute-done | bytes 131104 | tf_op jit(solution)/shard_map/ppermute | solution.py:414
  5.9 2.3 %collective-permute-start.2 = (f32[40,256]{1,0:T(8,128)S(1)}, f32[40,256]{1,0:T(8,128)S(1)}, u32[]{:S(2)}, u32[]{:S(2)}) collective-permute-start(f32[40,256]{1,0:T(8,128)S(1)} %get-tuple-element.34), channel_id=1, source_target_pairs={{2,0},{4,2},{6,4},{8,6},{10,8},{12,10},{14,12},{3,1},{5,3},{7,5},{... | collective-permute-start | bytes 122888 | tf_op jit(solution)/shard_map/ppermute | solution.py:418
  8.3 4.7 %collective-permute-start.1 = (f32[40,256]{1,0:T(8,128)S(1)}, f32[40,256]{1,0:T(8,128)S(1)}, u32[]{:S(2)}, u32[]{:S(2)}) collective-permute-start(f32[40,256]{1,0:T(8,128)S(1)} %get-tuple-element.35), channel_id=1, source_target_pairs={{0,2},{2,4},{4,6},{6,8},{8,10},{10,12},{12,14},{1,3},{3,5},{5,7},{... | collective-permute-start | bytes 122888 | tf_op jit(solution)/shard_map/ppermute | solution.py:419
  13.0 0.0 copy-done.4
  13.0 0.0 copy-done.3
  13.0 0.0 copy-done.2
  13.0 0.0 copy-done.1
  13.0 0.0 copy-done
  13.0 2.9 %tile.1 = (f32[32,16,128]{2,1,0:T(8,128)S(1)}, f32[2,304,128]{2,1,0:T(8,128)S(1)}, f32[2,9,3,16,128]{4,3,2,1,0:T(8,128)S(1)}, s32[32,8,128]{2,1,0:T(8,128)S(1)}, f32[4,8,128]{2,1,0:T(8,128)S(1)}) custom-call(f32[3,1,256,256]{3,2,1,0:T(8,128)S(1)} %copy-done, f32[3,1,256,256]{3,2,1,0:T(8,128)S(1)} %copy-done.1, f32[256,256]{1,0:T(8,128)S(1)} %copy-done.2, ...), custom_call_target="tpu_custom_call" | custom-call | flops 14000000 | bytes 3500000 | tf_op jit(solution)/shard_map/tile/pallas_call | solution.py:229
  16.0 0.0 collective-permute-done.2.below
  16.0 0.0 collective-permute-done.1.above
  16.0 0.5 %rim.1 = (f32[32,16,128]{2,1,0:T(8,128)S(1)}, f32[16,256]{1,0:T(8,128)S(1)}) custom-call(f32[32,16,128]{2,1,0:T(8,128)S(1)} %get-tuple-element.25.slots, s32[32,8,128]{2,1,0:T(8,128)S(1)} %get-tuple-element.26.marks, f32[4,8,128]{2,1,0:T(8,128)S(1)} %get-tuple-element.27.gains, f32[2,9,3,16,128]{4,3,2,1,0:T(8,128)S(1)} %get-tuple-element.28.rim, ...), custom_call_target="tpu_custom_call" | custom-call | flops 2000000 | bytes 1000000 | tf_op jit(solution)/shard_map/rim/pallas_call | solution.py:348
  16.5 25.0 %all_to_all.5.sent = f32[32,16,128]{2,1,0:T(8,128)S(1)} all-to-all(f32[32,16,128]{2,1,0:T(8,128)S(1)} %get-tuple-element.31), channel_id=1, replica_groups=mesh['emit'=32,'vx'=8,'vy'=2] {'emit'}, dimensions={0} | all-to-all | bytes 524288 | tf_op jit(solution)/shard_map/all_to_all | solution.py:424
  41.5 0.7 %finish.1 = (f32[1,16,128]{2,1,0:T(8,128)}, f32[1,256,256]{2,1,0:T(8,128)}) custom-call(f32[32,16,128]{2,1,0:T(8,128)S(1)} %all_to_all.5.sent, f32[2,304,128]{2,1,0:T(8,128)S(1)} %get-tuple-element.32.found_p, f32[16,256]{1,0:T(8,128)S(1)} %get-tuple-element.33.edge_p), custom_call_target="tpu_custom_call" | custom-call | flops 70000 | bytes 800000 | tf_op jit(solution)/shard_map/finish/pallas_call | solution.py:392
  (1 shorter events, 0.0 us)
Async XLA Ops:
  0.6 12.3 %copy-start.4 = (f32[256,256]{1,0:T(8,128)S(1)}, f32[256,256]{1,0:T(8,128)}, u32[]{:S(2)}) copy-start(f32[256,256]{1,0:T(8,128)} %refs_4_) | copy-start | bytes 786436
  0.6 12.3 %copy-start.3 = (f32[256,256]{1,0:T(8,128)S(1)}, f32[256,256]{1,0:T(8,128)}, u32[]{:S(2)}) copy-start(f32[256,256]{1,0:T(8,128)} %refs_3_) | copy-start | bytes 786436
  0.7 12.3 %copy-start.2 = (f32[256,256]{1,0:T(8,128)S(1)}, f32[256,256]{1,0:T(8,128)}, u32[]{:S(2)}) copy-start(f32[256,256]{1,0:T(8,128)} %refs_2_) | copy-start | bytes 786436
  0.7 12.3 %copy-start.1 = (f32[3,1,256,256]{3,2,1,0:T(8,128)S(1)}, f32[3,1,256,256]{3,2,1,0:T(8,128)}, u32[]{:S(2)}) copy-start(f32[3,1,256,256]{3,2,1,0:T(8,128)} %refs_1_) | copy-start | bytes 2359300
  0.7 12.3 %copy-start = (f32[3,1,256,256]{3,2,1,0:T(8,128)S(1)}, f32[3,1,256,256]{3,2,1,0:T(8,128)}, u32[]{:S(2)}) copy-start(f32[3,1,256,256]{3,2,1,0:T(8,128)} %refs_0_) | copy-start | bytes 2359300
  2.7 3.2 %collective-permute-start = (f32[256,128]{1,0:T(8,128)S(1)}, f32[256,128]{1,0:T(8,128)S(1)}, u32[]{:S(2)}, u32[]{:S(2)}) collective-permute-start(f32[256,128]{1,0:T(8,128)S(1)} %get-tuple-element.24), channel_id=1, source_target_pairs={{0,1},{1,0},{2,3},{3,2},{4,5},{5,4},{6,7},{7,6},{8,9},{9,8},{10,11... | collective-permute-start | bytes 393224 | tf_op jit(solution)/shard_map/ppermute | solution.py:414
  5.9 10.1 %collective-permute-start.2 = (f32[40,256]{1,0:T(8,128)S(1)}, f32[40,256]{1,0:T(8,128)S(1)}, u32[]{:S(2)}, u32[]{:S(2)}) collective-permute-start(f32[40,256]{1,0:T(8,128)S(1)} %get-tuple-element.34), channel_id=1, source_target_pairs={{2,0},{4,2},{6,4},{8,6},{10,8},{12,10},{14,12},{3,1},{5,3},{7,5},{... | collective-permute-start | bytes 122888 | tf_op jit(solution)/shard_map/ppermute | solution.py:418
  8.3 7.7 %collective-permute-start.1 = (f32[40,256]{1,0:T(8,128)S(1)}, f32[40,256]{1,0:T(8,128)S(1)}, u32[]{:S(2)}, u32[]{:S(2)}) collective-permute-start(f32[40,256]{1,0:T(8,128)S(1)} %get-tuple-element.35), channel_id=1, source_target_pairs={{0,2},{2,4},{4,6},{6,8},{8,10},{10,12},{12,14},{1,3},{3,5},{5,7},{... | collective-permute-start | bytes 122888 | tf_op jit(solution)/shard_map/ppermute | solution.py:419

commit v7 on v6

--- a/solution.py
+++ b/solution.py
@@ -21,27 +21,19 @@
     return pltpu.with_memory_space_constraint(array, pltpu.HBM)
 
 
-def pack_kernel(fwd, adj, courant, decay, strength, side_out, top_out, low_out, cols, tops, lows, sem):
+def side_kernel(fwd, adj, courant, decay, strength, side_out, cols, sem):
     rows = courant.shape[0]
     vy = lax.axis_index("vy")
     edge = pl.ds(pl.multiple_of((1 - vy) * LANES, LANES), LANES)
-    copies = []
-    for number, state in enumerate((fwd, adj)):
-        at = pl.ds(3 * number, 3)
-        copies.append((state.at[:, 0, :, edge], cols.at[at]))
-        copies.append((state.at[:, 0, pl.ds(0, SUB), :], tops.at[at]))
-        copies.append((state.at[:, 0, pl.ds(rows - SUB, SUB), :], lows.at[at]))
-    for number, field in enumerate((courant, decay, strength)):
-        copies.append((field.at[:, edge], cols.at[6 + number]))
-        copies.append((field.at[pl.ds(0, SUB), :], tops.at[6 + number]))
-        copies.append((field.at[pl.ds(rows - SUB, SUB), :], lows.at[6 + number]))
+    copies = [(state.at[:, 0, :, edge], cols.at[pl.ds(3 * number, 3)]) for number, state in enumerate((fwd, adj))]
+    copies += [(field.at[:, edge], cols.at[6 + number]) for number, field in enumerate((courant, decay, strength))]
     started = [pltpu.make_async_copy(src, dst, sem.at[n]) for n, (src, dst) in enumerate(copies)]
     for copy in started:
         copy.start()
     lane = lax.broadcasted_iota(jnp.int32, (SUB, LANES), 1)
     packed = [jnp.zeros((SUB, LANES), jnp.float32)] * (rows // SUB)
     for number, members in enumerate(((0, 1, 2), (3, 4, 5), (6,), (7,), (8,))):
-        started[3 * number].wait()
+        started[number].wait()
         for field in members:
             here = (lane >= HALO * field) & (lane < HALO * (field + 1))
             shift = HALO * field + HALO * (1 - vy)
@@ -49,33 +41,57 @@
                 packed[at] = jnp.where(here, pltpu.roll(cols[field, at * SUB : (at + 1) * SUB, :], shift, 1), packed[at])
     for at in range(rows // SUB):
         side_out[at * SUB : (at + 1) * SUB, :] = packed[at]
-    for number, copy in enumerate(started):
-        if number % 3:
-            copy.wait()
+
+
+def ends_kernel(fwd, adj, courant, decay, strength, top_out, low_out, tops, lows, sem):
+    rows = courant.shape[0]
+    copies = []
+    for first, ends in ((0, tops), (rows - SUB, lows)):
+        at = pl.ds(first, SUB)
+        copies += [(state.at[:, 0, at, :], ends.at[pl.ds(3 * number, 3)]) for number, state in enumerate((fwd, adj))]
+        copies += [(field.at[at, :], ends.at[6 + number]) for number, field in enumerate((courant, decay, strength))]
+    started = [pltpu.make_async_copy(src, dst, sem.at[n]) for n, (src, dst) in enumerate(copies)]
+    for copy in started:
+        copy.start()
+    for copy in started:
+        copy.wait()
     for out, edges, first in ((top_out, tops, 0), (low_out, lows, SUB - HALO)):
         for field in range(FIELDS):
             out[HALO * field : HALO * (field + 1), :] = edges[field, first : first + HALO, :]
         out[HALO * FIELDS : HALO * (FIELDS + 1), :] = jnp.zeros((HALO, 2 * LANES), jnp.float32)
 
 
-def pack(fwd_state, adj_state, courant, decay_rate, strength):
-    rows, columns = courant.shape
+def pack_side(*fields):
+    rows = fields[2].shape[0]
+    return pl.pallas_call(
+        side_kernel,
+        out_shape=jax.ShapeDtypeStruct((rows, LANES), jnp.float32),
+        in_specs=[pl.BlockSpec(memory_space=pltpu.HBM)] * 5,
+        out_specs=pl.BlockSpec(memory_space=pltpu.VMEM),
+        scratch_shapes=[pltpu.VMEM((FIELDS, rows, LANES), jnp.float32), pltpu.SemaphoreType.DMA((5,))],
+        compiler_params=pltpu.CompilerParams(vmem_limit_bytes=VMEM_LIMIT),
+        cost_estimate=pl.CostEstimate(flops=600000, bytes_accessed=1300000, transcendentals=0),
+        name="side",
+    )(*fields)
+
+
+def pack_ends(*fields):
+    columns = fields[2].shape[1]
     edge = jax.ShapeDtypeStruct((HALO * (FIELDS + 1), columns), jnp.float32)
     return pl.pallas_call(
-        pack_kernel,
-        out_shape=(jax.ShapeDtypeStruct((rows, LANES), jnp.float32), edge, edge),
+        ends_kernel,
+        out_shape=(edge, edge),
         in_specs=[pl.BlockSpec(memory_space=pltpu.HBM)] * 5,
-        out_specs=[pl.BlockSpec(memory_space=pltpu.VMEM)] * 3,
+        out_specs=[pl.BlockSpec(memory_space=pltpu.VMEM)] * 2,
         scratch_shapes=[
-            pltpu.VMEM((FIELDS, rows, LANES), jnp.float32),
             pltpu.VMEM((FIELDS, SUB, columns), jnp.float32),
             pltpu.VMEM((FIELDS, SUB, columns), jnp.float32),
-            pltpu.SemaphoreType.DMA((15,)),
+            pltpu.SemaphoreType.DMA((10,)),
         ],
         compiler_params=pltpu.CompilerParams(vmem_limit_bytes=VMEM_LIMIT),
-        cost_estimate=pl.CostEstimate(flops=600000, bytes_accessed=1500000, transcendentals=0),
-        name="pack",
-    )(fwd_state, adj_state, courant, decay_rate, strength)
+        cost_estimate=pl.CostEstimate(flops=30000, bytes_accessed=300000, transcendentals=0),
+        name="ends",
+    )(*fields)
 
 
 def tile_kernel(
@@ -409,9 +425,11 @@
     tiles = lax.axis_size("vx")
     rows = courant.shape[0]
     fields = (fwd_state, adj_state, courant, decay_rate, strength)
-    side, top, low = pack(*[in_hbm(field) for field in fields])
-    later, side = lax.optimization_barrier((fields, side))
-    side = lax.ppermute(side, "vy", [(0, 1), (1, 0)])
+    held = [in_hbm(field) for field in fields]
+    strips = pack_side(*held)
+    later, strips = lax.optimization_barrier((fields, strips))
+    side = lax.ppermute(strips, "vy", [(0, 1), (1, 0)])
+    top, low = pack_ends(*[in_hbm(field) for field in later])
     corners = (HALO * FIELDS, 0)
     top = lax.dynamic_update_slice(top, side[:HALO], corners)
     low = lax.dynamic_update_slice(low, side[rows - HALO :], corners)

time: 42.5 us -> 42.5 us (level)
  waiting for transfers between devices: 1.32 us -> 0.36 us
  Pallas kernels: 6.15 us -> 6.84 us
    ppermute x1, waiting for transfers between devices: 1.31 us -> 0.35 us  [shards(): side = lax.ppermute(strips, 'vy', [(0, 1), (1, 0)])]
    pallas_call x1 -> x2, Pallas kernels: 1.96 us -> 2.65 us  [the longest x1 1.69 us: pack_side(): pl.pallas_call(side_kernel, out_shape=jax.ShapeDtypeStruct((rows, LANES),...]
  transfers between devices with their start and end apart: 3 -> 3, of which waited for: 1 -> 1; matrix products, arithmetic and copies ran while one was open for 0% -> 0% of each run, Pallas kernels for 7% -> 9%
where the time goes in v7:
time: 42.5 us; the launch traced here: 42.2 us
  blocking collectives  25.1 us (59%)
  starting transfers between devices  9.09 us (21%)
  Pallas kernels  6.84 us (16%)
  between operations  0.78 us (2%)
    all_to_all x1, blocking collectives, shards(): sent = lax.all_to_all(ordered, 'emit', 0, 0, tiled=True)  25.1 us
    ppermute x1, starting transfers between devices, shards(): above = lax.ppermute(low, 'vx', [(i, i + 1) for i in range(tiles - 1)])  4.7 us
    pallas_call x1, Pallas kernels, run_tile(): pl.pallas_call(lambda *refs: tile_kernel(scale, *refs), out_shape=(jax.Sh...  2.94 us
    ppermute x1, starting transfers between devices, shards(): below = lax.ppermute(top, 'vx', [(i + 1, i) for i in range(tiles - 1)])  2.35 us
    ppermute x1, starting transfers between devices, shards(): side = lax.ppermute(strips, 'vy', [(0, 1), (1, 0)])  2.05 us
    pallas_call x1, Pallas kernels, pack_side(): pl.pallas_call(side_kernel, out_shape=jax.ShapeDtypeStruct((rows, LANES),...  1.69 us
    pallas_call x1, Pallas kernels, pack_ends(): pl.pallas_call(ends_kernel, out_shape=(edge, edge), in_specs=[pl.BlockSpe...  0.95 us
  transfers between devices with their start and end apart: 3, of which 1 were waited for; matrix products, arithmetic and copies ran while one was open for 0% of the time, Pallas kernels for 9%

profile of v7, /device:TPU:24, one launch (start us, length us, event | category | flops | bytes accessed | tf_op | source)
XLA Modules:
  0.0 42.2 jit_solution(12422363698085288996)
XLA Ops:
  0.6 1.7 %side.1 = f32[256,128]{1,0:T(8,128)S(1)} custom-call(f32[3,1,256,256]{3,2,1,0:T(8,128)} %fwd.2, f32[3,1,256,256]{3,2,1,0:T(8,128)} %adj.2, f32[256,256]{1,0:T(8,128)} %courant.2, f32[256,256]{1,0:T(8,128)} %decay.2, f32[256,256]{1,0:T(8,128)} %strength.2), custom_call_target="tpu_custom_call" | custom-call | flops 600000 | bytes 1300000 | tf_op jit(solution)/shard_map/side/pallas_call | solution.py:66
  2.3 0.0 copy-start
  2.3 0.0 copy-start.1
  2.4 0.0 copy-start.2
  2.4 0.0 copy-start.3
  2.4 0.0 copy-start.4
  2.4 2.1 %collective-permute-start = (f32[256,128]{1,0:T(8,128)S(1)}, f32[256,128]{1,0:T(8,128)S(1)}, u32[]{:S(2)}, u32[]{:S(2)}) collective-permute-start(f32[256,128]{1,0:T(8,128)S(1)} %side.1), channel_id=1, source_target_pairs={{0,1},{1,0},{2,3},{3,2},{4,5},{5,4},{6,7},{7,6},{8,9},{9,8},{10,11... | collective-permute-start | bytes 393224 | tf_op jit(solution)/shard_map/ppermute | solution.py:431
  4.4 1.0 %ends.1 = (f32[40,256]{1,0:T(8,128)S(1)}, f32[40,256]{1,0:T(8,128)S(1)}) custom-call(f32[3,1,256,256]{3,2,1,0:T(8,128)} %fwd.2, f32[3,1,256,256]{3,2,1,0:T(8,128)} %adj.2, f32[256,256]{1,0:T(8,128)} %courant.2, f32[256,256]{1,0:T(8,128)} %decay.2, f32[256,256]{1,0:T(8,128)} %strength.2), custom_call_target="tpu_custom_call" | custom-call | flops 30000 | bytes 300000 | tf_op jit(solution)/shard_map/ends/pallas_call | solution.py:81
  5.4 0.4 collective-permute-done.refs_5_
  5.8 2.3 %collective-permute-start.2 = (f32[40,256]{1,0:T(8,128)S(1)}, f32[40,256]{1,0:T(8,128)S(1)}, u32[]{:S(2)}, u32[]{:S(2)}) collective-permute-start(f32[40,256]{1,0:T(8,128)S(1)} %get-tuple-element.32), channel_id=1, source_target_pairs={{2,0},{4,2},{6,4},{8,6},{10,8},{12,10},{14,12},{3,1},{5,3},{7,5},{... | collective-permute-start | bytes 122888 | tf_op jit(solution)/shard_map/ppermute | solution.py:436
  8.1 4.7 %collective-permute-start.1 = (f32[40,256]{1,0:T(8,128)S(1)}, f32[40,256]{1,0:T(8,128)S(1)}, u32[]{:S(2)}, u32[]{:S(2)}) collective-permute-start(f32[40,256]{1,0:T(8,128)S(1)} %get-tuple-element.33), channel_id=1, source_target_pairs={{0,2},{2,4},{4,6},{6,8},{8,10},{10,12},{12,14},{1,3},{3,5},{5,7},{... | collective-permute-start | bytes 122888 | tf_op jit(solution)/shard_map/ppermute | solution.py:437
  12.8 0.0 copy-done
  12.8 0.0 copy-done.1
  12.9 0.0 copy-done.2
  12.9 0.0 copy-done.3
  12.9 0.0 copy-done.4
  12.9 2.9 %tile.1 = (f32[32,16,128]{2,1,0:T(8,128)S(1)}, f32[2,304,128]{2,1,0:T(8,128)S(1)}, f32[2,9,3,16,128]{4,3,2,1,0:T(8,128)S(1)}, s32[32,8,128]{2,1,0:T(8,128)S(1)}, f32[4,8,128]{2,1,0:T(8,128)S(1)}) custom-call(f32[3,1,256,256]{3,2,1,0:T(8,128)S(1)} %copy-done, f32[3,1,256,256]{3,2,1,0:T(8,128)S(1)} %copy-done.1, f32[256,256]{1,0:T(8,128)S(1)} %copy-done.2, ...), custom_call_target="tpu_custom_call" | custom-call | flops 14000000 | bytes 3500000 | tf_op jit(solution)/shard_map/tile/pallas_call | solution.py:245
  15.8 0.0 collective-permute-done.2.below
  15.8 0.0 collective-permute-done.1.above
  15.8 0.5 %rim.1 = (f32[32,16,128]{2,1,0:T(8,128)S(1)}, f32[16,256]{1,0:T(8,128)S(1)}) custom-call(f32[32,16,128]{2,1,0:T(8,128)S(1)} %get-tuple-element.23.slots, s32[32,8,128]{2,1,0:T(8,128)S(1)} %get-tuple-element.24.marks, f32[4,8,128]{2,1,0:T(8,128)S(1)} %get-tuple-element.25.gains, f32[2,9,3,16,128]{4,3,2,1,0:T(8,128)S(1)} %get-tuple-element.26.rim, ...), custom_call_target="tpu_custom_call" | custom-call | flops 2000000 | bytes 1000000 | tf_op jit(solution)/shard_map/rim/pallas_call | solution.py:364
  16.4 25.1 %all_to_all.5.sent = f32[32,16,128]{2,1,0:T(8,128)S(1)} all-to-all(f32[32,16,128]{2,1,0:T(8,128)S(1)} %get-tuple-element.29), channel_id=1, replica_groups=mesh['emit'=32,'vx'=8,'vy'=2] {'emit'}, dimensions={0} | all-to-all | bytes 524288 | tf_op jit(solution)/shard_map/all_to_all | solution.py:442
  41.4 0.7 %finish.1 = (f32[1,16,128]{2,1,0:T(8,128)}, f32[1,256,256]{2,1,0:T(8,128)}) custom-call(f32[32,16,128]{2,1,0:T(8,128)S(1)} %all_to_all.5.sent, f32[2,304,128]{2,1,0:T(8,128)S(1)} %get-tuple-element.30.found_p, f32[16,256]{1,0:T(8,128)S(1)} %get-tuple-element.31.edge_p), custom_call_target="tpu_custom_call" | custom-call | flops 70000 | bytes 800000 | tf_op jit(solution)/shard_map/finish/pallas_call | solution.py:408
  (1 shorter events, 0.0 us)
Async XLA Ops:
  2.3 10.5 %copy-start = (f32[3,1,256,256]{3,2,1,0:T(8,128)S(1)}, f32[3,1,256,256]{3,2,1,0:T(8,128)}, u32[]{:S(2)}) copy-start(f32[3,1,256,256]{3,2,1,0:T(8,128)} %fwd.2) | copy-start | bytes 2359300
  2.3 10.5 %copy-start.1 = (f32[3,1,256,256]{3,2,1,0:T(8,128)S(1)}, f32[3,1,256,256]{3,2,1,0:T(8,128)}, u32[]{:S(2)}) copy-start(f32[3,1,256,256]{3,2,1,0:T(8,128)} %adj.2) | copy-start | bytes 2359300
  2.4 10.5 %copy-start.2 = (f32[256,256]{1,0:T(8,128)S(1)}, f32[256,256]{1,0:T(8,128)}, u32[]{:S(2)}) copy-start(f32[256,256]{1,0:T(8,128)} %courant.2) | copy-start | bytes 786436
  2.4 10.5 %copy-start.3 = (f32[256,256]{1,0:T(8,128)S(1)}, f32[256,256]{1,0:T(8,128)}, u32[]{:S(2)}) copy-start(f32[256,256]{1,0:T(8,128)} %decay.2) | copy-start | bytes 786436
  2.4 10.5 %copy-start.4 = (f32[256,256]{1,0:T(8,128)S(1)}, f32[256,256]{1,0:T(8,128)}, u32[]{:S(2)}) copy-start(f32[256,256]{1,0:T(8,128)} %strength.2) | copy-start | bytes 786436
  2.4 3.4 %collective-permute-start = (f32[256,128]{1,0:T(8,128)S(1)}, f32[256,128]{1,0:T(8,128)S(1)}, u32[]{:S(2)}, u32[]{:S(2)}) collective-permute-start(f32[256,128]{1,0:T(8,128)S(1)} %side.1), channel_id=1, source_target_pairs={{0,1},{1,0},{2,3},{3,2},{4,5},{5,4},{6,7},{7,6},{8,9},{9,8},{10,11... | collective-permute-start | bytes 393224 | tf_op jit(solution)/shard_map/ppermute | solution.py:431
  5.8 10.1 %collective-permute-start.2 = (f32[40,256]{1,0:T(8,128)S(1)}, f32[40,256]{1,0:T(8,128)S(1)}, u32[]{:S(2)}, u32[]{:S(2)}) collective-permute-start(f32[40,256]{1,0:T(8,128)S(1)} %get-tuple-element.32), channel_id=1, source_target_pairs={{2,0},{4,2},{6,4},{8,6},{10,8},{12,10},{14,12},{3,1},{5,3},{7,5},{... | collective-permute-start | bytes 122888 | tf_op jit(solution)/shard_map/ppermute | solution.py:436
  8.1 7.7 %collective-permute-start.1 = (f32[40,256]{1,0:T(8,128)S(1)}, f32[40,256]{1,0:T(8,128)S(1)}, u32[]{:S(2)}, u32[]{:S(2)}) collective-permute-start(f32[40,256]{1,0:T(8,128)S(1)} %get-tuple-element.33), channel_id=1, source_target_pairs={{0,2},{2,4},{4,6},{6,8},{8,10},{10,12},{12,14},{1,3},{3,5},{5,7},{... | collective-permute-start | bytes 122888 | tf_op jit(solution)/shard_map/ppermute | solution.py:437
